TPU v7x, 32 devices: a whole 2x2x4 slice. The times are simulated.
32 devices in a mesh: dp: 32 (over z, y, x, core).
Axes of the slice: x: 2, y: 2, z: 4, core: 2. Of those that a mesh axis runs over, the one named last changes fastest.
Arguments:
- hidden_in: bfloat16 [4096, 640], P('dp'), may hold values from -6 to 6
- cotangent: bfloat16 [4096, 640], P('dp'), may hold values from -6 to 6
- params: float32 [5573632], P('dp'), may hold values from -4 to 4
- moment_one: float32 [5573632], P('dp'), may hold values from -6 to 6
- moment_two: float32 [5573632], P('dp'), may hold values from 0.02 to 0.5
- seq_lengths: int32 [64], replicated, may hold values from 0 to 128, as said below
- seq_owner: int32 [64], replicated, may hold values from 0 to 31, as said below
Outputs:
- block_out: bfloat16 [4096, 640], P('dp')
- grad_in: float32 [4096, 640], P('dp')
- grad_flat: float32 [5573632], P('dp')
- params_new: float32 [5573632], P('dp')
- moment_one_new: float32 [5573632], P('dp')
- moment_two_new: float32 [5573632], P('dp')
Inputs may be any that keep to these rules, and one draw needn't show every extreme that they name: `seq_lengths`: sequences 2j and 2j + 1 go to the same device; on each device their lengths sum to 1 to 128, and sequence 2j has a token or more; one sequence has exactly 128 tokens and its partner has none; other sequences 2j + 1 may have none too. `seq_owner`: each device holds exactly the two sequences 2j and 2j + 1 for one j.
All inputs are finite; a program needn't handle non-finite values.
Results may differ from a plain program's by a relative error of at most 0.012.
The roundings to bfloat16 on the way count: a program that leaves them out, or rounds other values in their place, can miss the bound.
Values may be sent and summed in bfloat16 or wider, within the bound.
No kernel may reach another device: no remote copies, remote signals or barrier semaphores. Data moves between devices by JAX's collectives and lax.ppermute only.
A program may use at most 128 MiB of HBM per device.

v0:
```python
import functools
import math

import jax
import jax.numpy as jnp
from jax import lax
from jax.experimental import pallas as pl
from jax.experimental.pallas import tpu as pltpu
from jax.sharding import PartitionSpec as P

D = 640
FF = 2048
HD = 256
HQ = 1024
CAP = 128
WINDOW = 64
STEP = 3
G1LEN = 1638400
G2LEN = 3932160
LANES = 128
ROWS = 16
GELU_SCALE = math.sqrt(2 / math.pi)
ATTN_PADDED, FFN_PADDED = 0, 2 * D


def rms_scale(values, gain_vec):
    return (
        values
        * lax.rsqrt(jnp.mean(values * values, axis=-1, keepdims=True) + 1e-06)
        * (1.0 + gain_vec)
    )


def rotate(values, cos_tab, sin_tab):
    half_dim = values.shape[-1] // 2
    lower_half = values[..., :half_dim]
    upper_half = values[..., half_dim:]
    return jnp.concatenate(
        [lower_half * cos_tab - upper_half * sin_tab, upper_half * cos_tab + lower_half * sin_tab],
        axis=-1,
    )


def gated_gelu(gate_proj, up_proj):
    return jax.nn.gelu(gate_proj, approximate=True) * up_proj


def times_transposed(rows_in, matrix):
    return lax.dot_general(
        rows_in, matrix, (((1,), (1,)), ((), ())), preferred_element_type=jnp.float32
    )


def slot_setup(seq_lengths, seq_owner, device):
    mine_mask = seq_owner == device
    own_lengths = jnp.where(mine_mask, seq_lengths, 0)
    seq_ends = jnp.cumsum(own_lengths, dtype=jnp.int32)
    seq_begins = seq_ends - own_lengths
    slot_index = jnp.arange(CAP, dtype=jnp.int32)
    column = slot_index[:, None]
    inside_mask = (
        mine_mask[None, :] & (seq_begins[None, :] <= column) & (column < seq_ends[None, :])
    )
    live_mask = jnp.any(inside_mask, axis=1)
    seq_label = jnp.sum(
        (mine_mask[None, :] & (seq_ends[None, :] <= column)).astype(jnp.int32),
        axis=1,
        dtype=jnp.int32,
    )
    position = jnp.sum(
        jnp.where(inside_mask, column - seq_begins[None, :], 0), axis=1, dtype=jnp.int32
    )
    row_slot = slot_index[:, None]
    col_slot = slot_index[None, :]
    allowed = live_mask[:, None] & live_mask[None, :] & (
        seq_label[:, None] == seq_label[None, :]
    ) & (col_slot <= row_slot) & (row_slot - col_slot < WINDOW) | (row_slot == col_slot)
    half_dim = HD // 2
    frequency = 10000.0 ** (-2.0 * jnp.arange(half_dim, dtype=jnp.float32) / HD)
    angles = position.astype(jnp.float32)[:, None] * frequency[None, :]
    live_wide = jnp.broadcast_to(live_mask[:, None], (CAP, LANES)).astype(jnp.float32)
    return jnp.concatenate(
        [jnp.cos(angles), jnp.sin(angles), allowed.astype(jnp.float32), live_wide], axis=1
    )


def rms_pull(raw, gain_vec, delta):
    scale = lax.rsqrt(jnp.mean(raw * raw, axis=-1, keepdims=True) + 1e-06)
    weighed = delta * (1.0 + gain_vec)
    shared = jnp.mean(raw * weighed, axis=-1, keepdims=True)
    return scale * weighed - raw * (scale * scale * scale * shared), delta * raw * scale


def rotate_pull(delta, cos_tab, sin_tab):
    half_dim = delta.shape[-1] // 2
    lower_half = delta[:, :half_dim]
    upper_half = delta[:, half_dim:]
    return jnp.concatenate(
        [lower_half * cos_tab + upper_half * sin_tab, upper_half * cos_tab - lower_half * sin_tab],
        axis=-1,
    )


def bit_orders(devices, tuned):
    bits = devices.bit_length() - 1
    if bits == 5:
        return [["cxyab".index(letter) for letter in order] for order in tuned]
    return [[1 + (shift + step) % (bits - 1) for step in range(bits - 1)] for shift in range(3)]


def across(block, bit, devices):
    return lax.ppermute(block, "dp", [(i, i ^ (1 << bit)) for i in range(devices)])


def offset_of(place, order):
    return sum(((place >> k) & 1) << bit for k, bit in enumerate(order))


def gather_chunks(pieces, orders, devices):
    held = [piece[None] for piece in pieces]
    for stage in range(len(orders[0]) - 1):
        came = [across(block, order[stage], devices) for block, order in zip(held, orders)]
        for chunk in range(1, len(came)):
            came[chunk] = lax.optimization_barrier((came[chunk], came[0]))[0]
        held = [jnp.concatenate(pair) for pair in zip(held, came)]
    last = [across(block, order[-1], devices) for block, order in zip(held, orders)]
    chunks = []
    for block, final in zip(held, last):
        if chunks:
            final = lax.optimization_barrier((final, chunks[0][-1]))[0]
        beside = across(block, 0, devices)
        final = lax.optimization_barrier((final, beside))[0]
        chunks.append((block, final, beside, across(final, 0, devices)))
    return chunks


def sent_blocks(chunks, orders, stage, devices):
    return [
        across(away, order[stage], devices)
        for (_, away), order in zip(chunks, orders)
    ]


def merged_blocks(chunks, came):
    merged = []
    for (home, _), arrived in zip(chunks, came):
        half = home.shape[0] // 2

        def added(low, high):
            return home[low:high].astype(jnp.float32) + arrived[low:high].astype(jnp.float32)

        if half:
            merged.append(
                (
                    added(0, half).astype(jnp.bfloat16),
                    added(half, 2 * half).astype(jnp.bfloat16),
                )
            )
        else:
            merged.append((added(0, 1)[0], None))
    return merged


def cut_rows(rows, parts):
    each = -(-rows // (parts * ROWS)) * ROWS
    return [(low, min(low + each, rows)) for low in range(0, rows, each)]


def whole_specs(count):
    return [pl.BlockSpec(memory_space=pltpu.VMEM)] * count


def owner_rows(device, index, order, extra, start, each):
    owner = device ^ extra
    for k, bit in enumerate(order):
        owner = owner ^ (((index >> k) & 1) << bit)
    return owner, owner * each + start


def copy_step(rows):
    return max(step for step in range(ROWS, 513, ROWS) if rows % step == 0)


def each_piece(padded, first, take, visit):
    def visit_plain(shift):
        step = copy_step(take)

        def visit_step(part):
            at = part * step
            visit(at, step, pl.multiple_of(first + shift + at, ROWS))

        if take == step:
            visit_step(0)
        else:
            pl.loop(0, take // step)(visit_step)

    if not padded:
        visit_plain(0)
        return
    units = take // ROWS
    inner = max(count for count in range(1, 41) if units % count == 0)
    number = first // ROWS

    def visit_units(row_of):
        def visit_some(step):
            for part in range(inner):
                at = (step * inner + part) * ROWS
                visit(at, ROWS, row_of(step * inner + part))

        if units == inner:
            visit_some(0)
        else:
            pl.loop(0, units // inner)(visit_some)

    longer = (ROWS + 1) * number
    pl.when(number + units <= padded)(lambda: visit_units(lambda k: longer + (ROWS + 1) * k))
    pl.when(number >= padded)(lambda: visit_plain(padded))
    pl.when((number < padded) & (number + units > padded))(
        lambda: visit_units(lambda k: ROWS * (number + k) + jnp.minimum(number + k, padded))
    )


def spread_blocks(padded, plan, views, device, spread, tails):
    for (order, extra, take, start, each), (block_ref, first_index, count, first_row) in zip(
        plan, views
    ):

        @pl.loop(0, count)
        def _(
            index,
            order=order,
            extra=extra,
            take=take,
            start=start,
            each=each,
            block_ref=block_ref,
            first_index=first_index,
            first_row=first_row,
        ):
            owner, first = owner_rows(device, index, order, extra, start, each)

            def spread_unit(at, unit, row):
                low = first_row + at
                if not isinstance(low, int):
                    low = pl.multiple_of(low, ROWS)
                spread[pl.ds(row, unit), :] = block_ref[
                    first_index + index, pl.ds(low, unit), :
                ].astype(jnp.float32)

            each_piece(padded, first, take, spread_unit)
            if tails is not None:
                tails[owner] = block_ref[index, take : take + tails.shape[1], :]


def pitch_of(columns):
    blocks = columns // LANES
    return blocks + (blocks == ROWS)


def fold_matrices(spread, targets):
    first = 0
    for matrix, offset, rows, columns in targets:
        blocks = columns // LANES
        pitch = pitch_of(columns)

        @pl.loop(0, rows // LANES)
        def _(step, matrix=matrix, offset=offset, blocks=blocks, pitch=pitch, first=first):
            base = first + step * (LANES * pitch)
            at = pl.ds(pl.multiple_of(step * LANES, LANES), LANES)
            for block in range(blocks):
                low = offset + block * LANES
                matrix[at, low : low + LANES] = spread[
                    pl.ds(base + block, LANES, stride=pitch), :
                ].astype(jnp.bfloat16)

        first += rows * pitch


def spread_grads(spread, products):
    first = 0
    for turned, right, columns in products:
        rows = turned.shape[0]
        blocks = columns // LANES
        pitch = pitch_of(columns)
        wide = 2 - blocks % 2
        for block in range(0, blocks, wide):
            product = jnp.dot(
                turned,
                right(block * LANES, (block + wide) * LANES),
                preferred_element_type=jnp.float32,
            )
            for part in range(wide):
                spread[pl.ds(first + block + part, rows, stride=pitch), :] = product[
                    :, part * LANES : (part + 1) * LANES
                ]
        first += rows * pitch


def place_blocks(padded, plan, device, spread, tails, targets):
    for target, order, extra, low, take, start, each in plan:
        target_ref = targets[target]

        @pl.loop(0, target_ref.shape[0])
        def _(
            index,
            target_ref=target_ref,
            order=order,
            extra=extra,
            low=low,
            take=take,
            start=start,
            each=each,
        ):
            owner, first = owner_rows(device, index, order, extra, start or 0, each)
            if start is None:
                target_ref[index, low : low + take, :] = tails[owner].astype(jnp.bfloat16)
                return

            def place_unit(at, unit, row):
                at = low + at
                if not isinstance(at, int):
                    at = pl.multiple_of(at, ROWS)
                target_ref[index, pl.ds(at, unit), :] = spread[pl.ds(row, unit), :].astype(
                    jnp.bfloat16
                )

            each_piece(padded, first, take, place_unit)


def attn_forward(hidden_in, qkv_weight, tables, gains):
    cos_tab = tables[:, :LANES]
    sin_tab = tables[:, LANES : 2 * LANES]
    open_pairs = tables[:, 2 * LANES : 3 * LANES] > 0.0
    gain_query = gains[:, D : D + HD]
    gain_key = gains[:, D + HD : D + 2 * HD]
    normed_in = rms_scale(hidden_in[...].astype(jnp.float32), gains[:, :D]).astype(jnp.bfloat16)
    raw = jnp.dot(normed_in, qkv_weight[...], preferred_element_type=jnp.float32)
    key_raw = raw[:, HQ : HQ + HD]
    values = raw[:, HQ + HD :].astype(jnp.bfloat16)
    keys = rotate(rms_scale(key_raw, gain_key), cos_tab, sin_tab).astype(jnp.bfloat16)
    heads = []
    for head in range(HQ // HD):
        query_raw = raw[:, head * HD : (head + 1) * HD]
        rot_query = rotate(rms_scale(query_raw, gain_query), cos_tab, sin_tab) * HD ** (-0.5)
        rot_query = rot_query.astype(jnp.bfloat16)
        scores = jnp.where(open_pairs, times_transposed(rot_query, keys), -1e30)
        row_max = jnp.max(scores, axis=-1, keepdims=True)
        raised = jnp.exp(scores - row_max)
        summed = jnp.sum(raised, axis=-1, keepdims=True)
        context = jnp.dot(
            (raised / summed).astype(jnp.bfloat16), values, preferred_element_type=jnp.float32
        ).astype(jnp.bfloat16)
        heads.append((query_raw, rot_query, scores, row_max + jnp.log(summed), context))
    return normed_in, key_raw, values, keys, heads, cos_tab, sin_tab


def join_gains(tails, gain_len, gains):
    lane = lax.broadcasted_iota(jnp.int32, (1, LANES), 1)
    tiles = [jnp.zeros((1, LANES), jnp.float32) for _ in range(gains.shape[1] // LANES)]
    for owner in range(tails.shape[0]):
        tile, shift = divmod(owner * gain_len, LANES)
        run = jnp.where(lane < gain_len, tails[owner].astype(jnp.float32)[0:1, :], 0.0)
        if shift:
            run = pltpu.roll(run, shift, 1)
        tiles[tile] += jnp.where(lane >= shift, run, 0.0)
        if shift + gain_len > LANES:
            tiles[tile + 1] += jnp.where(lane < shift, run, 0.0)
    for number, tile in enumerate(tiles):
        gains[:, number * LANES : (number + 1) * LANES] = tile


def attn_forward_kernel(plan, gain_len, device_ref, hidden_in, tables, *refs):
    if not gain_len:
        given, refs = refs[0], refs[1:]
    sources = refs[: len(plan)]
    refs = refs[len(plan) :]
    qkv_weight, out_weight, gains, attn_out, mid_stream = refs[:5]
    staging, spread, tails, context, sems = refs[5:]
    copies, views = [], []
    for number, source in enumerate(sources):
        count = source.shape[0]
        held = staging.at[pl.ds(number * count, count)]
        copies.append(pltpu.make_async_copy(source, held, sems.at[number]))
        views.append((held, 0, count, 0))
    for copy in copies:
        copy.start()
    for copy, step, view in zip(copies, plan, views):
        copy.wait()
        spread_blocks(
            ATTN_PADDED,
            [step],
            [view],
            device_ref[0],
            spread,
            tails if gain_len else None,
        )
    if gain_len:
        join_gains(tails, gain_len, gains)
    else:
        gains[...] = given[...]
    fold_matrices(
        spread,
        (
            (qkv_weight, 0, D, HQ),
            (qkv_weight, HQ, D, HD),
            (qkv_weight, HQ + HD, D, HD),
            (out_weight, 0, HQ, D),
        ),
    )
    heads = attn_forward(hidden_in, qkv_weight, tables, gains)[4]
    for head, parts in enumerate(heads):
        context[:, head * HD : (head + 1) * HD] = parts[-1]
    out = jnp.dot(context[...], out_weight[...], preferred_element_type=jnp.float32)
    attn_out[...] = out
    gain_post = gains[:, D + 2 * HD : 2 * D + 2 * HD]
    mid_stream[...] = hidden_in[...].astype(jnp.float32) + rms_scale(out, gain_post)


def forward_attn(plan, gain_len, tail_rows, devices, device, hidden_in, tables, given, arrays):
    shapes = [
        jax.ShapeDtypeStruct((D, HQ + 2 * HD), jnp.bfloat16),
        jax.ShapeDtypeStruct((HQ, D), jnp.bfloat16),
        jax.ShapeDtypeStruct((1, 4 * D + 2 * HD), jnp.float32),
        jax.ShapeDtypeStruct((CAP, D), jnp.float32),
        jax.ShapeDtypeStruct((CAP, D), jnp.float32),
    ]
    given = [] if gain_len else [given]
    held = (sum(array.shape[0] for array in arrays),) + arrays[0].shape[1:]
    return pl.pallas_call(
        functools.partial(attn_forward_kernel, plan, gain_len),
        out_shape=shapes,
        in_specs=[pl.BlockSpec(memory_space=pltpu.SMEM)]
        + whole_specs(2 + len(given))
        + [pl.BlockSpec(memory_space=pltpu.HBM)] * len(arrays),
        out_specs=whole_specs(len(shapes)),
        scratch_shapes=[
            pltpu.VMEM(held, jnp.bfloat16),
            pltpu.VMEM((G1LEN // LANES + ATTN_PADDED, LANES), jnp.float32),
            pltpu.VMEM((devices, tail_rows, LANES) if gain_len else (1, ROWS, LANES), jnp.bfloat16),
            pltpu.VMEM((CAP, HQ), jnp.bfloat16),
            pltpu.SemaphoreType.DMA((len(arrays),)),
        ],
        compiler_params=pltpu.CompilerParams(vmem_limit_bytes=24 << 20),
        cost_estimate=pl.CostEstimate(flops=0, bytes_accessed=64 << 20, transcendentals=0),
    )(device, hidden_in, tables, *given, *arrays)


def ffn_kernel(
    plan_in,
    staged,
    plan_out,
    device_ref,
    mid_ref,
    attn_out,
    cotangent,
    tables,
    gains,
    *refs,
):
    sources = refs[: len(plan_in)]
    refs = refs[len(plan_in) :]
    block_out, delta_mid_ref, delta_attn_ref, late_gains = refs[:4]
    targets = refs[4:-10]
    spread, gate_weight, up_weight, down_weight = refs[-10:-6]
    gates, ups, hidden, delta_gate, delta_up, sems = refs[-6:]
    device = device_ref[0]
    copies, views = [], []
    for source, (target, first_index, first_row) in zip(sources, staged):
        count, rows = source.shape[:2]
        held = targets[target]
        copies.append(
            pltpu.make_async_copy(
                source,
                held.at[pl.ds(first_index, count), pl.ds(first_row, rows), :],
                sems.at[len(copies)],
            )
        )
        views.append((held, first_index, count, first_row))
    for copy in copies:
        copy.start()
    mid_stream = mid_ref[...]
    gain_post = gains[:, D + 2 * HD : 2 * D + 2 * HD]
    gain_mid = gains[:, 2 * D + 2 * HD : 3 * D + 2 * HD]
    gain_last = gains[:, 3 * D + 2 * HD :]
    normed_mid = rms_scale(mid_stream, gain_mid).astype(jnp.bfloat16)
    for copy, plan, view in zip(copies, plan_in, views):
        copy.wait()
        spread_blocks(FFN_PADDED, [plan], [view], device, spread, None)
    fold_matrices(
        spread, ((gate_weight, 0, D, FF), (up_weight, 0, D, FF), (down_weight, 0, FF, D))
    )
    parts = [slice(low, low + 512) for low in range(0, FF, 512)]
    for at in parts:
        gate = jnp.dot(normed_mid, gate_weight[:, at], preferred_element_type=jnp.float32)
        up = jnp.dot(normed_mid, up_weight[:, at], preferred_element_type=jnp.float32)
        gates[:, at] = gate
        ups[:, at] = up
        hidden[:, at] = gated_gelu(gate, up).astype(jnp.bfloat16)
    ffn_out = jnp.dot(hidden[...], down_weight[...], preferred_element_type=jnp.float32)
    block_out[...] = (mid_stream + rms_scale(ffn_out, gain_last)).astype(jnp.bfloat16)
    delta_out = cotangent[...].astype(jnp.float32) * tables[:, 3 * LANES : 3 * LANES + 1]
    delta_ffn, gain_rows = rms_pull(ffn_out, gain_last, delta_out)
    late_gains[2:3, :] = jnp.sum(gain_rows, axis=0, keepdims=True)
    delta_ffn = delta_ffn.astype(jnp.bfloat16)
    delta_normed = jnp.zeros((CAP, D), jnp.float32)
    for at in parts:
        delta_hidden = times_transposed(delta_ffn, down_weight[at, :])
        gate = gates[:, at]
        raised = jnp.tanh(GELU_SCALE * (gate + 0.044715 * (gate * gate * gate)))
        share = 0.5 * (1.0 + raised)
        slope = share + (0.5 * GELU_SCALE) * gate * (1.0 - raised * raised) * (
            1.0 + (3 * 0.044715) * (gate * gate)
        )
        delta_gate[:, at] = (delta_hidden * ups[:, at] * slope).astype(jnp.bfloat16)
        delta_up[:, at] = (delta_hidden * (gate * share)).astype(jnp.bfloat16)
        delta_normed += times_transposed(delta_gate[:, at], gate_weight[:, at])
        delta_normed += times_transposed(delta_up[:, at], up_weight[:, at])
    delta_part, gain_rows = rms_pull(mid_stream, gain_mid, delta_normed)
    late_gains[1:2, :] = jnp.sum(gain_rows, axis=0, keepdims=True)
    delta_mid = delta_out + delta_part
    delta_mid_ref[...] = delta_mid
    delta_attn, gain_rows = rms_pull(attn_out[...], gain_post, delta_mid)
    late_gains[0:1, :] = jnp.sum(gain_rows, axis=0, keepdims=True)
    delta_attn_ref[...] = delta_attn.astype(jnp.bfloat16)
    turned = normed_mid.T
    spread_grads(
        spread,
        (
            (turned, lambda low, high: delta_gate[:, low:high], FF),
            (turned, lambda low, high: delta_up[:, low:high], FF),
            (hidden[...].T, lambda low, high: delta_ffn[:, low:high], D),
        ),
    )
    place_blocks(FFN_PADDED, plan_out, device, spread, None, targets)


def run_ffn(
    plan_in, staged, plan_out, block_shapes, device, mid, attn_out, cotangent, tables, gains, arrays
):
    flat_rows = G2LEN // LANES + FFN_PADDED
    shapes = [
        jax.ShapeDtypeStruct((CAP, D), jnp.bfloat16),
        jax.ShapeDtypeStruct((CAP, D), jnp.float32),
        jax.ShapeDtypeStruct((CAP, D), jnp.bfloat16),
        jax.ShapeDtypeStruct((3, D), jnp.float32),
    ] + [jax.ShapeDtypeStruct(shape, jnp.bfloat16) for shape in block_shapes]
    wide = pltpu.VMEM((CAP, FF), jnp.float32)
    narrow = pltpu.VMEM((CAP, FF), jnp.bfloat16)
    return pl.pallas_call(
        functools.partial(ffn_kernel, plan_in, staged, plan_out),
        out_shape=shapes,
        in_specs=[pl.BlockSpec(memory_space=pltpu.SMEM)]
        + whole_specs(5)
        + [pl.BlockSpec(memory_space=pltpu.HBM)] * len(arrays),
        out_specs=whole_specs(len(shapes)),
        scratch_shapes=[
            pltpu.VMEM((flat_rows, LANES), jnp.float32),
            pltpu.VMEM((D, FF), jnp.bfloat16),
            pltpu.VMEM((D, FF), jnp.bfloat16),
            pltpu.VMEM((FF, D), jnp.bfloat16),
            wide,
            wide,
            narrow,
            narrow,
            narrow,
            pltpu.SemaphoreType.DMA((len(arrays),)),
        ],
        compiler_params=pltpu.CompilerParams(vmem_limit_bytes=44 << 20),
        cost_estimate=pl.CostEstimate(flops=0, bytes_accessed=0, transcendentals=0),
    )(device, mid, attn_out, cotangent, tables, gains, *arrays)


def attn_back_kernel(
    plan,
    gain_len,
    device_ref,
    delta_attn,
    delta_mid,
    hidden_in,
    tables,
    gains,
    late_gains,
    qkv_weight,
    out_weight,
    grad_in,
    gain_grads,
    *refs,
):
    targets = refs[:-4]
    spread, tails, delta_raws, contexts = refs[-4:]
    device = device_ref[0]
    normed_in, key_raw, values, keys, heads, cos_tab, sin_tab = attn_forward(
        hidden_in, qkv_weight, tables, gains
    )
    gain_query = gains[:, D : D + HD]
    gain_key = gains[:, D + HD : D + 2 * HD]
    delta_context = times_transposed(delta_attn[...], out_weight[...]).astype(jnp.bfloat16)
    delta_key = jnp.zeros((CAP, HD), jnp.float32)
    delta_value = jnp.zeros((CAP, HD), jnp.float32)
    query_gain_rows = jnp.zeros((CAP, HD), jnp.float32)
    for head, (query_raw, queries, scores, log_total, context) in enumerate(heads):
        at = slice(head * HD, (head + 1) * HD)
        contexts[:, at] = context
        head_delta = delta_context[:, at]
        row_dot = jnp.sum(
            head_delta.astype(jnp.float32) * context.astype(jnp.float32), axis=-1, keepdims=True
        )
        prob_exact = jnp.exp(scores - log_total)
        delta_prob = times_transposed(head_delta, values)
        delta_score = prob_exact * (delta_prob - row_dot)
        turned = delta_score.T.astype(jnp.bfloat16)
        delta_score = delta_score.astype(jnp.bfloat16)
        delta_query = jnp.dot(delta_score, keys, preferred_element_type=jnp.float32)
        delta_key += jnp.dot(turned, queries, preferred_element_type=jnp.float32)
        delta_value += jnp.dot(
            prob_exact.T.astype(jnp.bfloat16), head_delta, preferred_element_type=jnp.float32
        )
        delta_rot = rotate_pull(delta_query * HD ** (-0.5), cos_tab, sin_tab)
        delta_raw, gain_rows = rms_pull(query_raw, gain_query, delta_rot)
        query_gain_rows += gain_rows
        delta_raws[:, at] = delta_raw.astype(jnp.bfloat16)
    delta_raw, gain_rows = rms_pull(key_raw, gain_key, rotate_pull(delta_key, cos_tab, sin_tab))
    delta_raws[:, HQ : HQ + HD] = delta_raw.astype(jnp.bfloat16)
    delta_raws[:, HQ + HD :] = delta_value.astype(jnp.bfloat16)
    gain_grads[:, D : D + HD] = jnp.sum(query_gain_rows, axis=0, keepdims=True)
    gain_grads[:, D + HD : D + 2 * HD] = jnp.sum(gain_rows, axis=0, keepdims=True)
    delta_in = times_transposed(delta_raws[...], qkv_weight[...])
    delta_part, gain_rows = rms_pull(
        hidden_in[...].astype(jnp.float32), gains[:, :D], delta_in
    )
    grad_in[...] = delta_mid[...] + delta_part
    gain_grads[:, :D] = jnp.sum(gain_rows, axis=0, keepdims=True)
    for late in range(3):
        at = slice((late + 1) * D + 2 * HD, (late + 2) * D + 2 * HD)
        gain_grads[:, at] = late_gains[late : late + 1, :]
    if gain_len:
        tails[...] = jnp.zeros_like(tails)
        lane = lax.broadcasted_iota(jnp.int32, (1, LANES), 1)
        for owner in range(tails.shape[0]):
            row, shift = divmod(owner * gain_len, LANES)
            piece = gain_grads[:, row * LANES : (row + 1) * LANES]
            if shift:
                piece = pltpu.roll(piece, LANES - shift, 1)
            if shift + gain_len > LANES:
                after = gain_grads[:, (row + 1) * LANES : (row + 2) * LANES]
                after = pltpu.roll(after, LANES - shift, 1)
                piece = jnp.where(lane < LANES - shift, piece, after)
            tails[owner, 0:1, :] = jnp.where(lane < gain_len, piece, 0.0)
    turned = normed_in.T
    delta_attn_value = delta_attn[...]
    spread_grads(
        spread,
        (
            (turned, lambda low, high: delta_raws[:, low:high], HQ),
            (turned, lambda low, high: delta_raws[:, HQ + low : HQ + high], HD),
            (turned, lambda low, high: delta_raws[:, HQ + HD + low : HQ + HD + high], HD),
            (contexts[...].T, lambda low, high: delta_attn_value[:, low:high], D),
        ),
    )
    place_blocks(ATTN_PADDED, plan, device, spread, tails, targets)


def back_attn(plan, gain_len, tail_rows, devices, block_shapes, device, *inputs):
    flat_rows = G1LEN // LANES + ATTN_PADDED
    shapes = [
        jax.ShapeDtypeStruct((CAP, D), jnp.float32),
        jax.ShapeDtypeStruct((1, 4 * D + 2 * HD), jnp.float32),
    ] + [jax.ShapeDtypeStruct(shape, jnp.bfloat16) for shape in block_shapes]
    tail_shape = (devices, tail_rows, LANES) if gain_len else (1, ROWS, LANES)
    return pl.pallas_call(
        functools.partial(attn_back_kernel, plan, gain_len),
        out_shape=shapes,
        in_specs=[pl.BlockSpec(memory_space=pltpu.SMEM)] + whole_specs(len(inputs)),
        out_specs=whole_specs(len(shapes)),
        scratch_shapes=[
            pltpu.VMEM((flat_rows, LANES), jnp.float32),
            pltpu.VMEM(tail_shape, jnp.float32),
            pltpu.VMEM((CAP, HQ + 2 * HD), jnp.bfloat16),
            pltpu.VMEM((CAP, HQ), jnp.bfloat16),
        ],
        compiler_params=pltpu.CompilerParams(vmem_limit_bytes=22 << 20),
        cost_estimate=pl.CostEstimate(flops=0, bytes_accessed=0, transcendentals=0),
    )(device, *inputs)


def gathered_blocks(pieces, chunks, orders, each, devices, device):
    arrays, plan, start = [], [], 0
    for piece, blocks, order in zip(pieces, chunks, orders):
        take = min(piece.shape[0], each - start)
        if each % ROWS:
            places = [offset_of(place, list(order) + [0]) for place in range(devices)]
            back = sorted(range(devices), key=places.__getitem__)
            mixed = offset_bits(device[0], list(order) + [0])
            arrays.append(
                jnp.take(jnp.concatenate(blocks), jnp.array(back, jnp.int32) ^ mixed, axis=0)
            )
            continue
        for part, block in enumerate(blocks):
            plan.append((order[:-1], offset_of(part, [order[-1], 0]), take, start, each))
            arrays.append(block)
        start += take
    if each % ROWS == 0:
        return arrays, plan, None
    table = jnp.concatenate(arrays, axis=1)
    flat = table[:, :each].reshape(1, devices * each, LANES)
    return [flat], [([], 0, devices * each, 0, 0)], table[:, each:]


def offset_bits(device, order):
    return sum(((device >> bit) & 1) << k for k, bit in enumerate(order))


def scatter_plan(each, tail_rows, orders, devices):
    parts = cut_rows(each + tail_rows, len(orders))
    half = devices // 2
    if each % ROWS:
        return [(0, [], 0, 0, devices * each, 0, 0)], [(1, devices * each, LANES)], parts
    plan = []
    for with_core in (1, 0):
        for (low, high), order in zip(parts, orders):
            order = order[::-1]
            plan.append((with_core, order, with_core, low, min(high, each) - low, low, each))
            if high > each:
                plan.append((with_core, order, with_core, each, tail_rows, None, each))
    return plan, [(half, each + tail_rows, LANES)] * 2, parts


def blocks_of(found, tails, parts, orders, devices, device):
    if len(found) == 2:
        return found
    table = found[0].reshape(devices, -1, LANES)
    table = table if tails is None else jnp.concatenate([table, tails], axis=1)
    blocks = []
    for with_core in (0, 1):
        chunks = []
        for (low, high), order in zip(parts, orders):
            places = range(devices // 2)
            offsets = [offset_of(place, order[::-1]) ^ with_core for place in places]
            owners = jnp.array(offsets, jnp.int32) ^ device[0]
            chunks.append(jnp.take(table[:, low:high], owners, axis=0))
        blocks.append(jnp.concatenate(chunks, axis=1))
    return blocks


def merge_kernel(parts, *refs):
    pairs = ((refs[0], refs[1]), (refs[2], refs[3]))
    targets = refs[4:]
    half = refs[0].shape[0] // 2
    for number, target in enumerate(targets):
        chunk, second = divmod(number, 2)

        @pl.loop(0, half)
        def _(index, target=target, chunk=chunk, first=second * half):
            at = 0
            for (home, came), (low, high) in zip(pairs, parts[chunk]):
                total = home[first + index, low:high, :].astype(jnp.float32)
                total += came[first + index, low:high, :].astype(jnp.float32)
                target[index, at : at + high - low, :] = total.astype(jnp.bfloat16)
                at += high - low


def cores_merged(parts, *blocks):
    half = blocks[0].shape[0] // 2
    if any((high - low) % ROWS for chunk in parts for low, high in chunk):
        pairs = (blocks[:2], blocks[2:])
        joined = []
        for chunk in parts:
            sums = [
                home[:, low:high].astype(jnp.float32) + came[:, low:high].astype(jnp.float32)
                for (home, came), (low, high) in zip(pairs, chunk)
            ]
            total = jnp.concatenate(sums, axis=1).astype(jnp.bfloat16)
            joined.append((total[:half], total[half:]))
        return joined
    shapes = [
        jax.ShapeDtypeStruct((half, sum(high - low for low, high in chunk), LANES), jnp.bfloat16)
        for chunk in parts
        for _ in range(2)
    ]
    found = pl.pallas_call(
        functools.partial(merge_kernel, parts),
        out_shape=shapes,
        in_specs=whole_specs(4),
        out_specs=whole_specs(len(shapes)),
        compiler_params=pltpu.CompilerParams(vmem_limit_bytes=20 << 20),
        cost_estimate=pl.CostEstimate(flops=0, bytes_accessed=0, transcendentals=0),
    )(*blocks)
    return list(zip(found[::2], found[1::2]))


def adam_update(weight_shard, gradient, moment_one, moment_two):
    moment_one = 0.9 * moment_one + 0.1 * gradient
    moment_two = 0.999 * moment_two + 0.001 * gradient * gradient
    fix_one = 1.0 - 0.9**STEP
    fix_two = 1.0 - 0.999**STEP
    weight_shard = weight_shard - 0.02 * (
        moment_one / fix_one / (jnp.sqrt(moment_two / fix_two) + 1e-08) + 0.1 * weight_shard
    )
    return (weight_shard, moment_one, moment_two)


def per_device(hidden_in, cotangent, params, moment_one, moment_two, seq_lengths, seq_owner):
    devices = lax.axis_size("dp")
    device = lax.axis_index("dp").astype(jnp.int32)
    here = device.reshape(1)
    attn_len = G1LEN // devices
    ffn_len = G2LEN // devices
    gain_len = params.shape[0] - attn_len - ffn_len
    attn_rows = attn_len // LANES
    tail_rows = -(-(attn_rows + 1) // ROWS) * ROWS - attn_rows
    pad = tail_rows * LANES - gain_len
    rounded = params.astype(jnp.bfloat16)
    first_piece = jnp.concatenate(
        [rounded[:attn_len], rounded[attn_len + ffn_len :], jnp.zeros((pad,), jnp.bfloat16)]
    ).reshape(-1, LANES)
    second_piece = rounded[attn_len : attn_len + ffn_len].reshape(-1, LANES)
    ffn_rows = ffn_len // LANES
    second_pieces = [second_piece[low:high] for low, high in cut_rows(ffn_rows, 2)]
    orders = bit_orders(devices, ("abxy", "bxya", "byax"))
    pieces = [first_piece, *second_pieces]
    chunks = gather_chunks(pieces, orders, devices)
    arrays, plan, tails = gathered_blocks(
        pieces[:1], chunks[:1], orders[:1], attn_rows, devices, here
    )
    ffn_arrays, ffn_plan, unused = gathered_blocks(
        pieces[1:], chunks[1:], orders[1:], ffn_rows, devices, here
    )
    aligned = attn_rows % ROWS == 0
    tables = slot_setup(seq_lengths, seq_owner, device)
    given = None
    if not aligned:
        given = tails.reshape(devices, -1)[:, :gain_len].astype(jnp.float32).reshape(1, -1)
    qkv_weight, out_weight, gains, attn_out, mid_stream = forward_attn(
        plan,
        gain_len if aligned else 0,
        tail_rows,
        devices,
        here,
        hidden_in,
        tables,
        given,
        arrays,
    )
    orders = bit_orders(devices, ("yxba", "ayxb", "xayb"))
    out_plan, block_shapes, ffn_parts = scatter_plan(ffn_rows, 0, orders, devices)
    staged = [(0, 0, 0)]
    if len(block_shapes) == 2:
        staged = [
            (part // 2, part % 2 * (devices // 4), low)
            for low, _ in cut_rows(ffn_rows, 2)
            for part in range(4)
        ]
    block_out, delta_mid, delta_attn, late_gains, *found = run_ffn(
        ffn_plan,
        staged,
        out_plan,
        block_shapes,
        here,
        mid_stream,
        attn_out,
        cotangent,
        tables,
        gains,
        ffn_arrays,
    )
    ffn_home, ffn_away = blocks_of(found, None, ffn_parts, orders, devices, here)
    ffn_came = across(ffn_away, 0, devices)
    attn_plan, block_shapes, attn_parts = scatter_plan(attn_rows, tail_rows, orders, devices)
    grad_in, gain_grads, *found = back_attn(
        attn_plan,
        gain_len if aligned else 0,
        tail_rows,
        devices,
        block_shapes,
        here,
        delta_attn,
        delta_mid,
        hidden_in,
        tables,
        gains,
        late_gains,
        qkv_weight,
        out_weight,
    )
    gain_table = None
    if not aligned:
        gain_table = gain_grads.reshape(devices, gain_len).astype(jnp.bfloat16)
        gain_table = jnp.pad(gain_table, ((0, 0), (0, pad))).reshape(devices, tail_rows, LANES)
    attn_home, attn_away = blocks_of(found, gain_table, attn_parts, orders, devices, here)
    attn_came = across(attn_away, 0, devices)
    parts = [
        [cut[chunk] for cut in (ffn_parts, attn_parts) if chunk < len(cut)]
        for chunk in range(len(ffn_parts))
    ]
    chunks = cores_merged(parts, ffn_home, ffn_came, attn_home, attn_came)
    for stage in range(len(orders[0])):
        chunks = merged_blocks(chunks, sent_blocks(chunks, orders, stage, devices))
    rows = [chunk for chunk, _ in chunks]
    ffn_take = [high - low for low, high in ffn_parts]
    ffn_shard = [chunk[:take].reshape(-1) for chunk, take in zip(rows, ffn_take)]
    attn_shard = jnp.concatenate([chunk[take:].reshape(-1) for chunk, take in zip(rows, ffn_take)])
    grad_shard = jnp.concatenate(
        [attn_shard[:attn_len], *ffn_shard, attn_shard[attn_len : attn_len + gain_len]]
    )
    params_new, moment_one_new, moment_two_new = adam_update(
        params, grad_shard, moment_one, moment_two
    )
    return (block_out, grad_in, grad_shard, params_new, moment_one_new, moment_two_new)


def solution(mesh):
    in_specs = (P("dp", None), P("dp", None), P("dp"), P("dp"), P("dp"), P(), P())
    out_specs = (P("dp", None), P("dp", None), P("dp"), P("dp"), P("dp"), P("dp"))
    return jax.shard_map(
        per_device, mesh=mesh, in_specs=in_specs, out_specs=out_specs, check_vma=False
    )
```

profile of v0, /device:TPU:0, one launch (start us, length us, event | category | flops | bytes accessed | tf_op | source)
XLA Modules:
  0.0 179.6 jit_solution(18404986707241800972)
XLA Ops:
  2.5 3.0 %collective-permute-start = (bf16[1,416,128]{2,1,0:T(8,128)(2,1)S(1)}, bf16[1,416,128]{2,1,0:T(8,128)(2,1)S(1)}, u32[]{:S(2)}, u32[]{:S(2)}) collective-permute-start(bf16[1,416,128]{2,1,0:T(8,128)(2,1)S(1)} %bitcast.26), channel_id=1, source_target_pairs={{0,8},{1,9},{2,10},{3,11},{4,12},{5,13},{6,14},{7,15},{8,0},{9,1},... | collective-permute-start | bytes 319496 | tf_op jit(solution)/shard_map/ppermute | solution.py:112
  5.5 3.0 %collective-permute-done = bf16[1,416,128]{2,1,0:T(8,128)(2,1)S(1)} collective-permute-done((bf16[1,416,128]{2,1,0:T(8,128)(2,1)S(1)}, bf16[1,416,128]{2,1,0:T(8,128)(2,1)S(1)}, u32[]{:S(2)}, u32[]{:S(2)}) %collective-permute-start) | collective-permute-done | bytes 106528 | tf_op jit(solution)/shard_map/ppermute | solution.py:112
  8.5 2.8 %collective-permute-start.1 = (bf16[2,416,128]{2,1,0:T(8,128)(2,1)S(1)}, bf16[2,416,128]{2,1,0:T(8,128)(2,1)S(1)}, u32[]{:S(2)}, u32[]{:S(2)}) collective-permute-start(bf16[2,416,128]{2,1,0:T(8,128)(2,1)S(1)} %pad_maximum_fusion.9), channel_id=1, source_target_pairs={{0,16},{1,17},{2,18},{3,19},{4,20},{5,21},{6,22},{7,23},{8,24},{9,... | collective-permute-start | bytes 638984 | tf_op jit(solution)/shard_map/ppermute | solution.py:112
  11.6 12.3 %collective-permute-done.1 = bf16[2,416,128]{2,1,0:T(8,128)(2,1)S(1)} collective-permute-done((bf16[2,416,128]{2,1,0:T(8,128)(2,1)S(1)}, bf16[2,416,128]{2,1,0:T(8,128)(2,1)S(1)}, u32[]{:S(2)}, u32[]{:S(2)}) %collective-permute-start.1) | collective-permute-done | bytes 213024 | tf_op jit(solution)/shard_map/ppermute | solution.py:112
  23.9 1.6 collective-permute-start.2
  26.9 8.0 %collective-permute-done.12 = bf16[1,480,128]{2,1,0:T(8,128)(2,1)S(1)} collective-permute-done((bf16[1,480,128]{2,1,0:T(8,128)(2,1)S(1)}, bf16[1,480,128]{2,1,0:T(8,128)(2,1)S(1)}, u32[]{:S(2)}, u32[]{:S(2)}) %collective-permute-start.12) | collective-permute-done | bytes 122912 | tf_op jit(solution)/shard_map/ppermute | solution.py:112
  34.9 1.6 collective-permute-start.13
  36.5 3.0 %collective-permute-done.7 = bf16[2,480,128]{2,1,0:T(8,128)(2,1)S(1)} collective-permute-done((bf16[2,480,128]{2,1,0:T(8,128)(2,1)S(1)}, bf16[2,480,128]{2,1,0:T(8,128)(2,1)S(1)}, u32[]{:S(2)}, u32[]{:S(2)}) %collective-permute-start.7) | collective-permute-done | bytes 245792 | tf_op jit(solution)/shard_map/ppermute | solution.py:112
  43.0 10.9 %collective-permute-done.8 = bf16[4,480,128]{2,1,0:T(8,128)(2,1)S(1)} collective-permute-done((bf16[4,480,128]{2,1,0:T(8,128)(2,1)S(1)}, bf16[4,480,128]{2,1,0:T(8,128)(2,1)S(1)}, u32[]{:S(2)}, u32[]{:S(2)}) %collective-permute-start.8) | collective-permute-done | bytes 491552 | tf_op jit(solution)/shard_map/ppermute | solution.py:112
  57.6 14.2 %collective-permute-done.3.refs_1_ = bf16[8,416,128]{2,1,0:T(8,128)(2,1)} collective-permute-done((bf16[8,416,128]{2,1,0:T(8,128)(2,1)S(1)}, bf16[8,416,128]{2,1,0:T(8,128)(2,1)}, u32[]{:S(2)}, u32[]{:S(2)}) %collective-permute-start.3) | collective-permute-done | bytes 852000 | tf_op jit(solution)/shard_map/ppermute | solution.py:112
  72.2 6.2 %collective-permute-done.9.refs_1_ = bf16[8,480,128]{2,1,0:T(8,128)(2,1)} collective-permute-done((bf16[8,480,128]{2,1,0:T(8,128)(2,1)S(1)}, bf16[8,480,128]{2,1,0:T(8,128)(2,1)}, u32[]{:S(2)}, u32[]{:S(2)}) %collective-permute-start.9) | collective-permute-done | bytes 983072 | tf_op jit(solution)/shard_map/ppermute | solution.py:112
  81.1 4.4 %shard_map.118 = (bf16[640,1536]{1,0:T(8,128)(2,1)S(1)}, bf16[1024,640]{1,0:T(8,128)(2,1)S(1)}, f32[1,3072]{1,0:T(1,128)S(1)}, f32[128,640]{1,0:T(8,128)S(1)}, f32[128,640]{1,0:T(8,128)S(1)}) custom-call(s32[1]{0:T(128)} %bitcast.device_ref, bf16[128,640]{1,0:T(8,128)(2,1)S(1)} %copy-done.3, f32[128,512]{1,0:T(8,128)S(1)} %pad_maximum_fusion.6.tables, ...), custom_call_target="tpu_custom_call" | custom-call | bytes 67108864 | tf_op jit(solution)/shard_map/pallas_call | solution.py:429
  85.5 19.3 %shard_map.119 = (bf16[128,640]{1,0:T(8,128)(2,1)}, f32[128,640]{1,0:T(8,128)S(1)}, bf16[128,640]{1,0:T(8,128)(2,1)S(1)}, f32[3,640]{1,0:T(4,128)S(1)}, bf16[16,...) custom-call(s32[1]{0:T(128)} %bitcast.device_ref, f32[128,640]{1,0:T(8,128)S(1)} %get-tuple-element.38.mid_ref, ...), custom_call_target="tpu_custom_call" | custom-call | tf_op jit(solution)/shard_map/pallas_call | solution.py:549
  105.4 6.1 %shard_map.120 = (f32[128,640]{1,0:T(8,128)}, f32[1,3072]{1,0:T(1,128)}, bf16[16,416,128]{2,1,0:T(8,128)(2,1)S(1)}, bf16[16,416,128]{2,1,0:T(8,128)(2,1)S(1)}) custom-call(s32[1]{0:T(128)} %bitcast.device_ref, bf16[128,640]{1,0:T(8,128)(2,1)S(1)} %get-tuple-element.52.delta_attn, f32[128,640]{1,0:T(8,128)S(1)} %get-tuple-element.53.delta_mid, ...), custom_call_target="tpu_custom_call" | custom-call | tf_op jit(solution)/shard_map/pallas_call | solution.py:670
  111.6 3.6 %collective-permute-done.19.refs_3_ = bf16[16,416,128]{2,1,0:T(8,128)(2,1)S(1)} collective-permute-done((bf16[16,416,128]{2,1,0:T(8,128)(2,1)S(1)}, bf16[16,416,128]{2,1,0:T(8,128)(2,1)S(1)}, u32[]{:S(2)}, u32[]{:S(2)}) %collective-permute-start.19) | collective-permute-done | bytes 1703968 | tf_op jit(solution)/shard_map/ppermute | solution.py:112
  120.1 19.1 %collective-permute-done.28 = bf16[8,448,128]{2,1,0:T(8,128)(2,1)S(1)} collective-permute-done((bf16[8,448,128]{2,1,0:T(8,128)(2,1)S(1)}, bf16[8,448,128]{2,1,0:T(8,128)(2,1)S(1)}, u32[]{:S(2)}, u32[]{:S(2)}) %collective-permute-start.28) | collective-permute-done | bytes 917536 | tf_op jit(solution)/shard_map/ppermute | solution.py:112
  143.8 8.4 %collective-permute-done.29 = bf16[4,448,128]{2,1,0:T(8,128)(2,1)S(1)} collective-permute-done((bf16[4,448,128]{2,1,0:T(8,128)(2,1)S(1)}, bf16[4,448,128]{2,1,0:T(8,128)(2,1)S(1)}, u32[]{:S(2)}, u32[]{:S(2)}) %collective-permute-start.29) | collective-permute-done | bytes 458784 | tf_op jit(solution)/shard_map/ppermute | solution.py:112
  153.3 3.4 %collective-permute-start.22 = (bf16[2,464,128]{2,1,0:T(8,128)(2,1)S(1)}, bf16[2,464,128]{2,1,0:T(8,128)(2,1)S(1)}, u32[]{:S(2)}, u32[]{:S(2)}) collective-permute-start(bf16[2,464,128]{2,1,0:T(8,128)(2,1)S(1)} %get-tuple-element.82), channel_id=1, source_target_pairs={{0,16},{1,17},{2,18},{3,19},{4,20},{5,21},{6,22},{7,23},{8,24},{9,... | collective-permute-start | bytes 712712 | tf_op jit(solution)/shard_map/ppermute | solution.py:112
  159.1 3.4 %collective-permute-start.31 = (bf16[1,448,128]{2,1,0:T(8,128)(2,1)S(1)}, bf16[1,448,128]{2,1,0:T(8,128)(2,1)S(1)}, u32[]{:S(2)}, u32[]{:S(2)}) collective-permute-start(bf16[1,448,128]{2,1,0:T(8,128)(2,1)S(1)} %add_convert_fusion.16), channel_id=1, source_target_pairs={{0,16},{1,17},{2,18},{3,19},{4,20},{5,21},{6,22},{7,23},{8,24},{9,... | collective-permute-start | bytes 344072 | tf_op jit(solution)/shard_map/ppermute | solution.py:112
  162.5 6.3 %collective-permute-done.22 = bf16[2,464,128]{2,1,0:T(8,128)(2,1)S(1)} collective-permute-done((bf16[2,464,128]{2,1,0:T(8,128)(2,1)S(1)}, bf16[2,464,128]{2,1,0:T(8,128)(2,1)S(1)}, u32[]{:S(2)}, u32[]{:S(2)}) %collective-permute-start.22) | collective-permute-done | bytes 237600 | tf_op jit(solution)/shard_map/ppermute | solution.py:112
  169.7 3.4 %collective-permute-start.27 = (bf16[1,464,128]{2,1,0:T(8,128)(2,1)S(1)}, bf16[1,464,128]{2,1,0:T(8,128)(2,1)S(1)}, u32[]{:S(2)}, u32[]{:S(2)}) collective-permute-start(bf16[1,464,128]{2,1,0:T(8,128)(2,1)S(1)} %add_convert_fusion.12), channel_id=1, source_target_pairs={{0,16},{1,17},{2,18},{3,19},{4,20},{5,21},{6,22},{7,23},{8,24},{9,... | collective-permute-start | bytes 356360 | tf_op jit(solution)/shard_map/ppermute | solution.py:112
  173.2 2.3 %collective-permute-done.23 = bf16[1,464,128]{2,1,0:T(8,128)(2,1)S(1)} collective-permute-done((bf16[1,464,128]{2,1,0:T(8,128)(2,1)S(1)}, bf16[1,464,128]{2,1,0:T(8,128)(2,1)S(1)}, u32[]{:S(2)}, u32[]{:S(2)}) %collective-permute-start.23) | collective-permute-done | bytes 118816 | tf_op jit(solution)/shard_map/ppermute | solution.py:112
  175.6 2.1 %collective-permute-done.27 = bf16[1,464,128]{2,1,0:T(8,128)(2,1)S(1)} collective-permute-done((bf16[1,464,128]{2,1,0:T(8,128)(2,1)S(1)}, bf16[1,464,128]{2,1,0:T(8,128)(2,1)S(1)}, u32[]{:S(2)}, u32[]{:S(2)}) %collective-permute-start.27) | collective-permute-done | bytes 118816 | tf_op jit(solution)/shard_map/ppermute | solution.py:112
  177.9 1.7 multiply_subtract_fusion
  (116 shorter events, 28.4 us)
Async XLA Ops:
  8.5 15.3 %collective-permute-start.1 = (bf16[2,416,128]{2,1,0:T(8,128)(2,1)S(1)}, bf16[2,416,128]{2,1,0:T(8,128)(2,1)S(1)}, u32[]{:S(2)}, u32[]{:S(2)}) collective-permute-start(bf16[2,416,128]{2,1,0:T(8,128)(2,1)S(1)} %pad_maximum_fusion.9), channel_id=1, source_target_pairs={{0,16},{1,17},{2,18},{3,19},{4,20},{5,21},{6,22},{7,23},{8,24},{9,... | collective-permute-start | bytes 638984 | tf_op jit(solution)/shard_map/ppermute | solution.py:112
  11.3 14.4 %collective-permute-start.6 = (bf16[1,480,128]{2,1,0:T(8,128)(2,1)S(1)}, bf16[1,480,128]{2,1,0:T(8,128)(2,1)S(1)}, u32[]{:S(2)}, u32[]{:S(2)}) collective-permute-start(bf16[1,480,128]{2,1,0:T(8,128)(2,1)S(1)} %get-tuple-element.88), channel_id=1, source_target_pairs={{0,16},{1,17},{2,18},{3,19},{4,20},{5,21},{6,22},{7,23},{8,24},{9,... | collective-permute-start | bytes 368648 | tf_op jit(solution)/shard_map/ppermute | solution.py:112
  23.9 15.7 %collective-permute-start.2 = (bf16[4,416,128]{2,1,0:T(8,128)(2,1)S(1)}, bf16[4,416,128]{2,1,0:T(8,128)(2,1)S(1)}, u32[]{:S(2)}, u32[]{:S(2)}) collective-permute-start(bf16[4,416,128]{2,1,0:T(8,128)(2,1)S(1)} %pad_maximum_fusion.5), channel_id=1, source_target_pairs={{0,2},{1,3},{2,0},{3,1},{4,6},{5,7},{6,4},{7,5},{8,10},{9,11},{10,... | collective-permute-start | bytes 1277960 | tf_op jit(solution)/shard_map/ppermute | solution.py:112
  25.8 13.8 %collective-permute-start.7 = (bf16[2,480,128]{2,1,0:T(8,128)(2,1)S(1)}, bf16[2,480,128]{2,1,0:T(8,128)(2,1)S(1)}, u32[]{:S(2)}, u32[]{:S(2)}) collective-permute-start(bf16[2,480,128]{2,1,0:T(8,128)(2,1)S(1)} %pad_maximum_fusion.7), channel_id=1, source_target_pairs={{0,2},{1,3},{2,0},{3,1},{4,6},{5,7},{6,4},{7,5},{8,10},{9,11},{10,... | collective-permute-start | bytes 737288 | tf_op jit(solution)/shard_map/ppermute | solution.py:112
  26.9 8.0 %collective-permute-start.12 = (bf16[1,480,128]{2,1,0:T(8,128)(2,1)S(1)}, bf16[1,480,128]{2,1,0:T(8,128)(2,1)S(1)}, u32[]{:S(2)}, u32[]{:S(2)}) collective-permute-start(bf16[1,480,128]{2,1,0:T(8,128)(2,1)S(1)} %get-tuple-element.87), channel_id=1, source_target_pairs={{0,16},{1,17},{2,18},{3,19},{4,20},{5,21},{6,22},{7,23},{8,24},{9,... | collective-permute-start | bytes 368648 | tf_op jit(solution)/shard_map/ppermute | solution.py:112
  39.7 17.0 %collective-permute-start.4 = (bf16[8,416,128]{2,1,0:T(8,128)(2,1)S(1)}, bf16[8,416,128]{2,1,0:T(8,128)(2,1)S(1)}, u32[]{:S(2)}, u32[]{:S(2)}) collective-permute-start(bf16[8,416,128]{2,1,0:T(8,128)(2,1)S(1)} %pad_maximum_fusion.2.refs_0_), channel_id=1, source_target_pairs={{0,1},{1,0},{2,3},{3,2},{4,5},{5,4},{6,7},{7,6},{8,9},{9,8},{10,11... | collective-permute-start | bytes 2555912 | tf_op jit(solution)/shard_map/ppermute | solution.py:112
  39.8 14.1 %collective-permute-start.8 = (bf16[4,480,128]{2,1,0:T(8,128)(2,1)S(1)}, bf16[4,480,128]{2,1,0:T(8,128)(2,1)S(1)}, u32[]{:S(2)}, u32[]{:S(2)}) collective-permute-start(bf16[4,480,128]{2,1,0:T(8,128)(2,1)S(1)} %pad_maximum_fusion.3), channel_id=1, source_target_pairs={{0,4},{1,5},{2,6},{3,7},{4,0},{5,1},{6,2},{7,3},{8,12},{9,13},{10,... | collective-permute-start | bytes 1474568 | tf_op jit(solution)/shard_map/ppermute | solution.py:112
  41.2 30.7 %collective-permute-start.3 = (bf16[8,416,128]{2,1,0:T(8,128)(2,1)S(1)}, bf16[8,416,128]{2,1,0:T(8,128)(2,1)}, u32[]{:S(2)}, u32[]{:S(2)}) collective-permute-start(bf16[8,416,128]{2,1,0:T(8,128)(2,1)S(1)} %pad_maximum_fusion.2.refs_0_), channel_id=1, source_target_pairs={{0,4},{1,5},{2,6},{3,7},{4,0},{5,1},{6,2},{7,3},{8,12},{9,13},{10,... | collective-permute-start | bytes 2555912 | tf_op jit(solution)/shard_map/ppermute | solution.py:112
  42.8 12.3 %collective-permute-start.14 = (bf16[4,480,128]{2,1,0:T(8,128)(2,1)S(1)}, bf16[4,480,128]{2,1,0:T(8,128)(2,1)S(1)}, u32[]{:S(2)}, u32[]{:S(2)}) collective-permute-start(bf16[4,480,128]{2,1,0:T(8,128)(2,1)S(1)} %pad_maximum_fusion.4), channel_id=1, source_target_pairs={{0,8},{1,9},{2,10},{3,11},{4,12},{5,13},{6,14},{7,15},{8,0},{9,1},... | collective-permute-start | bytes 1474568 | tf_op jit(solution)/shard_map/ppermute | solution.py:112
  54.0 24.4 %collective-permute-start.10 = (bf16[8,480,128]{2,1,0:T(8,128)(2,1)S(1)}, bf16[8,480,128]{2,1,0:T(8,128)(2,1)}, u32[]{:S(2)}, u32[]{:S(2)}) collective-permute-start(bf16[8,480,128]{2,1,0:T(8,128)(2,1)S(1)} %pad_maximum_fusion.refs_0_), channel_id=1, source_target_pairs={{0,1},{1,0},{2,3},{3,2},{4,5},{5,4},{6,7},{7,6},{8,9},{9,8},{10,11... | collective-permute-start | bytes 2949128 | tf_op jit(solution)/shard_map/ppermute | solution.py:112
  54.1 24.3 %collective-permute-start.9 = (bf16[8,480,128]{2,1,0:T(8,128)(2,1)S(1)}, bf16[8,480,128]{2,1,0:T(8,128)(2,1)}, u32[]{:S(2)}, u32[]{:S(2)}) collective-permute-start(bf16[8,480,128]{2,1,0:T(8,128)(2,1)S(1)} %pad_maximum_fusion.refs_0_), channel_id=1, source_target_pairs={{0,8},{1,9},{2,10},{3,11},{4,12},{5,13},{6,14},{7,15},{8,0},{9,1},... | collective-permute-start | bytes 2949128 | tf_op jit(solution)/shard_map/ppermute | solution.py:112
  55.2 23.9 %collective-permute-start.15 = (bf16[8,480,128]{2,1,0:T(8,128)(2,1)S(1)}, bf16[8,480,128]{2,1,0:T(8,128)(2,1)}, u32[]{:S(2)}, u32[]{:S(2)}) collective-permute-start(bf16[8,480,128]{2,1,0:T(8,128)(2,1)S(1)} %pad_maximum_fusion.1.refs_4_), channel_id=1, source_target_pairs={{0,2},{1,3},{2,0},{3,1},{4,6},{5,7},{6,4},{7,5},{8,10},{9,11},{10,... | collective-permute-start | bytes 2949128 | tf_op jit(solution)/shard_map/ppermute | solution.py:112
  57.6 21.5 %collective-permute-start.16 = (bf16[8,480,128]{2,1,0:T(8,128)(2,1)S(1)}, bf16[8,480,128]{2,1,0:T(8,128)(2,1)}, u32[]{:S(2)}, u32[]{:S(2)}) collective-permute-start(bf16[8,480,128]{2,1,0:T(8,128)(2,1)S(1)} %pad_maximum_fusion.1.refs_4_), channel_id=1, source_target_pairs={{0,1},{1,0},{2,3},{3,2},{4,5},{5,4},{6,7},{7,6},{8,9},{9,8},{10,11... | collective-permute-start | bytes 2949128 | tf_op jit(solution)/shard_map/ppermute | solution.py:112
  104.9 10.3 %collective-permute-start.18 = (bf16[16,960,128]{2,1,0:T(8,128)(2,1)}, bf16[16,960,128]{2,1,0:T(8,128)(2,1)S(1)}, u32[]{:S(2)}, u32[]{:S(2)}) collective-permute-start(bf16[16,960,128]{2,1,0:T(8,128)(2,1)} %get-tuple-element.59), channel_id=1, source_target_pairs={{0,1},{1,0},{2,3},{3,2},{4,5},{5,4},{6,7},{7,6},{8,9},{9,8},{10,11... | collective-permute-start | bytes 11796488 | tf_op jit(solution)/shard_map/ppermute | solution.py:112
  116.7 22.5 %collective-permute-start.28 = (bf16[8,448,128]{2,1,0:T(8,128)(2,1)S(1)}, bf16[8,448,128]{2,1,0:T(8,128)(2,1)S(1)}, u32[]{:S(2)}, u32[]{:S(2)}) collective-permute-start(bf16[8,448,128]{2,1,0:T(8,128)(2,1)S(1)} %get-tuple-element.67), channel_id=1, source_target_pairs={{0,2},{1,3},{2,0},{3,1},{4,6},{5,7},{6,4},{7,5},{8,10},{9,11},{10,... | collective-permute-start | bytes 2752520 | tf_op jit(solution)/shard_map/ppermute | solution.py:112
  118.2 22.8 %collective-permute-start.20 = (bf16[8,464,128]{2,1,0:T(8,128)(2,1)S(1)}, bf16[8,464,128]{2,1,0:T(8,128)(2,1)S(1)}, u32[]{:S(2)}, u32[]{:S(2)}) collective-permute-start(bf16[8,464,128]{2,1,0:T(8,128)(2,1)S(1)} %get-tuple-element.63), channel_id=1, source_target_pairs={{0,4},{1,5},{2,6},{3,7},{4,0},{5,1},{6,2},{7,3},{8,12},{9,13},{10,... | collective-permute-start | bytes 2850824 | tf_op jit(solution)/shard_map/ppermute | solution.py:112
  119.8 23.4 %collective-permute-start.24 = (bf16[8,464,128]{2,1,0:T(8,128)(2,1)S(1)}, bf16[8,464,128]{2,1,0:T(8,128)(2,1)S(1)}, u32[]{:S(2)}, u32[]{:S(2)}) collective-permute-start(bf16[8,464,128]{2,1,0:T(8,128)(2,1)S(1)} %get-tuple-element.65), channel_id=1, source_target_pairs={{0,8},{1,9},{2,10},{3,11},{4,12},{5,13},{6,14},{7,15},{8,0},{9,1},... | collective-permute-start | bytes 2850824 | tf_op jit(solution)/shard_map/ppermute | solution.py:112
  139.4 12.7 %collective-permute-start.29 = (bf16[4,448,128]{2,1,0:T(8,128)(2,1)S(1)}, bf16[4,448,128]{2,1,0:T(8,128)(2,1)S(1)}, u32[]{:S(2)}, u32[]{:S(2)}) collective-permute-start(bf16[4,448,128]{2,1,0:T(8,128)(2,1)S(1)} %get-tuple-element.80), channel_id=1, source_target_pairs={{0,8},{1,9},{2,10},{3,11},{4,12},{5,13},{6,14},{7,15},{8,0},{9,1},... | collective-permute-start | bytes 1376264 | tf_op jit(solution)/shard_map/ppermute | solution.py:112
  141.3 11.8 %collective-permute-start.21 = (bf16[4,464,128]{2,1,0:T(8,128)(2,1)S(1)}, bf16[4,464,128]{2,1,0:T(8,128)(2,1)S(1)}, u32[]{:S(2)}, u32[]{:S(2)}) collective-permute-start(bf16[4,464,128]{2,1,0:T(8,128)(2,1)S(1)} %get-tuple-element.76), channel_id=1, source_target_pairs={{0,2},{1,3},{2,0},{3,1},{4,6},{5,7},{6,4},{7,5},{8,10},{9,11},{10,... | collective-permute-start | bytes 1425416 | tf_op jit(solution)/shard_map/ppermute | solution.py:112
  143.4 13.3 %collective-permute-start.25 = (bf16[4,464,128]{2,1,0:T(8,128)(2,1)S(1)}, bf16[4,464,128]{2,1,0:T(8,128)(2,1)S(1)}, u32[]{:S(2)}, u32[]{:S(2)}) collective-permute-start(bf16[4,464,128]{2,1,0:T(8,128)(2,1)S(1)} %get-tuple-element.78), channel_id=1, source_target_pairs={{0,4},{1,5},{2,6},{3,7},{4,0},{5,1},{6,2},{7,3},{8,12},{9,13},{10,... | collective-permute-start | bytes 1425416 | tf_op jit(solution)/shard_map/ppermute | solution.py:112
  153.3 15.6 %collective-permute-start.22 = (bf16[2,464,128]{2,1,0:T(8,128)(2,1)S(1)}, bf16[2,464,128]{2,1,0:T(8,128)(2,1)S(1)}, u32[]{:S(2)}, u32[]{:S(2)}) collective-permute-start(bf16[2,464,128]{2,1,0:T(8,128)(2,1)S(1)} %get-tuple-element.82), channel_id=1, source_target_pairs={{0,16},{1,17},{2,18},{3,19},{4,20},{5,21},{6,22},{7,23},{8,24},{9,... | collective-permute-start | bytes 712712 | tf_op jit(solution)/shard_map/ppermute | solution.py:112
  156.8 12.8 %collective-permute-start.26 = (bf16[2,464,128]{2,1,0:T(8,128)(2,1)S(1)}, bf16[2,464,128]{2,1,0:T(8,128)(2,1)S(1)}, u32[]{:S(2)}, u32[]{:S(2)}) collective-permute-start(bf16[2,464,128]{2,1,0:T(8,128)(2,1)S(1)} %get-tuple-element.84), channel_id=1, source_target_pairs={{0,2},{1,3},{2,0},{3,1},{4,6},{5,7},{6,4},{7,5},{8,10},{9,11},{10,... | collective-permute-start | bytes 712712 | tf_op jit(solution)/shard_map/ppermute | solution.py:112
  159.1 14.0 %collective-permute-start.31 = (bf16[1,448,128]{2,1,0:T(8,128)(2,1)S(1)}, bf16[1,448,128]{2,1,0:T(8,128)(2,1)S(1)}, u32[]{:S(2)}, u32[]{:S(2)}) collective-permute-start(bf16[1,448,128]{2,1,0:T(8,128)(2,1)S(1)} %add_convert_fusion.16), channel_id=1, source_target_pairs={{0,16},{1,17},{2,18},{3,19},{4,20},{5,21},{6,22},{7,23},{8,24},{9,... | collective-permute-start | bytes 344072 | tf_op jit(solution)/shard_map/ppermute | solution.py:112
  169.7 8.0 %collective-permute-start.27 = (bf16[1,464,128]{2,1,0:T(8,128)(2,1)S(1)}, bf16[1,464,128]{2,1,0:T(8,128)(2,1)S(1)}, u32[]{:S(2)}, u32[]{:S(2)}) collective-permute-start(bf16[1,464,128]{2,1,0:T(8,128)(2,1)S(1)} %add_convert_fusion.12), channel_id=1, source_target_pairs={{0,16},{1,17},{2,18},{3,19},{4,20},{5,21},{6,22},{7,23},{8,24},{9,... | collective-permute-start | bytes 356360 | tf_op jit(solution)/shard_map/ppermute | solution.py:112
  (19 other events, 187.3 us)
where the time goes:
time: 180 us
  waiting for transfers between devices  104 us (58%)
  starting transfers between devices  34.5 us (19%)
  Pallas kernels  31.4 us (17%)
  other arithmetic  5.63 us (3%)
  local copies, waits for them, and re-layouts  3.06 us (2%)
    ppermute x32, waiting for transfers between devices, across(): lax.ppermute(block, 'dp', [(i, i ^ 1 << bit) for i in range(devices)])  104 us
    ppermute x32, starting transfers between devices, across(): lax.ppermute(block, 'dp', [(i, i ^ 1 << bit) for i in range(devices)])  34.5 us
    pallas_call x1, Pallas kernels, run_ffn(): pl.pallas_call(functools.partial(ffn_kernel, plan_in, staged, plan_out),...  19.3 us
    pallas_call x1, Pallas kernels, back_attn(): pl.pallas_call(functools.partial(attn_back_kernel, plan, gain_len), out_s...  6.12 us
    pallas_call x1, Pallas kernels, forward_attn(): pl.pallas_call(functools.partial(attn_forward_kernel, plan, gain_len), ou...  4.41 us
  transfers between devices with their start and end apart: 32, of which 21 were waited for; matrix products, arithmetic and copies ran while one was open for 2% of the time, Pallas kernels for 6%

commit v1 on v0

--- a/solution.py
+++ b/solution.py
@@ -116,22 +116,12 @@
     return sum(((place >> k) & 1) << bit for k, bit in enumerate(order))
 
 
-def gather_chunks(pieces, orders, devices):
-    held = [piece[None] for piece in pieces]
-    for stage in range(len(orders[0]) - 1):
-        came = [across(block, order[stage], devices) for block, order in zip(held, orders)]
-        for chunk in range(1, len(came)):
-            came[chunk] = lax.optimization_barrier((came[chunk], came[0]))[0]
-        held = [jnp.concatenate(pair) for pair in zip(held, came)]
-    last = [across(block, order[-1], devices) for block, order in zip(held, orders)]
-    chunks = []
-    for block, final in zip(held, last):
-        if chunks:
-            final = lax.optimization_barrier((final, chunks[0][-1]))[0]
-        beside = across(block, 0, devices)
-        final = lax.optimization_barrier((final, beside))[0]
-        chunks.append((block, final, beside, across(final, 0, devices)))
-    return chunks
+def gather_chunk(piece, order, devices):
+    held = piece[None]
+    for bit in order[:-1]:
+        held = jnp.concatenate([held, across(held, bit, devices)])
+    last = across(held, order[-1], devices)
+    return (held, last, across(held, 0, devices), across(last, 0, devices))
 
 
 def sent_blocks(chunks, orders, stage, devices):
@@ -248,8 +238,10 @@
                 ].astype(jnp.float32)
 
             each_piece(padded, first, take, spread_unit)
-            if tails is not None:
-                tails[owner] = block_ref[index, take : take + tails.shape[1], :]
+            if tails is not None and start + take == each:
+                tails[owner] = block_ref[
+                    first_index + index, first_row + take : first_row + take + tails.shape[1], :
+                ]
 
 
 def pitch_of(columns):
@@ -369,7 +361,7 @@
         gains[:, number * LANES : (number + 1) * LANES] = tile
 
 
-def attn_forward_kernel(plan, gain_len, device_ref, hidden_in, tables, *refs):
+def attn_forward_kernel(plan, windows, gain_len, device_ref, hidden_in, tables, *refs):
     if not gain_len:
         given, refs = refs[0], refs[1:]
     sources = refs[: len(plan)]
@@ -377,11 +369,16 @@
     qkv_weight, out_weight, gains, attn_out, mid_stream = refs[:5]
     staging, spread, tails, context, sems = refs[5:]
     copies, views = [], []
-    for number, source in enumerate(sources):
+    for number, (source, (low, rows)) in enumerate(zip(sources, windows)):
         count = source.shape[0]
-        held = staging.at[pl.ds(number * count, count)]
-        copies.append(pltpu.make_async_copy(source, held, sems.at[number]))
-        views.append((held, 0, count, 0))
+        copies.append(
+            pltpu.make_async_copy(
+                source.at[:, pl.ds(low, rows), :],
+                staging.at[pl.ds(number * count, count), pl.ds(0, rows), :],
+                sems.at[number],
+            )
+        )
+        views.append((staging, number * count, count, 0))
     for copy in copies:
         copy.start()
     for copy, step, view in zip(copies, plan, views):
@@ -416,7 +413,9 @@
     mid_stream[...] = hidden_in[...].astype(jnp.float32) + rms_scale(out, gain_post)
 
 
-def forward_attn(plan, gain_len, tail_rows, devices, device, hidden_in, tables, given, arrays):
+def forward_attn(
+    plan, windows, gain_len, tail_rows, devices, device, hidden_in, tables, given, arrays
+):
     shapes = [
         jax.ShapeDtypeStruct((D, HQ + 2 * HD), jnp.bfloat16),
         jax.ShapeDtypeStruct((HQ, D), jnp.bfloat16),
@@ -425,9 +424,10 @@
         jax.ShapeDtypeStruct((CAP, D), jnp.float32),
     ]
     given = [] if gain_len else [given]
-    held = (sum(array.shape[0] for array in arrays),) + arrays[0].shape[1:]
+    most = max(rows for _, rows in windows)
+    held = (sum(array.shape[0] for array in arrays), most, LANES)
     return pl.pallas_call(
-        functools.partial(attn_forward_kernel, plan, gain_len),
+        functools.partial(attn_forward_kernel, plan, windows, gain_len),
         out_shape=shapes,
         in_specs=[pl.BlockSpec(memory_space=pltpu.SMEM)]
         + whole_specs(2 + len(given))
@@ -465,12 +465,12 @@
     gates, ups, hidden, delta_gate, delta_up, sems = refs[-6:]
     device = device_ref[0]
     copies, views = [], []
-    for source, (target, first_index, first_row) in zip(sources, staged):
-        count, rows = source.shape[:2]
+    for source, (target, first_index, first_row, low, rows) in zip(sources, staged):
+        count = source.shape[0]
         held = targets[target]
         copies.append(
             pltpu.make_async_copy(
-                source,
+                source.at[:, pl.ds(low, rows), :],
                 held.at[pl.ds(first_index, count), pl.ds(first_row, rows), :],
                 sems.at[len(copies)],
             )
@@ -683,27 +683,27 @@
     )(device, *inputs)
 
 
-def gathered_blocks(pieces, chunks, orders, each, devices, device):
-    arrays, plan, start = [], [], 0
-    for piece, blocks, order in zip(pieces, chunks, orders):
-        take = min(piece.shape[0], each - start)
+def gathered_blocks(chunks, cuts, orders, each, devices, device):
+    arrays, windows, plan, start = [], [], [], 0
+    for blocks, (low, high), order in zip(chunks, cuts, orders):
+        take = min(high - low, each - start)
         if each % ROWS:
             places = [offset_of(place, list(order) + [0]) for place in range(devices)]
             back = sorted(range(devices), key=places.__getitem__)
             mixed = offset_bits(device[0], list(order) + [0])
-            arrays.append(
-                jnp.take(jnp.concatenate(blocks), jnp.array(back, jnp.int32) ^ mixed, axis=0)
-            )
+            table = jnp.take(jnp.concatenate(blocks), jnp.array(back, jnp.int32) ^ mixed, axis=0)
+            arrays.append(table[:, low:high])
             continue
         for part, block in enumerate(blocks):
             plan.append((order[:-1], offset_of(part, [order[-1], 0]), take, start, each))
+            windows.append((low, high - low))
             arrays.append(block)
         start += take
     if each % ROWS == 0:
-        return arrays, plan, None
+        return arrays, windows, plan, None
     table = jnp.concatenate(arrays, axis=1)
     flat = table[:, :each].reshape(1, devices * each, LANES)
-    return [flat], [([], 0, devices * each, 0, 0)], table[:, each:]
+    return [flat], [(0, devices * each)], [([], 0, devices * each, 0, 0)], table[:, each:]
 
 
 def offset_bits(device, order):
@@ -815,15 +815,23 @@
     ).reshape(-1, LANES)
     second_piece = rounded[attn_len : attn_len + ffn_len].reshape(-1, LANES)
     ffn_rows = ffn_len // LANES
-    second_pieces = [second_piece[low:high] for low, high in cut_rows(ffn_rows, 2)]
     orders = bit_orders(devices, ("abxy", "bxya", "byax"))
-    pieces = [first_piece, *second_pieces]
-    chunks = gather_chunks(pieces, orders, devices)
-    arrays, plan, tails = gathered_blocks(
-        pieces[:1], chunks[:1], orders[:1], attn_rows, devices, here
-    )
-    ffn_arrays, ffn_plan, unused = gathered_blocks(
-        pieces[1:], chunks[1:], orders[1:], ffn_rows, devices, here
+    ffn_parts = cut_rows(ffn_rows, 3)
+    attn_parts = cut_rows(attn_rows + tail_rows, 3)
+    pieces, attn_cuts = [], []
+    for chunk, (low, high) in enumerate(ffn_parts):
+        piece = second_piece[low:high]
+        if chunk < len(attn_parts):
+            attn_cuts.append((high - low, high - low + attn_parts[chunk][1] - attn_parts[chunk][0]))
+            piece = jnp.concatenate([piece, first_piece[slice(*attn_parts[chunk])]])
+        pieces.append(piece)
+    chunks = [gather_chunk(piece, order, devices) for piece, order in zip(pieces, orders)]
+    arrays, attn_windows, plan, tails = gathered_blocks(
+        chunks, attn_cuts, orders, attn_rows, devices, here
+    )
+    ffn_cuts = [(0, high - low) for low, high in ffn_parts]
+    ffn_arrays, ffn_windows, ffn_plan, unused = gathered_blocks(
+        chunks, ffn_cuts, orders, ffn_rows, devices, here
     )
     aligned = attn_rows % ROWS == 0
     tables = slot_setup(seq_lengths, seq_owner, device)
@@ -832,6 +840,7 @@
         given = tails.reshape(devices, -1)[:, :gain_len].astype(jnp.float32).reshape(1, -1)
     qkv_weight, out_weight, gains, attn_out, mid_stream = forward_attn(
         plan,
+        attn_windows,
         gain_len if aligned else 0,
         tail_rows,
         devices,
@@ -843,11 +852,11 @@
     )
     orders = bit_orders(devices, ("yxba", "ayxb", "xayb"))
     out_plan, block_shapes, ffn_parts = scatter_plan(ffn_rows, 0, orders, devices)
-    staged = [(0, 0, 0)]
+    staged = [(0, 0, 0, *ffn_windows[0])]
     if len(block_shapes) == 2:
         staged = [
-            (part // 2, part % 2 * (devices // 4), low)
-            for low, _ in cut_rows(ffn_rows, 2)
+            (part // 2, part % 2 * (devices // 4), low, 0, high - low)
+            for low, high in ffn_parts
             for part in range(4)
         ]
     block_out, delta_mid, delta_attn, late_gains, *found = run_ffn(

time: 180 us -> 171 us (0.950)
  waiting for transfers between devices: 104 us -> 92.9 us
  starting transfers between devices: 34.5 us -> 37.2 us
  local copies, waits for them, and re-layouts: 3.06 us -> 1.01 us
    ppermute x32, waiting for transfers between devices: 104 us -> 92.9 us  [across(): lax.ppermute(block, 'dp', [(i, i ^ 1 << bit) for i in range(devices)])]
    ppermute x32, starting transfers between devices: 34.5 us -> 37.2 us  [across(): lax.ppermute(block, 'dp', [(i, i ^ 1 << bit) for i in range(devices)])]
    unnamed x25, local copies, waits for them, and re-layouts: 2.16 us -> 0.1 us
  transfers between devices with their start and end apart: 32 -> 32, of which waited for: 21 -> 19; matrix products, arithmetic and copies ran while one was open for 2% -> 2% of each run, Pallas kernels for 6% -> 4%
where the time goes in v1:
time: 171 us
  waiting for transfers between devices  92.9 us (54%)
  starting transfers between devices  37.2 us (22%)
  Pallas kernels  32.9 us (19%)
  other arithmetic  5.75 us (3%)
    ppermute x32, waiting for transfers between devices, across(): lax.ppermute(block, 'dp', [(i, i ^ 1 << bit) for i in range(devices)])  92.9 us
    ppermute x32, starting transfers between devices, across(): lax.ppermute(block, 'dp', [(i, i ^ 1 << bit) for i in range(devices)])  37.2 us
    pallas_call x1, Pallas kernels, run_ffn(): pl.pallas_call(functools.partial(ffn_kernel, plan_in, staged, plan_out),...  20.3 us
    pallas_call x1, Pallas kernels, back_attn(): pl.pallas_call(functools.partial(attn_back_kernel, plan, gain_len), out_s...  6.04 us
    pallas_call x1, Pallas kernels, forward_attn(): pl.pallas_call(functools.partial(attn_forward_kernel, plan, windows, gain...  5 us
  transfers between devices with their start and end apart: 32, of which 19 were waited for; matrix products, arithmetic and copies ran while one was open for 2% of the time, Pallas kernels for 4%

profile of v1, /device:TPU:0, one launch (start us, length us, event | category | flops | bytes accessed | tf_op | source)
XLA Modules:
  0.0 170.8 jit_solution(15362225378700706962)
XLA Ops:
  1.8 3.1 %collective-permute-start = (bf16[1,464,128]{2,1,0:T(8,128)(2,1)S(1)}, bf16[1,464,128]{2,1,0:T(8,128)(2,1)S(1)}, u32[]{:S(2)}, u32[]{:S(2)}) collective-permute-start(bf16[1,464,128]{2,1,0:T(8,128)(2,1)S(1)} %maximum_bitcast_fusion), channel_id=1, source_target_pairs={{0,8},{1,9},{2,10},{3,11},{4,12},{5,13},{6,14},{7,15},{8,0},{9,1},... | collective-permute-start | bytes 356360 | tf_op jit(solution)/shard_map/ppermute | solution.py:112
  4.9 2.7 %collective-permute-start.6 = (bf16[1,464,128]{2,1,0:T(8,128)(2,1)S(1)}, bf16[1,464,128]{2,1,0:T(8,128)(2,1)S(1)}, u32[]{:S(2)}, u32[]{:S(2)}) collective-permute-start(bf16[1,464,128]{2,1,0:T(8,128)(2,1)S(1)} %maximum_bitcast_fusion.1), channel_id=1, source_target_pairs={{0,16},{1,17},{2,18},{3,19},{4,20},{5,21},{6,22},{7,23},{8,24},{9,... | collective-permute-start | bytes 356360 | tf_op jit(solution)/shard_map/ppermute | solution.py:112
  8.3 4.9 %collective-permute-done.6 = bf16[1,464,128]{2,1,0:T(8,128)(2,1)S(1)} collective-permute-done((bf16[1,464,128]{2,1,0:T(8,128)(2,1)S(1)}, bf16[1,464,128]{2,1,0:T(8,128)(2,1)S(1)}, u32[]{:S(2)}, u32[]{:S(2)}) %collective-permute-start.6) | collective-permute-done | bytes 118816 | tf_op jit(solution)/shard_map/ppermute | solution.py:112
  15.1 2.7 %collective-permute-start.1 = (bf16[2,464,128]{2,1,0:T(8,128)(2,1)S(1)}, bf16[2,464,128]{2,1,0:T(8,128)(2,1)S(1)}, u32[]{:S(2)}, u32[]{:S(2)}) collective-permute-start(bf16[2,464,128]{2,1,0:T(8,128)(2,1)S(1)} %pad_maximum_fusion.7), channel_id=1, source_target_pairs={{0,16},{1,17},{2,18},{3,19},{4,20},{5,21},{6,22},{7,23},{8,24},{9,... | collective-permute-start | bytes 712712 | tf_op jit(solution)/shard_map/ppermute | solution.py:112
  17.9 10.0 %collective-permute-done.12 = bf16[1,448,128]{2,1,0:T(8,128)(2,1)S(1)} collective-permute-done((bf16[1,448,128]{2,1,0:T(8,128)(2,1)S(1)}, bf16[1,448,128]{2,1,0:T(8,128)(2,1)S(1)}, u32[]{:S(2)}, u32[]{:S(2)}) %collective-permute-start.12) | collective-permute-done | bytes 114720 | tf_op jit(solution)/shard_map/ppermute | solution.py:112
  31.3 2.7 %collective-permute-done.13 = bf16[2,448,128]{2,1,0:T(8,128)(2,1)S(1)} collective-permute-done((bf16[2,448,128]{2,1,0:T(8,128)(2,1)S(1)}, bf16[2,448,128]{2,1,0:T(8,128)(2,1)S(1)}, u32[]{:S(2)}, u32[]{:S(2)}) %collective-permute-start.13) | collective-permute-done | bytes 229408 | tf_op jit(solution)/shard_map/ppermute | solution.py:112
  34.1 5.0 %collective-permute-done.8 = bf16[4,464,128]{2,1,0:T(8,128)(2,1)S(1)} collective-permute-done((bf16[4,464,128]{2,1,0:T(8,128)(2,1)S(1)}, bf16[4,464,128]{2,1,0:T(8,128)(2,1)S(1)}, u32[]{:S(2)}, u32[]{:S(2)}) %collective-permute-start.8) | collective-permute-done | bytes 475168 | tf_op jit(solution)/shard_map/ppermute | solution.py:112
  39.2 4.0 %collective-permute-start.9 = (bf16[8,464,128]{2,1,0:T(8,128)(2,1)S(1)}, bf16[8,464,128]{2,1,0:T(8,128)(2,1)}, u32[]{:S(2)}, u32[]{:S(2)}) collective-permute-start(bf16[8,464,128]{2,1,0:T(8,128)(2,1)S(1)} %pad_maximum_fusion.1.refs_4_), channel_id=1, source_target_pairs={{0,8},{1,9},{2,10},{3,11},{4,12},{5,13},{6,14},{7,15},{8,0},{9,1},... | collective-permute-start | bytes 2850824 | tf_op jit(solution)/shard_map/ppermute | solution.py:112
  47.8 15.8 %collective-permute-done.9.refs_5_ = bf16[8,464,128]{2,1,0:T(8,128)(2,1)} collective-permute-done((bf16[8,464,128]{2,1,0:T(8,128)(2,1)S(1)}, bf16[8,464,128]{2,1,0:T(8,128)(2,1)}, u32[]{:S(2)}, u32[]{:S(2)}) %collective-permute-start.9) | collective-permute-done | bytes 950304 | tf_op jit(solution)/shard_map/ppermute | solution.py:112
  65.2 2.7 %collective-permute-done.15.refs_9_ = bf16[8,448,128]{2,1,0:T(8,128)(2,1)} collective-permute-done((bf16[8,448,128]{2,1,0:T(8,128)(2,1)S(1)}, bf16[8,448,128]{2,1,0:T(8,128)(2,1)}, u32[]{:S(2)}, u32[]{:S(2)}) %collective-permute-start.15) | collective-permute-done | bytes 917536 | tf_op jit(solution)/shard_map/ppermute | solution.py:112
  68.8 1.9 %collective-permute-done.17.refs_11_ = bf16[8,448,128]{2,1,0:T(8,128)(2,1)S(1)} collective-permute-done((bf16[8,448,128]{2,1,0:T(8,128)(2,1)}, bf16[8,448,128]{2,1,0:T(8,128)(2,1)S(1)}, u32[]{:S(2)}, u32[]{:S(2)}) %collective-permute-start.17) | collective-permute-done | bytes 917536 | tf_op jit(solution)/shard_map/ppermute | solution.py:112
  70.7 5.0 %shard_map.118 = (bf16[640,1536]{1,0:T(8,128)(2,1)S(1)}, bf16[1024,640]{1,0:T(8,128)(2,1)S(1)}, f32[1,3072]{1,0:T(1,128)S(1)}, f32[128,640]{1,0:T(8,128)S(1)}, f32[128,640]{1,0:T(8,128)S(1)}) custom-call(s32[1]{0:T(128)} %bitcast.device_ref, bf16[128,640]{1,0:T(8,128)(2,1)S(1)} %copy-done.3, f32[128,512]{1,0:T(8,128)S(1)} %pad_maximum_fusion.6.tables, ...), custom_call_target="tpu_custom_call" | custom-call | bytes 67108864 | tf_op jit(solution)/shard_map/pallas_call | solution.py:429
  75.7 20.3 %shard_map.119 = (bf16[128,640]{1,0:T(8,128)(2,1)}, f32[128,640]{1,0:T(8,128)S(1)}, bf16[128,640]{1,0:T(8,128)(2,1)S(1)}, f32[3,640]{1,0:T(4,128)S(1)}, bf16[16,...) custom-call(s32[1]{0:T(128)} %bitcast.device_ref, f32[128,640]{1,0:T(8,128)S(1)} %get-tuple-element.26.mid_ref, ...), custom_call_target="tpu_custom_call" | custom-call | tf_op jit(solution)/shard_map/pallas_call | solution.py:549
  96.2 6.0 %shard_map.120 = (f32[128,640]{1,0:T(8,128)}, f32[1,3072]{1,0:T(1,128)}, bf16[16,416,128]{2,1,0:T(8,128)(2,1)S(1)}, bf16[16,416,128]{2,1,0:T(8,128)(2,1)S(1)}) custom-call(s32[1]{0:T(128)} %bitcast.device_ref, bf16[128,640]{1,0:T(8,128)(2,1)S(1)} %get-tuple-element.30.delta_attn, f32[128,640]{1,0:T(8,128)S(1)} %get-tuple-element.31.delta_mid, ...), custom_call_target="tpu_custom_call" | custom-call | tf_op jit(solution)/shard_map/pallas_call | solution.py:670
  102.6 3.2 %collective-permute-done.19.refs_3_ = bf16[16,416,128]{2,1,0:T(8,128)(2,1)S(1)} collective-permute-done((bf16[16,416,128]{2,1,0:T(8,128)(2,1)S(1)}, bf16[16,416,128]{2,1,0:T(8,128)(2,1)S(1)}, u32[]{:S(2)}, u32[]{:S(2)}) %collective-permute-start.19) | collective-permute-done | bytes 1703968 | tf_op jit(solution)/shard_map/ppermute | solution.py:112
  109.6 20.5 %collective-permute-done.28 = bf16[8,448,128]{2,1,0:T(8,128)(2,1)S(1)} collective-permute-done((bf16[8,448,128]{2,1,0:T(8,128)(2,1)S(1)}, bf16[8,448,128]{2,1,0:T(8,128)(2,1)S(1)}, u32[]{:S(2)}, u32[]{:S(2)}) %collective-permute-start.28) | collective-permute-done | bytes 917536 | tf_op jit(solution)/shard_map/ppermute | solution.py:112
  133.7 8.7 %collective-permute-done.29 = bf16[4,448,128]{2,1,0:T(8,128)(2,1)S(1)} collective-permute-done((bf16[4,448,128]{2,1,0:T(8,128)(2,1)S(1)}, bf16[4,448,128]{2,1,0:T(8,128)(2,1)S(1)}, u32[]{:S(2)}, u32[]{:S(2)}) %collective-permute-start.29) | collective-permute-done | bytes 458784 | tf_op jit(solution)/shard_map/ppermute | solution.py:112
  143.5 3.4 %collective-permute-start.22 = (bf16[2,464,128]{2,1,0:T(8,128)(2,1)S(1)}, bf16[2,464,128]{2,1,0:T(8,128)(2,1)S(1)}, u32[]{:S(2)}, u32[]{:S(2)}) collective-permute-start(bf16[2,464,128]{2,1,0:T(8,128)(2,1)S(1)} %get-tuple-element.60), channel_id=1, source_target_pairs={{0,16},{1,17},{2,18},{3,19},{4,20},{5,21},{6,22},{7,23},{8,24},{9,... | collective-permute-start | bytes 712712 | tf_op jit(solution)/shard_map/ppermute | solution.py:112
  149.9 3.4 %collective-permute-start.31 = (bf16[1,448,128]{2,1,0:T(8,128)(2,1)S(1)}, bf16[1,448,128]{2,1,0:T(8,128)(2,1)S(1)}, u32[]{:S(2)}, u32[]{:S(2)}) collective-permute-start(bf16[1,448,128]{2,1,0:T(8,128)(2,1)S(1)} %add_convert_fusion.16), channel_id=1, source_target_pairs={{0,16},{1,17},{2,18},{3,19},{4,20},{5,21},{6,22},{7,23},{8,24},{9,... | collective-permute-start | bytes 344072 | tf_op jit(solution)/shard_map/ppermute | solution.py:112
  153.3 6.5 %collective-permute-done.22 = bf16[2,464,128]{2,1,0:T(8,128)(2,1)S(1)} collective-permute-done((bf16[2,464,128]{2,1,0:T(8,128)(2,1)S(1)}, bf16[2,464,128]{2,1,0:T(8,128)(2,1)S(1)}, u32[]{:S(2)}, u32[]{:S(2)}) %collective-permute-start.22) | collective-permute-done | bytes 237600 | tf_op jit(solution)/shard_map/ppermute | solution.py:112
  160.0 3.1 %collective-permute-start.27 = (bf16[1,464,128]{2,1,0:T(8,128)(2,1)S(1)}, bf16[1,464,128]{2,1,0:T(8,128)(2,1)S(1)}, u32[]{:S(2)}, u32[]{:S(2)}) collective-permute-start(bf16[1,464,128]{2,1,0:T(8,128)(2,1)S(1)} %add_convert_fusion.12), channel_id=1, source_target_pairs={{0,16},{1,17},{2,18},{3,19},{4,20},{5,21},{6,22},{7,23},{8,24},{9,... | collective-permute-start | bytes 356360 | tf_op jit(solution)/shard_map/ppermute | solution.py:112
  163.2 3.7 %collective-permute-done.23 = bf16[1,464,128]{2,1,0:T(8,128)(2,1)S(1)} collective-permute-done((bf16[1,464,128]{2,1,0:T(8,128)(2,1)S(1)}, bf16[1,464,128]{2,1,0:T(8,128)(2,1)S(1)}, u32[]{:S(2)}, u32[]{:S(2)}) %collective-permute-start.23) | collective-permute-done | bytes 118816 | tf_op jit(solution)/shard_map/ppermute | solution.py:112
  167.0 1.8 %collective-permute-done.27 = bf16[1,464,128]{2,1,0:T(8,128)(2,1)S(1)} collective-permute-done((bf16[1,464,128]{2,1,0:T(8,128)(2,1)S(1)}, bf16[1,464,128]{2,1,0:T(8,128)(2,1)S(1)}, u32[]{:S(2)}, u32[]{:S(2)}) %collective-permute-start.27) | collective-permute-done | bytes 118816 | tf_op jit(solution)/shard_map/ppermute | solution.py:112
  169.0 1.8 %multiply_subtract_fusion = (f32[174176]{0:T(1024)}, f32[174176]{0:T(1024)}, f32[174176]{0:T(1024)}) fusion(f32[174176]{0:T(1024)S(1)} %copy-done.5, f32[174176]{0:T(1024)S(1)} %constant_dynamic-update-slice_fusion, f32[174176]{0:T(1024)S(1)} %copy-done.7, f32[174176]{0:T(1024)S(1)} %copy-done.8), kind=kLoop, calls=%fused_computation.11 | loop fusion | flops 2612640 | bytes 4876928 | tf_op jit(solution)/shard_map/sub | solution.py:796
  (121 shorter events, 26.8 us)
Async XLA Ops:
  1.8 13.3 %collective-permute-start = (bf16[1,464,128]{2,1,0:T(8,128)(2,1)S(1)}, bf16[1,464,128]{2,1,0:T(8,128)(2,1)S(1)}, u32[]{:S(2)}, u32[]{:S(2)}) collective-permute-start(bf16[1,464,128]{2,1,0:T(8,128)(2,1)S(1)} %maximum_bitcast_fusion), channel_id=1, source_target_pairs={{0,8},{1,9},{2,10},{3,11},{4,12},{5,13},{6,14},{7,15},{8,0},{9,1},... | collective-permute-start | bytes 356360 | tf_op jit(solution)/shard_map/ppermute | solution.py:112
  4.9 8.3 %collective-permute-start.6 = (bf16[1,464,128]{2,1,0:T(8,128)(2,1)S(1)}, bf16[1,464,128]{2,1,0:T(8,128)(2,1)S(1)}, u32[]{:S(2)}, u32[]{:S(2)}) collective-permute-start(bf16[1,464,128]{2,1,0:T(8,128)(2,1)S(1)} %maximum_bitcast_fusion.1), channel_id=1, source_target_pairs={{0,16},{1,17},{2,18},{3,19},{4,20},{5,21},{6,22},{7,23},{8,24},{9,... | collective-permute-start | bytes 356360 | tf_op jit(solution)/shard_map/ppermute | solution.py:112
  13.2 16.2 %collective-permute-start.7 = (bf16[2,464,128]{2,1,0:T(8,128)(2,1)S(1)}, bf16[2,464,128]{2,1,0:T(8,128)(2,1)S(1)}, u32[]{:S(2)}, u32[]{:S(2)}) collective-permute-start(bf16[2,464,128]{2,1,0:T(8,128)(2,1)S(1)} %pad_maximum_fusion.8), channel_id=1, source_target_pairs={{0,2},{1,3},{2,0},{3,1},{4,6},{5,7},{6,4},{7,5},{8,10},{9,11},{10,... | collective-permute-start | bytes 712712 | tf_op jit(solution)/shard_map/ppermute | solution.py:112
  14.8 13.1 %collective-permute-start.12 = (bf16[1,448,128]{2,1,0:T(8,128)(2,1)S(1)}, bf16[1,448,128]{2,1,0:T(8,128)(2,1)S(1)}, u32[]{:S(2)}, u32[]{:S(2)}) collective-permute-start(bf16[1,448,128]{2,1,0:T(8,128)(2,1)S(1)} %maximum_bitcast_fusion.2), channel_id=1, source_target_pairs={{0,16},{1,17},{2,18},{3,19},{4,20},{5,21},{6,22},{7,23},{8,24},{9,... | collective-permute-start | bytes 344072 | tf_op jit(solution)/shard_map/ppermute | solution.py:112
  15.1 15.5 %collective-permute-start.1 = (bf16[2,464,128]{2,1,0:T(8,128)(2,1)S(1)}, bf16[2,464,128]{2,1,0:T(8,128)(2,1)S(1)}, u32[]{:S(2)}, u32[]{:S(2)}) collective-permute-start(bf16[2,464,128]{2,1,0:T(8,128)(2,1)S(1)} %pad_maximum_fusion.7), channel_id=1, source_target_pairs={{0,16},{1,17},{2,18},{3,19},{4,20},{5,21},{6,22},{7,23},{8,24},{9,... | collective-permute-start | bytes 712712 | tf_op jit(solution)/shard_map/ppermute | solution.py:112
  29.5 9.5 %collective-permute-start.8 = (bf16[4,464,128]{2,1,0:T(8,128)(2,1)S(1)}, bf16[4,464,128]{2,1,0:T(8,128)(2,1)S(1)}, u32[]{:S(2)}, u32[]{:S(2)}) collective-permute-start(bf16[4,464,128]{2,1,0:T(8,128)(2,1)S(1)} %pad_maximum_fusion.4), channel_id=1, source_target_pairs={{0,4},{1,5},{2,6},{3,7},{4,0},{5,1},{6,2},{7,3},{8,12},{9,13},{10,... | collective-permute-start | bytes 1425416 | tf_op jit(solution)/shard_map/ppermute | solution.py:112
  30.7 12.6 %collective-permute-start.2 = (bf16[4,464,128]{2,1,0:T(8,128)(2,1)S(1)}, bf16[4,464,128]{2,1,0:T(8,128)(2,1)S(1)}, u32[]{:S(2)}, u32[]{:S(2)}) collective-permute-start(bf16[4,464,128]{2,1,0:T(8,128)(2,1)S(1)} %pad_maximum_fusion.3), channel_id=1, source_target_pairs={{0,2},{1,3},{2,0},{3,1},{4,6},{5,7},{6,4},{7,5},{8,10},{9,11},{10,... | collective-permute-start | bytes 1425416 | tf_op jit(solution)/shard_map/ppermute | solution.py:112
  34.0 10.9 %collective-permute-start.14 = (bf16[4,448,128]{2,1,0:T(8,128)(2,1)S(1)}, bf16[4,448,128]{2,1,0:T(8,128)(2,1)S(1)}, u32[]{:S(2)}, u32[]{:S(2)}) collective-permute-start(bf16[4,448,128]{2,1,0:T(8,128)(2,1)S(1)} %pad_maximum_fusion.5), channel_id=1, source_target_pairs={{0,8},{1,9},{2,10},{3,11},{4,12},{5,13},{6,14},{7,15},{8,0},{9,1},... | collective-permute-start | bytes 1376264 | tf_op jit(solution)/shard_map/ppermute | solution.py:112
  39.2 24.4 %collective-permute-start.9 = (bf16[8,464,128]{2,1,0:T(8,128)(2,1)S(1)}, bf16[8,464,128]{2,1,0:T(8,128)(2,1)}, u32[]{:S(2)}, u32[]{:S(2)}) collective-permute-start(bf16[8,464,128]{2,1,0:T(8,128)(2,1)S(1)} %pad_maximum_fusion.1.refs_4_), channel_id=1, source_target_pairs={{0,8},{1,9},{2,10},{3,11},{4,12},{5,13},{6,14},{7,15},{8,0},{9,1},... | collective-permute-start | bytes 2850824 | tf_op jit(solution)/shard_map/ppermute | solution.py:112
  43.3 21.9 %collective-permute-start.3 = (bf16[8,464,128]{2,1,0:T(8,128)(2,1)S(1)}, bf16[8,464,128]{2,1,0:T(8,128)(2,1)}, u32[]{:S(2)}, u32[]{:S(2)}) collective-permute-start(bf16[8,464,128]{2,1,0:T(8,128)(2,1)S(1)} %pad_maximum_fusion.refs_0_), channel_id=1, source_target_pairs={{0,4},{1,5},{2,6},{3,7},{4,0},{5,1},{6,2},{7,3},{8,12},{9,13},{10,... | collective-permute-start | bytes 2850824 | tf_op jit(solution)/shard_map/ppermute | solution.py:112
  45.1 22.9 %collective-permute-start.15 = (bf16[8,448,128]{2,1,0:T(8,128)(2,1)S(1)}, bf16[8,448,128]{2,1,0:T(8,128)(2,1)}, u32[]{:S(2)}, u32[]{:S(2)}) collective-permute-start(bf16[8,448,128]{2,1,0:T(8,128)(2,1)S(1)} %pad_maximum_fusion.2.refs_8_), channel_id=1, source_target_pairs={{0,2},{1,3},{2,0},{3,1},{4,6},{5,7},{6,4},{7,5},{8,10},{9,11},{10,... | collective-permute-start | bytes 2752520 | tf_op jit(solution)/shard_map/ppermute | solution.py:112
  46.0 22.7 %collective-permute-start.10 = (bf16[8,464,128]{2,1,0:T(8,128)(2,1)S(1)}, bf16[8,464,128]{2,1,0:T(8,128)(2,1)S(1)}, u32[]{:S(2)}, u32[]{:S(2)}) collective-permute-start(bf16[8,464,128]{2,1,0:T(8,128)(2,1)S(1)} %pad_maximum_fusion.1.refs_4_), channel_id=1, source_target_pairs={{0,1},{1,0},{2,3},{3,2},{4,5},{5,4},{6,7},{7,6},{8,9},{9,8},{10,11... | collective-permute-start | bytes 2850824 | tf_op jit(solution)/shard_map/ppermute | solution.py:112
  47.7 21.1 %collective-permute-start.4 = (bf16[8,464,128]{2,1,0:T(8,128)(2,1)S(1)}, bf16[8,464,128]{2,1,0:T(8,128)(2,1)S(1)}, u32[]{:S(2)}, u32[]{:S(2)}) collective-permute-start(bf16[8,464,128]{2,1,0:T(8,128)(2,1)S(1)} %pad_maximum_fusion.refs_0_), channel_id=1, source_target_pairs={{0,1},{1,0},{2,3},{3,2},{4,5},{5,4},{6,7},{7,6},{8,9},{9,8},{10,11... | collective-permute-start | bytes 2850824 | tf_op jit(solution)/shard_map/ppermute | solution.py:112
  96.0 9.8 %collective-permute-start.18 = (bf16[16,960,128]{2,1,0:T(8,128)(2,1)}, bf16[16,960,128]{2,1,0:T(8,128)(2,1)S(1)}, u32[]{:S(2)}, u32[]{:S(2)}) collective-permute-start(bf16[16,960,128]{2,1,0:T(8,128)(2,1)} %get-tuple-element.37), channel_id=1, source_target_pairs={{0,1},{1,0},{2,3},{3,2},{4,5},{5,4},{6,7},{7,6},{8,9},{9,8},{10,11... | collective-permute-start | bytes 11796488 | tf_op jit(solution)/shard_map/ppermute | solution.py:112
  107.4 22.7 %collective-permute-start.28 = (bf16[8,448,128]{2,1,0:T(8,128)(2,1)S(1)}, bf16[8,448,128]{2,1,0:T(8,128)(2,1)S(1)}, u32[]{:S(2)}, u32[]{:S(2)}) collective-permute-start(bf16[8,448,128]{2,1,0:T(8,128)(2,1)S(1)} %get-tuple-element.45), channel_id=1, source_target_pairs={{0,2},{1,3},{2,0},{3,1},{4,6},{5,7},{6,4},{7,5},{8,10},{9,11},{10,... | collective-permute-start | bytes 2752520 | tf_op jit(solution)/shard_map/ppermute | solution.py:112
  108.0 23.0 %collective-permute-start.20 = (bf16[8,464,128]{2,1,0:T(8,128)(2,1)S(1)}, bf16[8,464,128]{2,1,0:T(8,128)(2,1)S(1)}, u32[]{:S(2)}, u32[]{:S(2)}) collective-permute-start(bf16[8,464,128]{2,1,0:T(8,128)(2,1)S(1)} %get-tuple-element.41), channel_id=1, source_target_pairs={{0,4},{1,5},{2,6},{3,7},{4,0},{5,1},{6,2},{7,3},{8,12},{9,13},{10,... | collective-permute-start | bytes 2850824 | tf_op jit(solution)/shard_map/ppermute | solution.py:112
  108.5 24.3 %collective-permute-start.24 = (bf16[8,464,128]{2,1,0:T(8,128)(2,1)S(1)}, bf16[8,464,128]{2,1,0:T(8,128)(2,1)S(1)}, u32[]{:S(2)}, u32[]{:S(2)}) collective-permute-start(bf16[8,464,128]{2,1,0:T(8,128)(2,1)S(1)} %get-tuple-element.43), channel_id=1, source_target_pairs={{0,8},{1,9},{2,10},{3,11},{4,12},{5,13},{6,14},{7,15},{8,0},{9,1},... | collective-permute-start | bytes 2850824 | tf_op jit(solution)/shard_map/ppermute | solution.py:112
  130.3 12.0 %collective-permute-start.29 = (bf16[4,448,128]{2,1,0:T(8,128)(2,1)S(1)}, bf16[4,448,128]{2,1,0:T(8,128)(2,1)S(1)}, u32[]{:S(2)}, u32[]{:S(2)}) collective-permute-start(bf16[4,448,128]{2,1,0:T(8,128)(2,1)S(1)} %get-tuple-element.58), channel_id=1, source_target_pairs={{0,8},{1,9},{2,10},{3,11},{4,12},{5,13},{6,14},{7,15},{8,0},{9,1},... | collective-permute-start | bytes 1376264 | tf_op jit(solution)/shard_map/ppermute | solution.py:112
  131.3 12.1 %collective-permute-start.21 = (bf16[4,464,128]{2,1,0:T(8,128)(2,1)S(1)}, bf16[4,464,128]{2,1,0:T(8,128)(2,1)S(1)}, u32[]{:S(2)}, u32[]{:S(2)}) collective-permute-start(bf16[4,464,128]{2,1,0:T(8,128)(2,1)S(1)} %get-tuple-element.54), channel_id=1, source_target_pairs={{0,2},{1,3},{2,0},{3,1},{4,6},{5,7},{6,4},{7,5},{8,10},{9,11},{10,... | collective-permute-start | bytes 1425416 | tf_op jit(solution)/shard_map/ppermute | solution.py:112
  133.1 13.8 %collective-permute-start.25 = (bf16[4,464,128]{2,1,0:T(8,128)(2,1)S(1)}, bf16[4,464,128]{2,1,0:T(8,128)(2,1)S(1)}, u32[]{:S(2)}, u32[]{:S(2)}) collective-permute-start(bf16[4,464,128]{2,1,0:T(8,128)(2,1)S(1)} %get-tuple-element.56), channel_id=1, source_target_pairs={{0,4},{1,5},{2,6},{3,7},{4,0},{5,1},{6,2},{7,3},{8,12},{9,13},{10,... | collective-permute-start | bytes 1425416 | tf_op jit(solution)/shard_map/ppermute | solution.py:112
  143.5 16.3 %collective-permute-start.22 = (bf16[2,464,128]{2,1,0:T(8,128)(2,1)S(1)}, bf16[2,464,128]{2,1,0:T(8,128)(2,1)S(1)}, u32[]{:S(2)}, u32[]{:S(2)}) collective-permute-start(bf16[2,464,128]{2,1,0:T(8,128)(2,1)S(1)} %get-tuple-element.60), channel_id=1, source_target_pairs={{0,16},{1,17},{2,18},{3,19},{4,20},{5,21},{6,22},{7,23},{8,24},{9,... | collective-permute-start | bytes 712712 | tf_op jit(solution)/shard_map/ppermute | solution.py:112
  147.1 12.9 %collective-permute-start.26 = (bf16[2,464,128]{2,1,0:T(8,128)(2,1)S(1)}, bf16[2,464,128]{2,1,0:T(8,128)(2,1)S(1)}, u32[]{:S(2)}, u32[]{:S(2)}) collective-permute-start(bf16[2,464,128]{2,1,0:T(8,128)(2,1)S(1)} %get-tuple-element.62), channel_id=1, source_target_pairs={{0,2},{1,3},{2,0},{3,1},{4,6},{5,7},{6,4},{7,5},{8,10},{9,11},{10,... | collective-permute-start | bytes 712712 | tf_op jit(solution)/shard_map/ppermute | solution.py:112
  149.9 13.3 %collective-permute-start.31 = (bf16[1,448,128]{2,1,0:T(8,128)(2,1)S(1)}, bf16[1,448,128]{2,1,0:T(8,128)(2,1)S(1)}, u32[]{:S(2)}, u32[]{:S(2)}) collective-permute-start(bf16[1,448,128]{2,1,0:T(8,128)(2,1)S(1)} %add_convert_fusion.16), channel_id=1, source_target_pairs={{0,16},{1,17},{2,18},{3,19},{4,20},{5,21},{6,22},{7,23},{8,24},{9,... | collective-permute-start | bytes 344072 | tf_op jit(solution)/shard_map/ppermute | solution.py:112
  160.0 8.8 %collective-permute-start.27 = (bf16[1,464,128]{2,1,0:T(8,128)(2,1)S(1)}, bf16[1,464,128]{2,1,0:T(8,128)(2,1)S(1)}, u32[]{:S(2)}, u32[]{:S(2)}) collective-permute-start(bf16[1,464,128]{2,1,0:T(8,128)(2,1)S(1)} %add_convert_fusion.12), channel_id=1, source_target_pairs={{0,16},{1,17},{2,18},{3,19},{4,20},{5,21},{6,22},{7,23},{8,24},{9,... | collective-permute-start | bytes 356360 | tf_op jit(solution)/shard_map/ppermute | solution.py:112
  (19 other events, 142.0 us)

commit v2 on v0

--- a/solution.py
+++ b/solution.py
@@ -127,10 +127,8 @@
     chunks = []
     for block, final in zip(held, last):
         if chunks:
-            final = lax.optimization_barrier((final, chunks[0][-1]))[0]
-        beside = across(block, 0, devices)
-        final = lax.optimization_barrier((final, beside))[0]
-        chunks.append((block, final, beside, across(final, 0, devices)))
+            final = lax.optimization_barrier((final, *chunks[0][2:]))[0]
+        chunks.append((block, final, across(block, 0, devices), across(final, 0, devices)))
     return chunks
 
 

time: 180 us -> 164 us (0.911)
  waiting for transfers between devices: 104 us -> 85.9 us
  starting transfers between devices: 34.5 us -> 38.7 us
  local copies, waits for them, and re-layouts: 3.06 us -> 0.99 us
    ppermute x32, waiting for transfers between devices: 104 us -> 85.9 us  [across(): lax.ppermute(block, 'dp', [(i, i ^ 1 << bit) for i in range(devices)])]
    ppermute x32, starting transfers between devices: 34.5 us -> 38.7 us  [across(): lax.ppermute(block, 'dp', [(i, i ^ 1 << bit) for i in range(devices)])]
    unnamed x25 -> x21, local copies, waits for them, and re-layouts: 2.16 us -> 0.1 us
  transfers between devices with their start and end apart: 32 -> 32, of which waited for: 21 -> 20; matrix products, arithmetic and copies ran while one was open for 2% -> 2% of each run, Pallas kernels for 6% -> 7%
where the time goes in v2:
time: 164 us
  waiting for transfers between devices  85.9 us (52%)
  starting transfers between devices  38.7 us (24%)
  Pallas kernels  31.6 us (19%)
  other arithmetic  5.66 us (3%)
    ppermute x32, waiting for transfers between devices, across(): lax.ppermute(block, 'dp', [(i, i ^ 1 << bit) for i in range(devices)])  85.9 us
    ppermute x32, starting transfers between devices, across(): lax.ppermute(block, 'dp', [(i, i ^ 1 << bit) for i in range(devices)])  38.7 us
    pallas_call x1, Pallas kernels, run_ffn(): pl.pallas_call(functools.partial(ffn_kernel, plan_in, staged, plan_out),...  19.4 us
    pallas_call x1, Pallas kernels, back_attn(): pl.pallas_call(functools.partial(attn_back_kernel, plan, gain_len), out_s...  6.12 us
    pallas_call x1, Pallas kernels, forward_attn(): pl.pallas_call(functools.partial(attn_forward_kernel, plan, gain_len), ou...  4.61 us
  transfers between devices with their start and end apart: 32, of which 20 were waited for; matrix products, arithmetic and copies ran while one was open for 2% of the time, Pallas kernels for 7%

profile of v2, /device:TPU:0, one launch (start us, length us, event | category | flops | bytes accessed | tf_op | source)
XLA Modules:
  0.0 163.9 jit_solution(17575375906173219669)
XLA Ops:
  2.5 3.0 %collective-permute-start = (bf16[1,416,128]{2,1,0:T(8,128)(2,1)S(1)}, bf16[1,416,128]{2,1,0:T(8,128)(2,1)S(1)}, u32[]{:S(2)}, u32[]{:S(2)}) collective-permute-start(bf16[1,416,128]{2,1,0:T(8,128)(2,1)S(1)} %bitcast.26), channel_id=1, source_target_pairs={{0,8},{1,9},{2,10},{3,11},{4,12},{5,13},{6,14},{7,15},{8,0},{9,1},... | collective-permute-start | bytes 319496 | tf_op jit(solution)/shard_map/ppermute | solution.py:112
  5.5 2.7 %collective-permute-start.12 = (bf16[1,480,128]{2,1,0:T(8,128)(2,1)S(1)}, bf16[1,480,128]{2,1,0:T(8,128)(2,1)S(1)}, u32[]{:S(2)}, u32[]{:S(2)}) collective-permute-start(bf16[1,480,128]{2,1,0:T(8,128)(2,1)S(1)} %get-tuple-element.81), channel_id=1, source_target_pairs={{0,16},{1,17},{2,18},{3,19},{4,20},{5,21},{6,22},{7,23},{8,24},{9,... | collective-permute-start | bytes 368648 | tf_op jit(solution)/shard_map/ppermute | solution.py:112
  8.5 3.9 %collective-permute-start.1 = (bf16[2,416,128]{2,1,0:T(8,128)(2,1)S(1)}, bf16[2,416,128]{2,1,0:T(8,128)(2,1)S(1)}, u32[]{:S(2)}, u32[]{:S(2)}) collective-permute-start(bf16[2,416,128]{2,1,0:T(8,128)(2,1)S(1)} %pad_maximum_fusion.9), channel_id=1, source_target_pairs={{0,16},{1,17},{2,18},{3,19},{4,20},{5,21},{6,22},{7,23},{8,24},{9,... | collective-permute-start | bytes 638984 | tf_op jit(solution)/shard_map/ppermute | solution.py:112
  12.5 9.7 %collective-permute-done.12 = bf16[1,480,128]{2,1,0:T(8,128)(2,1)S(1)} collective-permute-done((bf16[1,480,128]{2,1,0:T(8,128)(2,1)S(1)}, bf16[1,480,128]{2,1,0:T(8,128)(2,1)S(1)}, u32[]{:S(2)}, u32[]{:S(2)}) %collective-permute-start.12) | collective-permute-done | bytes 122912 | tf_op jit(solution)/shard_map/ppermute | solution.py:112
  22.1 2.6 %collective-permute-done.6 = bf16[1,480,128]{2,1,0:T(8,128)(2,1)S(1)} collective-permute-done((bf16[1,480,128]{2,1,0:T(8,128)(2,1)S(1)}, bf16[1,480,128]{2,1,0:T(8,128)(2,1)S(1)}, u32[]{:S(2)}, u32[]{:S(2)}) %collective-permute-start.6) | collective-permute-done | bytes 122912 | tf_op jit(solution)/shard_map/ppermute | solution.py:112
  31.1 4.2 %collective-permute-done.7 = bf16[2,480,128]{2,1,0:T(8,128)(2,1)S(1)} collective-permute-done((bf16[2,480,128]{2,1,0:T(8,128)(2,1)S(1)}, bf16[2,480,128]{2,1,0:T(8,128)(2,1)S(1)}, u32[]{:S(2)}, u32[]{:S(2)}) %collective-permute-start.7) | collective-permute-done | bytes 245792 | tf_op jit(solution)/shard_map/ppermute | solution.py:112
  35.5 6.3 %collective-permute-done.2 = bf16[4,416,128]{2,1,0:T(8,128)(2,1)S(1)} collective-permute-done((bf16[4,416,128]{2,1,0:T(8,128)(2,1)S(1)}, bf16[4,416,128]{2,1,0:T(8,128)(2,1)S(1)}, u32[]{:S(2)}, u32[]{:S(2)}) %collective-permute-start.2) | collective-permute-done | bytes 426016 | tf_op jit(solution)/shard_map/ppermute | solution.py:112
  42.5 2.3 %collective-permute-done.14 = bf16[4,480,128]{2,1,0:T(8,128)(2,1)S(1)} collective-permute-done((bf16[4,480,128]{2,1,0:T(8,128)(2,1)S(1)}, bf16[4,480,128]{2,1,0:T(8,128)(2,1)S(1)}, u32[]{:S(2)}, u32[]{:S(2)}) %collective-permute-start.14) | collective-permute-done | bytes 491552 | tf_op jit(solution)/shard_map/ppermute | solution.py:112
  46.6 4.7 %collective-permute-start.9 = (bf16[8,480,128]{2,1,0:T(8,128)(2,1)S(1)}, bf16[8,480,128]{2,1,0:T(8,128)(2,1)}, u32[]{:S(2)}, u32[]{:S(2)}) collective-permute-start(bf16[8,480,128]{2,1,0:T(8,128)(2,1)S(1)} %pad_maximum_fusion.refs_0_), channel_id=1, source_target_pairs={{0,8},{1,9},{2,10},{3,11},{4,12},{5,13},{6,14},{7,15},{8,0},{9,1},... | collective-permute-start | bytes 2949128 | tf_op jit(solution)/shard_map/ppermute | solution.py:112
  53.0 9.7 %collective-permute-done.3.refs_1_ = bf16[8,416,128]{2,1,0:T(8,128)(2,1)} collective-permute-done((bf16[8,416,128]{2,1,0:T(8,128)(2,1)S(1)}, bf16[8,416,128]{2,1,0:T(8,128)(2,1)}, u32[]{:S(2)}, u32[]{:S(2)}) %collective-permute-start.3) | collective-permute-done | bytes 852000 | tf_op jit(solution)/shard_map/ppermute | solution.py:112
  66.8 4.6 %shard_map.118 = (bf16[640,1536]{1,0:T(8,128)(2,1)S(1)}, bf16[1024,640]{1,0:T(8,128)(2,1)S(1)}, f32[1,3072]{1,0:T(1,128)S(1)}, f32[128,640]{1,0:T(8,128)S(1)}, f32[128,640]{1,0:T(8,128)S(1)}) custom-call(s32[1]{0:T(128)} %bitcast.device_ref, bf16[128,640]{1,0:T(8,128)(2,1)S(1)} %copy-done.1, f32[128,512]{1,0:T(8,128)S(1)} %pad_maximum_fusion.6.tables, ...), custom_call_target="tpu_custom_call" | custom-call | bytes 67108864 | tf_op jit(solution)/shard_map/pallas_call | solution.py:427
  71.4 19.4 %shard_map.119 = (bf16[128,640]{1,0:T(8,128)(2,1)}, f32[128,640]{1,0:T(8,128)S(1)}, bf16[128,640]{1,0:T(8,128)(2,1)S(1)}, f32[3,640]{1,0:T(4,128)S(1)}, bf16[16,...) custom-call(s32[1]{0:T(128)} %bitcast.device_ref, f32[128,640]{1,0:T(8,128)S(1)} %get-tuple-element.34.mid_ref, ...), custom_call_target="tpu_custom_call" | custom-call | tf_op jit(solution)/shard_map/pallas_call | solution.py:547
  91.1 6.1 %shard_map.120 = (f32[128,640]{1,0:T(8,128)}, f32[1,3072]{1,0:T(1,128)}, bf16[16,416,128]{2,1,0:T(8,128)(2,1)S(1)}, bf16[16,416,128]{2,1,0:T(8,128)(2,1)S(1)}) custom-call(s32[1]{0:T(128)} %bitcast.device_ref, bf16[128,640]{1,0:T(8,128)(2,1)S(1)} %get-tuple-element.46.delta_attn, f32[128,640]{1,0:T(8,128)S(1)} %get-tuple-element.47.delta_mid, ...), custom_call_target="tpu_custom_call" | custom-call | tf_op jit(solution)/shard_map/pallas_call | solution.py:668
  97.5 3.3 %collective-permute-done.19.refs_3_ = bf16[16,416,128]{2,1,0:T(8,128)(2,1)S(1)} collective-permute-done((bf16[16,416,128]{2,1,0:T(8,128)(2,1)S(1)}, bf16[16,416,128]{2,1,0:T(8,128)(2,1)S(1)}, u32[]{:S(2)}, u32[]{:S(2)}) %collective-permute-start.19) | collective-permute-done | bytes 1703968 | tf_op jit(solution)/shard_map/ppermute | solution.py:112
  104.0 1.9 %collective-permute-start.24 = (bf16[8,464,128]{2,1,0:T(8,128)(2,1)S(1)}, bf16[8,464,128]{2,1,0:T(8,128)(2,1)S(1)}, u32[]{:S(2)}, u32[]{:S(2)}) collective-permute-start(bf16[8,464,128]{2,1,0:T(8,128)(2,1)S(1)} %get-tuple-element.59), channel_id=1, source_target_pairs={{0,8},{1,9},{2,10},{3,11},{4,12},{5,13},{6,14},{7,15},{8,0},{9,1},... | collective-permute-start | bytes 2850824 | tf_op jit(solution)/shard_map/ppermute | solution.py:112
  105.8 19.1 %collective-permute-done.28 = bf16[8,448,128]{2,1,0:T(8,128)(2,1)S(1)} collective-permute-done((bf16[8,448,128]{2,1,0:T(8,128)(2,1)S(1)}, bf16[8,448,128]{2,1,0:T(8,128)(2,1)S(1)}, u32[]{:S(2)}, u32[]{:S(2)}) %collective-permute-start.28) | collective-permute-done | bytes 917536 | tf_op jit(solution)/shard_map/ppermute | solution.py:112
  125.2 2.1 %collective-permute-start.29 = (bf16[4,448,128]{2,1,0:T(8,128)(2,1)S(1)}, bf16[4,448,128]{2,1,0:T(8,128)(2,1)S(1)}, u32[]{:S(2)}, u32[]{:S(2)}) collective-permute-start(bf16[4,448,128]{2,1,0:T(8,128)(2,1)S(1)} %get-tuple-element.74), channel_id=1, source_target_pairs={{0,8},{1,9},{2,10},{3,11},{4,12},{5,13},{6,14},{7,15},{8,0},{9,1},... | collective-permute-start | bytes 1376264 | tf_op jit(solution)/shard_map/ppermute | solution.py:112
  130.2 7.3 %collective-permute-done.29 = bf16[4,448,128]{2,1,0:T(8,128)(2,1)S(1)} collective-permute-done((bf16[4,448,128]{2,1,0:T(8,128)(2,1)S(1)}, bf16[4,448,128]{2,1,0:T(8,128)(2,1)S(1)}, u32[]{:S(2)}, u32[]{:S(2)}) %collective-permute-start.29) | collective-permute-done | bytes 458784 | tf_op jit(solution)/shard_map/ppermute | solution.py:112
  139.8 2.2 %collective-permute-start.22 = (bf16[2,464,128]{2,1,0:T(8,128)(2,1)S(1)}, bf16[2,464,128]{2,1,0:T(8,128)(2,1)S(1)}, u32[]{:S(2)}, u32[]{:S(2)}) collective-permute-start(bf16[2,464,128]{2,1,0:T(8,128)(2,1)S(1)} %get-tuple-element.76), channel_id=1, source_target_pairs={{0,16},{1,17},{2,18},{3,19},{4,20},{5,21},{6,22},{7,23},{8,24},{9,... | collective-permute-start | bytes 712712 | tf_op jit(solution)/shard_map/ppermute | solution.py:112
  143.2 2.8 %collective-permute-done.30 = bf16[2,448,128]{2,1,0:T(8,128)(2,1)S(1)} collective-permute-done((bf16[2,448,128]{2,1,0:T(8,128)(2,1)S(1)}, bf16[2,448,128]{2,1,0:T(8,128)(2,1)S(1)}, u32[]{:S(2)}, u32[]{:S(2)}) %collective-permute-start.30) | collective-permute-done | bytes 229408 | tf_op jit(solution)/shard_map/ppermute | solution.py:112
  147.4 8.0 %collective-permute-done.22 = bf16[2,464,128]{2,1,0:T(8,128)(2,1)S(1)} collective-permute-done((bf16[2,464,128]{2,1,0:T(8,128)(2,1)S(1)}, bf16[2,464,128]{2,1,0:T(8,128)(2,1)S(1)}, u32[]{:S(2)}, u32[]{:S(2)}) %collective-permute-start.22) | collective-permute-done | bytes 237600 | tf_op jit(solution)/shard_map/ppermute | solution.py:112
  155.7 2.7 %collective-permute-start.27 = (bf16[1,464,128]{2,1,0:T(8,128)(2,1)S(1)}, bf16[1,464,128]{2,1,0:T(8,128)(2,1)S(1)}, u32[]{:S(2)}, u32[]{:S(2)}) collective-permute-start(bf16[1,464,128]{2,1,0:T(8,128)(2,1)S(1)} %add_convert_fusion.12), channel_id=1, source_target_pairs={{0,16},{1,17},{2,18},{3,19},{4,20},{5,21},{6,22},{7,23},{8,24},{9,... | collective-permute-start | bytes 356360 | tf_op jit(solution)/shard_map/ppermute | solution.py:112
  158.4 3.5 %collective-permute-done.23 = bf16[1,464,128]{2,1,0:T(8,128)(2,1)S(1)} collective-permute-done((bf16[1,464,128]{2,1,0:T(8,128)(2,1)S(1)}, bf16[1,464,128]{2,1,0:T(8,128)(2,1)S(1)}, u32[]{:S(2)}, u32[]{:S(2)}) %collective-permute-start.23) | collective-permute-done | bytes 118816 | tf_op jit(solution)/shard_map/ppermute | solution.py:112
  162.2 1.7 %multiply_subtract_fusion = (f32[174176]{0:T(1024)}, f32[174176]{0:T(1024)}, f32[174176]{0:T(1024)}) fusion(f32[174176]{0:T(1024)S(1)} %copy-done.3, f32[174176]{0:T(1024)S(1)} %constant_dynamic-update-slice_fusion, f32[174176]{0:T(1024)S(1)} %copy-done.5, f32[174176]{0:T(1024)S(1)} %copy-done.6), kind=kLoop, calls=%fused_computation.11 | loop fusion | flops 2612640 | bytes 4876928 | tf_op jit(solution)/shard_map/sub | solution.py:794
  (112 shorter events, 29.0 us)
Async XLA Ops:
  5.5 16.6 %collective-permute-start.12 = (bf16[1,480,128]{2,1,0:T(8,128)(2,1)S(1)}, bf16[1,480,128]{2,1,0:T(8,128)(2,1)S(1)}, u32[]{:S(2)}, u32[]{:S(2)}) collective-permute-start(bf16[1,480,128]{2,1,0:T(8,128)(2,1)S(1)} %get-tuple-element.81), channel_id=1, source_target_pairs={{0,16},{1,17},{2,18},{3,19},{4,20},{5,21},{6,22},{7,23},{8,24},{9,... | collective-permute-start | bytes 368648 | tf_op jit(solution)/shard_map/ppermute | solution.py:112
  8.2 16.6 %collective-permute-start.6 = (bf16[1,480,128]{2,1,0:T(8,128)(2,1)S(1)}, bf16[1,480,128]{2,1,0:T(8,128)(2,1)S(1)}, u32[]{:S(2)}, u32[]{:S(2)}) collective-permute-start(bf16[1,480,128]{2,1,0:T(8,128)(2,1)S(1)} %get-tuple-element.82), channel_id=1, source_target_pairs={{0,16},{1,17},{2,18},{3,19},{4,20},{5,21},{6,22},{7,23},{8,24},{9,... | collective-permute-start | bytes 368648 | tf_op jit(solution)/shard_map/ppermute | solution.py:112
  8.5 19.8 %collective-permute-start.1 = (bf16[2,416,128]{2,1,0:T(8,128)(2,1)S(1)}, bf16[2,416,128]{2,1,0:T(8,128)(2,1)S(1)}, u32[]{:S(2)}, u32[]{:S(2)}) collective-permute-start(bf16[2,416,128]{2,1,0:T(8,128)(2,1)S(1)} %pad_maximum_fusion.9), channel_id=1, source_target_pairs={{0,16},{1,17},{2,18},{3,19},{4,20},{5,21},{6,22},{7,23},{8,24},{9,... | collective-permute-start | bytes 638984 | tf_op jit(solution)/shard_map/ppermute | solution.py:112
  26.4 8.9 %collective-permute-start.7 = (bf16[2,480,128]{2,1,0:T(8,128)(2,1)S(1)}, bf16[2,480,128]{2,1,0:T(8,128)(2,1)S(1)}, u32[]{:S(2)}, u32[]{:S(2)}) collective-permute-start(bf16[2,480,128]{2,1,0:T(8,128)(2,1)S(1)} %pad_maximum_fusion.7), channel_id=1, source_target_pairs={{0,2},{1,3},{2,0},{3,1},{4,6},{5,7},{6,4},{7,5},{8,10},{9,11},{10,... | collective-permute-start | bytes 737288 | tf_op jit(solution)/shard_map/ppermute | solution.py:112
  28.3 13.5 %collective-permute-start.2 = (bf16[4,416,128]{2,1,0:T(8,128)(2,1)S(1)}, bf16[4,416,128]{2,1,0:T(8,128)(2,1)S(1)}, u32[]{:S(2)}, u32[]{:S(2)}) collective-permute-start(bf16[4,416,128]{2,1,0:T(8,128)(2,1)S(1)} %pad_maximum_fusion.5), channel_id=1, source_target_pairs={{0,2},{1,3},{2,0},{3,1},{4,6},{5,7},{6,4},{7,5},{8,10},{9,11},{10,... | collective-permute-start | bytes 1277960 | tf_op jit(solution)/shard_map/ppermute | solution.py:112
  35.3 9.5 %collective-permute-start.14 = (bf16[4,480,128]{2,1,0:T(8,128)(2,1)S(1)}, bf16[4,480,128]{2,1,0:T(8,128)(2,1)S(1)}, u32[]{:S(2)}, u32[]{:S(2)}) collective-permute-start(bf16[4,480,128]{2,1,0:T(8,128)(2,1)S(1)} %pad_maximum_fusion.4), channel_id=1, source_target_pairs={{0,8},{1,9},{2,10},{3,11},{4,12},{5,13},{6,14},{7,15},{8,0},{9,1},... | collective-permute-start | bytes 1474568 | tf_op jit(solution)/shard_map/ppermute | solution.py:112
  35.5 11.1 %collective-permute-start.8 = (bf16[4,480,128]{2,1,0:T(8,128)(2,1)S(1)}, bf16[4,480,128]{2,1,0:T(8,128)(2,1)S(1)}, u32[]{:S(2)}, u32[]{:S(2)}) collective-permute-start(bf16[4,480,128]{2,1,0:T(8,128)(2,1)S(1)} %pad_maximum_fusion.3), channel_id=1, source_target_pairs={{0,4},{1,5},{2,6},{3,7},{4,0},{5,1},{6,2},{7,3},{8,12},{9,13},{10,... | collective-permute-start | bytes 1474568 | tf_op jit(solution)/shard_map/ppermute | solution.py:112
  41.9 20.8 %collective-permute-start.3 = (bf16[8,416,128]{2,1,0:T(8,128)(2,1)S(1)}, bf16[8,416,128]{2,1,0:T(8,128)(2,1)}, u32[]{:S(2)}, u32[]{:S(2)}) collective-permute-start(bf16[8,416,128]{2,1,0:T(8,128)(2,1)S(1)} %pad_maximum_fusion.2.refs_0_), channel_id=1, source_target_pairs={{0,4},{1,5},{2,6},{3,7},{4,0},{5,1},{6,2},{7,3},{8,12},{9,13},{10,... | collective-permute-start | bytes 2555912 | tf_op jit(solution)/shard_map/ppermute | solution.py:112
  46.6 18.7 %collective-permute-start.9 = (bf16[8,480,128]{2,1,0:T(8,128)(2,1)S(1)}, bf16[8,480,128]{2,1,0:T(8,128)(2,1)}, u32[]{:S(2)}, u32[]{:S(2)}) collective-permute-start(bf16[8,480,128]{2,1,0:T(8,128)(2,1)S(1)} %pad_maximum_fusion.refs_0_), channel_id=1, source_target_pairs={{0,8},{1,9},{2,10},{3,11},{4,12},{5,13},{6,14},{7,15},{8,0},{9,1},... | collective-permute-start | bytes 2949128 | tf_op jit(solution)/shard_map/ppermute | solution.py:112
  51.5 14.3 %collective-permute-start.15 = (bf16[8,480,128]{2,1,0:T(8,128)(2,1)S(1)}, bf16[8,480,128]{2,1,0:T(8,128)(2,1)}, u32[]{:S(2)}, u32[]{:S(2)}) collective-permute-start(bf16[8,480,128]{2,1,0:T(8,128)(2,1)S(1)} %pad_maximum_fusion.1.refs_4_), channel_id=1, source_target_pairs={{0,2},{1,3},{2,0},{3,1},{4,6},{5,7},{6,4},{7,5},{8,10},{9,11},{10,... | collective-permute-start | bytes 2949128 | tf_op jit(solution)/shard_map/ppermute | solution.py:112
  53.0 10.6 %collective-permute-start.4 = (bf16[8,416,128]{2,1,0:T(8,128)(2,1)S(1)}, bf16[8,416,128]{2,1,0:T(8,128)(2,1)}, u32[]{:S(2)}, u32[]{:S(2)}) collective-permute-start(bf16[8,416,128]{2,1,0:T(8,128)(2,1)S(1)} %pad_maximum_fusion.2.refs_0_), channel_id=1, source_target_pairs={{0,1},{1,0},{2,3},{3,2},{4,5},{5,4},{6,7},{7,6},{8,9},{9,8},{10,11... | collective-permute-start | bytes 2555912 | tf_op jit(solution)/shard_map/ppermute | solution.py:112
  63.1 8.3 %collective-permute-start.10 = (bf16[8,480,128]{2,1,0:T(8,128)(2,1)S(1)}, bf16[8,480,128]{2,1,0:T(8,128)(2,1)S(1)}, u32[]{:S(2)}, u32[]{:S(2)}) collective-permute-start(bf16[8,480,128]{2,1,0:T(8,128)(2,1)S(1)} %pad_maximum_fusion.refs_0_), channel_id=1, source_target_pairs={{0,1},{1,0},{2,3},{3,2},{4,5},{5,4},{6,7},{7,6},{8,9},{9,8},{10,11... | collective-permute-start | bytes 2949128 | tf_op jit(solution)/shard_map/ppermute | solution.py:112
  63.6 7.8 %collective-permute-start.16 = (bf16[8,480,128]{2,1,0:T(8,128)(2,1)S(1)}, bf16[8,480,128]{2,1,0:T(8,128)(2,1)S(1)}, u32[]{:S(2)}, u32[]{:S(2)}) collective-permute-start(bf16[8,480,128]{2,1,0:T(8,128)(2,1)S(1)} %pad_maximum_fusion.1.refs_4_), channel_id=1, source_target_pairs={{0,1},{1,0},{2,3},{3,2},{4,5},{5,4},{6,7},{7,6},{8,9},{9,8},{10,11... | collective-permute-start | bytes 2949128 | tf_op jit(solution)/shard_map/ppermute | solution.py:112
  90.8 10.1 %collective-permute-start.18 = (bf16[16,960,128]{2,1,0:T(8,128)(2,1)}, bf16[16,960,128]{2,1,0:T(8,128)(2,1)S(1)}, u32[]{:S(2)}, u32[]{:S(2)}) collective-permute-start(bf16[16,960,128]{2,1,0:T(8,128)(2,1)} %get-tuple-element.53), channel_id=1, source_target_pairs={{0,1},{1,0},{2,3},{3,2},{4,5},{5,4},{6,7},{7,6},{8,9},{9,8},{10,11... | collective-permute-start | bytes 11796488 | tf_op jit(solution)/shard_map/ppermute | solution.py:112
  102.4 22.6 %collective-permute-start.28 = (bf16[8,448,128]{2,1,0:T(8,128)(2,1)S(1)}, bf16[8,448,128]{2,1,0:T(8,128)(2,1)S(1)}, u32[]{:S(2)}, u32[]{:S(2)}) collective-permute-start(bf16[8,448,128]{2,1,0:T(8,128)(2,1)S(1)} %get-tuple-element.61), channel_id=1, source_target_pairs={{0,2},{1,3},{2,0},{3,1},{4,6},{5,7},{6,4},{7,5},{8,10},{9,11},{10,... | collective-permute-start | bytes 2752520 | tf_op jit(solution)/shard_map/ppermute | solution.py:112
  103.9 23.3 %collective-permute-start.20 = (bf16[8,464,128]{2,1,0:T(8,128)(2,1)S(1)}, bf16[8,464,128]{2,1,0:T(8,128)(2,1)S(1)}, u32[]{:S(2)}, u32[]{:S(2)}) collective-permute-start(bf16[8,464,128]{2,1,0:T(8,128)(2,1)S(1)} %get-tuple-element.57), channel_id=1, source_target_pairs={{0,4},{1,5},{2,6},{3,7},{4,0},{5,1},{6,2},{7,3},{8,12},{9,13},{10,... | collective-permute-start | bytes 2850824 | tf_op jit(solution)/shard_map/ppermute | solution.py:112
  104.0 25.1 %collective-permute-start.24 = (bf16[8,464,128]{2,1,0:T(8,128)(2,1)S(1)}, bf16[8,464,128]{2,1,0:T(8,128)(2,1)S(1)}, u32[]{:S(2)}, u32[]{:S(2)}) collective-permute-start(bf16[8,464,128]{2,1,0:T(8,128)(2,1)S(1)} %get-tuple-element.59), channel_id=1, source_target_pairs={{0,8},{1,9},{2,10},{3,11},{4,12},{5,13},{6,14},{7,15},{8,0},{9,1},... | collective-permute-start | bytes 2850824 | tf_op jit(solution)/shard_map/ppermute | solution.py:112
  125.2 12.3 %collective-permute-start.29 = (bf16[4,448,128]{2,1,0:T(8,128)(2,1)S(1)}, bf16[4,448,128]{2,1,0:T(8,128)(2,1)S(1)}, u32[]{:S(2)}, u32[]{:S(2)}) collective-permute-start(bf16[4,448,128]{2,1,0:T(8,128)(2,1)S(1)} %get-tuple-element.74), channel_id=1, source_target_pairs={{0,8},{1,9},{2,10},{3,11},{4,12},{5,13},{6,14},{7,15},{8,0},{9,1},... | collective-permute-start | bytes 1376264 | tf_op jit(solution)/shard_map/ppermute | solution.py:112
  127.5 12.1 %collective-permute-start.21 = (bf16[4,464,128]{2,1,0:T(8,128)(2,1)S(1)}, bf16[4,464,128]{2,1,0:T(8,128)(2,1)S(1)}, u32[]{:S(2)}, u32[]{:S(2)}) collective-permute-start(bf16[4,464,128]{2,1,0:T(8,128)(2,1)S(1)} %get-tuple-element.70), channel_id=1, source_target_pairs={{0,2},{1,3},{2,0},{3,1},{4,6},{5,7},{6,4},{7,5},{8,10},{9,11},{10,... | collective-permute-start | bytes 1425416 | tf_op jit(solution)/shard_map/ppermute | solution.py:112
  129.3 13.7 %collective-permute-start.25 = (bf16[4,464,128]{2,1,0:T(8,128)(2,1)S(1)}, bf16[4,464,128]{2,1,0:T(8,128)(2,1)S(1)}, u32[]{:S(2)}, u32[]{:S(2)}) collective-permute-start(bf16[4,464,128]{2,1,0:T(8,128)(2,1)S(1)} %get-tuple-element.72), channel_id=1, source_target_pairs={{0,4},{1,5},{2,6},{3,7},{4,0},{5,1},{6,2},{7,3},{8,12},{9,13},{10,... | collective-permute-start | bytes 1425416 | tf_op jit(solution)/shard_map/ppermute | solution.py:112
  137.6 8.4 %collective-permute-start.30 = (bf16[2,448,128]{2,1,0:T(8,128)(2,1)S(1)}, bf16[2,448,128]{2,1,0:T(8,128)(2,1)S(1)}, u32[]{:S(2)}, u32[]{:S(2)}) collective-permute-start(bf16[2,448,128]{2,1,0:T(8,128)(2,1)S(1)} %get-tuple-element.80), channel_id=1, source_target_pairs={{0,4},{1,5},{2,6},{3,7},{4,0},{5,1},{6,2},{7,3},{8,12},{9,13},{10,... | collective-permute-start | bytes 688136 | tf_op jit(solution)/shard_map/ppermute | solution.py:112
  139.8 15.7 %collective-permute-start.22 = (bf16[2,464,128]{2,1,0:T(8,128)(2,1)S(1)}, bf16[2,464,128]{2,1,0:T(8,128)(2,1)S(1)}, u32[]{:S(2)}, u32[]{:S(2)}) collective-permute-start(bf16[2,464,128]{2,1,0:T(8,128)(2,1)S(1)} %get-tuple-element.76), channel_id=1, source_target_pairs={{0,16},{1,17},{2,18},{3,19},{4,20},{5,21},{6,22},{7,23},{8,24},{9,... | collective-permute-start | bytes 712712 | tf_op jit(solution)/shard_map/ppermute | solution.py:112
  143.2 12.4 %collective-permute-start.26 = (bf16[2,464,128]{2,1,0:T(8,128)(2,1)S(1)}, bf16[2,464,128]{2,1,0:T(8,128)(2,1)S(1)}, u32[]{:S(2)}, u32[]{:S(2)}) collective-permute-start(bf16[2,464,128]{2,1,0:T(8,128)(2,1)S(1)} %get-tuple-element.78), channel_id=1, source_target_pairs={{0,2},{1,3},{2,0},{3,1},{4,6},{5,7},{6,4},{7,5},{8,10},{9,11},{10,... | collective-permute-start | bytes 712712 | tf_op jit(solution)/shard_map/ppermute | solution.py:112
  146.1 12.2 %collective-permute-start.31 = (bf16[1,448,128]{2,1,0:T(8,128)(2,1)S(1)}, bf16[1,448,128]{2,1,0:T(8,128)(2,1)S(1)}, u32[]{:S(2)}, u32[]{:S(2)}) collective-permute-start(bf16[1,448,128]{2,1,0:T(8,128)(2,1)S(1)} %add_convert_fusion.16), channel_id=1, source_target_pairs={{0,16},{1,17},{2,18},{3,19},{4,20},{5,21},{6,22},{7,23},{8,24},{9,... | collective-permute-start | bytes 344072 | tf_op jit(solution)/shard_map/ppermute | solution.py:112
  (17 other events, 145.3 us)

commit v3 on v2

--- a/solution.py
+++ b/solution.py
@@ -367,28 +367,57 @@
         gains[:, number * LANES : (number + 1) * LANES] = tile
 
 
-def attn_forward_kernel(plan, gain_len, device_ref, hidden_in, tables, *refs):
+def layer_kernel(
+    attn_plan,
+    ffn_plan,
+    staged,
+    plan_out,
+    gain_len,
+    device_ref,
+    hidden_in,
+    cotangent,
+    tables,
+    *refs,
+):
     if not gain_len:
         given, refs = refs[0], refs[1:]
-    sources = refs[: len(plan)]
-    refs = refs[len(plan) :]
-    qkv_weight, out_weight, gains, attn_out, mid_stream = refs[:5]
-    staging, spread, tails, context, sems = refs[5:]
+    attn_sources = refs[: len(attn_plan)]
+    ffn_sources = refs[len(attn_plan) : len(attn_plan) + len(ffn_plan)]
+    refs = refs[len(attn_plan) + len(ffn_plan) :]
+    qkv_weight, out_weight, gains = refs[:3]
+    block_out, delta_mid_ref, delta_attn_ref, late_gains = refs[3:7]
+    targets = refs[7:-16]
+    staging, tails, context, attn_out, mid_ref, attn_sems = refs[-16:-10]
+    spread, gate_weight, up_weight, down_weight = refs[-10:-6]
+    gates, ups, hidden, delta_gate, delta_up, sems = refs[-6:]
+    device = device_ref[0]
+    ffn_copies, ffn_views = [], []
+    for source, (target, first_index, first_row) in zip(ffn_sources, staged):
+        count, rows = source.shape[:2]
+        held = targets[target]
+        ffn_copies.append(
+            pltpu.make_async_copy(
+                source,
+                held.at[pl.ds(first_index, count), pl.ds(first_row, rows), :],
+                sems.at[len(ffn_copies)],
+            )
+        )
+        ffn_views.append((held, first_index, count, first_row))
     copies, views = [], []
-    for number, source in enumerate(sources):
+    for number, source in enumerate(attn_sources):
         count = source.shape[0]
         held = staging.at[pl.ds(number * count, count)]
-        copies.append(pltpu.make_async_copy(source, held, sems.at[number]))
+        copies.append(pltpu.make_async_copy(source, held, attn_sems.at[number]))
         views.append((held, 0, count, 0))
-    for copy in copies:
+    for copy in copies + ffn_copies:
         copy.start()
-    for copy, step, view in zip(copies, plan, views):
+    for copy, step, view in zip(copies, attn_plan, views):
         copy.wait()
         spread_blocks(
             ATTN_PADDED,
             [step],
             [view],
-            device_ref[0],
+            device,
             spread,
             tails if gain_len else None,
         )
@@ -411,77 +440,12 @@
     out = jnp.dot(context[...], out_weight[...], preferred_element_type=jnp.float32)
     attn_out[...] = out
     gain_post = gains[:, D + 2 * HD : 2 * D + 2 * HD]
-    mid_stream[...] = hidden_in[...].astype(jnp.float32) + rms_scale(out, gain_post)
-
-
-def forward_attn(plan, gain_len, tail_rows, devices, device, hidden_in, tables, given, arrays):
-    shapes = [
-        jax.ShapeDtypeStruct((D, HQ + 2 * HD), jnp.bfloat16),
-        jax.ShapeDtypeStruct((HQ, D), jnp.bfloat16),
-        jax.ShapeDtypeStruct((1, 4 * D + 2 * HD), jnp.float32),
-        jax.ShapeDtypeStruct((CAP, D), jnp.float32),
-        jax.ShapeDtypeStruct((CAP, D), jnp.float32),
-    ]
-    given = [] if gain_len else [given]
-    held = (sum(array.shape[0] for array in arrays),) + arrays[0].shape[1:]
-    return pl.pallas_call(
-        functools.partial(attn_forward_kernel, plan, gain_len),
-        out_shape=shapes,
-        in_specs=[pl.BlockSpec(memory_space=pltpu.SMEM)]
-        + whole_specs(2 + len(given))
-        + [pl.BlockSpec(memory_space=pltpu.HBM)] * len(arrays),
-        out_specs=whole_specs(len(shapes)),
-        scratch_shapes=[
-            pltpu.VMEM(held, jnp.bfloat16),
-            pltpu.VMEM((G1LEN // LANES + ATTN_PADDED, LANES), jnp.float32),
-            pltpu.VMEM((devices, tail_rows, LANES) if gain_len else (1, ROWS, LANES), jnp.bfloat16),
-            pltpu.VMEM((CAP, HQ), jnp.bfloat16),
-            pltpu.SemaphoreType.DMA((len(arrays),)),
-        ],
-        compiler_params=pltpu.CompilerParams(vmem_limit_bytes=24 << 20),
-        cost_estimate=pl.CostEstimate(flops=0, bytes_accessed=64 << 20, transcendentals=0),
-    )(device, hidden_in, tables, *given, *arrays)
-
-
-def ffn_kernel(
-    plan_in,
-    staged,
-    plan_out,
-    device_ref,
-    mid_ref,
-    attn_out,
-    cotangent,
-    tables,
-    gains,
-    *refs,
-):
-    sources = refs[: len(plan_in)]
-    refs = refs[len(plan_in) :]
-    block_out, delta_mid_ref, delta_attn_ref, late_gains = refs[:4]
-    targets = refs[4:-10]
-    spread, gate_weight, up_weight, down_weight = refs[-10:-6]
-    gates, ups, hidden, delta_gate, delta_up, sems = refs[-6:]
-    device = device_ref[0]
-    copies, views = [], []
-    for source, (target, first_index, first_row) in zip(sources, staged):
-        count, rows = source.shape[:2]
-        held = targets[target]
-        copies.append(
-            pltpu.make_async_copy(
-                source,
-                held.at[pl.ds(first_index, count), pl.ds(first_row, rows), :],
-                sems.at[len(copies)],
-            )
-        )
-        views.append((held, first_index, count, first_row))
-    for copy in copies:
-        copy.start()
+    mid_ref[...] = hidden_in[...].astype(jnp.float32) + rms_scale(out, gain_post)
     mid_stream = mid_ref[...]
-    gain_post = gains[:, D + 2 * HD : 2 * D + 2 * HD]
     gain_mid = gains[:, 2 * D + 2 * HD : 3 * D + 2 * HD]
     gain_last = gains[:, 3 * D + 2 * HD :]
     normed_mid = rms_scale(mid_stream, gain_mid).astype(jnp.bfloat16)
-    for copy, plan, view in zip(copies, plan_in, views):
+    for copy, plan, view in zip(ffn_copies, ffn_plan, ffn_views):
         copy.wait()
         spread_blocks(FFN_PADDED, [plan], [view], device, spread, None)
     fold_matrices(
@@ -532,27 +496,53 @@
     place_blocks(FFN_PADDED, plan_out, device, spread, None, targets)
 
 
-def run_ffn(
-    plan_in, staged, plan_out, block_shapes, device, mid, attn_out, cotangent, tables, gains, arrays
+def run_layer(
+    attn_plan,
+    ffn_plan,
+    staged,
+    plan_out,
+    block_shapes,
+    gain_len,
+    tail_rows,
+    devices,
+    device,
+    hidden_in,
+    cotangent,
+    tables,
+    given,
+    attn_arrays,
+    ffn_arrays,
 ):
-    flat_rows = G2LEN // LANES + FFN_PADDED
     shapes = [
+        jax.ShapeDtypeStruct((D, HQ + 2 * HD), jnp.bfloat16),
+        jax.ShapeDtypeStruct((HQ, D), jnp.bfloat16),
+        jax.ShapeDtypeStruct((1, 4 * D + 2 * HD), jnp.float32),
         jax.ShapeDtypeStruct((CAP, D), jnp.bfloat16),
         jax.ShapeDtypeStruct((CAP, D), jnp.float32),
         jax.ShapeDtypeStruct((CAP, D), jnp.bfloat16),
         jax.ShapeDtypeStruct((3, D), jnp.float32),
     ] + [jax.ShapeDtypeStruct(shape, jnp.bfloat16) for shape in block_shapes]
+    given = [] if gain_len else [given]
+    arrays = [*attn_arrays, *ffn_arrays]
+    held = (sum(array.shape[0] for array in attn_arrays),) + attn_arrays[0].shape[1:]
+    model = pltpu.VMEM((CAP, D), jnp.float32)
     wide = pltpu.VMEM((CAP, FF), jnp.float32)
     narrow = pltpu.VMEM((CAP, FF), jnp.bfloat16)
     return pl.pallas_call(
-        functools.partial(ffn_kernel, plan_in, staged, plan_out),
+        functools.partial(layer_kernel, attn_plan, ffn_plan, staged, plan_out, gain_len),
         out_shape=shapes,
         in_specs=[pl.BlockSpec(memory_space=pltpu.SMEM)]
-        + whole_specs(5)
+        + whole_specs(3 + len(given))
         + [pl.BlockSpec(memory_space=pltpu.HBM)] * len(arrays),
         out_specs=whole_specs(len(shapes)),
         scratch_shapes=[
-            pltpu.VMEM((flat_rows, LANES), jnp.float32),
+            pltpu.VMEM(held, jnp.bfloat16),
+            pltpu.VMEM((devices, tail_rows, LANES) if gain_len else (1, ROWS, LANES), jnp.bfloat16),
+            pltpu.VMEM((CAP, HQ), jnp.bfloat16),
+            model,
+            model,
+            pltpu.SemaphoreType.DMA((len(attn_arrays),)),
+            pltpu.VMEM((G2LEN // LANES + FFN_PADDED, LANES), jnp.float32),
             pltpu.VMEM((D, FF), jnp.bfloat16),
             pltpu.VMEM((D, FF), jnp.bfloat16),
             pltpu.VMEM((FF, D), jnp.bfloat16),
@@ -561,11 +551,11 @@
             narrow,
             narrow,
             narrow,
-            pltpu.SemaphoreType.DMA((len(arrays),)),
+            pltpu.SemaphoreType.DMA((len(ffn_arrays),)),
         ],
-        compiler_params=pltpu.CompilerParams(vmem_limit_bytes=44 << 20),
+        compiler_params=pltpu.CompilerParams(vmem_limit_bytes=52 << 20),
         cost_estimate=pl.CostEstimate(flops=0, bytes_accessed=0, transcendentals=0),
-    )(device, mid, attn_out, cotangent, tables, gains, *arrays)
+    )(device, hidden_in, cotangent, tables, *given, *arrays)
 
 
 def attn_back_kernel(
@@ -828,17 +818,6 @@
     given = None
     if not aligned:
         given = tails.reshape(devices, -1)[:, :gain_len].astype(jnp.float32).reshape(1, -1)
-    qkv_weight, out_weight, gains, attn_out, mid_stream = forward_attn(
-        plan,
-        gain_len if aligned else 0,
-        tail_rows,
-        devices,
-        here,
-        hidden_in,
-        tables,
-        given,
-        arrays,
-    )
     orders = bit_orders(devices, ("yxba", "ayxb", "xayb"))
     out_plan, block_shapes, ffn_parts = scatter_plan(ffn_rows, 0, orders, devices)
     staged = [(0, 0, 0)]
@@ -848,17 +827,21 @@
             for low, _ in cut_rows(ffn_rows, 2)
             for part in range(4)
         ]
-    block_out, delta_mid, delta_attn, late_gains, *found = run_ffn(
+    qkv_weight, out_weight, gains, block_out, delta_mid, delta_attn, late_gains, *found = run_layer(
+        plan,
         ffn_plan,
         staged,
         out_plan,
         block_shapes,
+        gain_len if aligned else 0,
+        tail_rows,
+        devices,
         here,
-        mid_stream,
-        attn_out,
+        hidden_in,
         cotangent,
         tables,
-        gains,
+        given,
+        arrays,
         ffn_arrays,
     )
     ffn_home, ffn_away = blocks_of(found, None, ffn_parts, orders, devices, here)

time: 164 us -> 174 us (1.061)
  waiting for transfers between devices: 85.9 us -> 89.9 us
  local copies, waits for them, and re-layouts: 0.99 us -> 4.8 us
  Pallas kernels: 31.6 us -> 34 us
    ppermute x32, waiting for transfers between devices: 85.9 us -> 89.9 us  [across(): lax.ppermute(block, 'dp', [(i, i ^ 1 << bit) for i in range(devices)])]
    unnamed x21 -> x37, local copies, waits for them, and re-layouts: 0.1 us -> 3.91 us
    pallas_call x2 -> x1, Pallas kernels: 24 us -> 26.5 us  [run_layer(): pl.pallas_call(functools.partial(layer_kernel, attn_plan, ffn_plan, stage...]
  transfers between devices with their start and end apart: 32 -> 32, of which waited for: 20 -> 23; matrix products, arithmetic and copies ran while one was open for 2% -> 2% of each run, Pallas kernels for 7% -> 3%
where the time goes in v3:
time: 174 us
  waiting for transfers between devices  89.9 us (52%)
  starting transfers between devices  38.7 us (22%)
  Pallas kernels  34 us (20%)
  other arithmetic  5.7 us (3%)
  local copies, waits for them, and re-layouts  4.8 us (3%)
    ppermute x32, waiting for transfers between devices, across(): lax.ppermute(block, 'dp', [(i, i ^ 1 << bit) for i in range(devices)])  89.9 us
    ppermute x32, starting transfers between devices, across(): lax.ppermute(block, 'dp', [(i, i ^ 1 << bit) for i in range(devices)])  38.7 us
    pallas_call x1, Pallas kernels, run_layer(): pl.pallas_call(functools.partial(layer_kernel, attn_plan, ffn_plan, stage...  26.5 us
    pallas_call x1, Pallas kernels, back_attn(): pl.pallas_call(functools.partial(attn_back_kernel, plan, gain_len), out_s...  6.04 us
    unnamed x37, local copies, waits for them, and re-layouts  3.91 us
  transfers between devices with their start and end apart: 32, of which 23 were waited for; matrix products, arithmetic and copies ran while one was open for 2% of the time, Pallas kernels for 3%

profile of v3, /device:TPU:0, one launch (start us, length us, event | category | flops | bytes accessed | tf_op | source)
XLA Modules:
  0.0 174.3 jit_solution(960514997750968803)
XLA Ops:
  2.5 3.0 %collective-permute-start = (bf16[1,416,128]{2,1,0:T(8,128)(2,1)S(1)}, bf16[1,416,128]{2,1,0:T(8,128)(2,1)S(1)}, u32[]{:S(2)}, u32[]{:S(2)}) collective-permute-start(bf16[1,416,128]{2,1,0:T(8,128)(2,1)S(1)} %bitcast.26), channel_id=1, source_target_pairs={{0,8},{1,9},{2,10},{3,11},{4,12},{5,13},{6,14},{7,15},{8,0},{9,1},... | collective-permute-start | bytes 319496 | tf_op jit(solution)/shard_map/ppermute | solution.py:112
  5.5 2.7 %collective-permute-start.12 = (bf16[1,480,128]{2,1,0:T(8,128)(2,1)S(1)}, bf16[1,480,128]{2,1,0:T(8,128)(2,1)S(1)}, u32[]{:S(2)}, u32[]{:S(2)}) collective-permute-start(bf16[1,480,128]{2,1,0:T(8,128)(2,1)S(1)} %get-tuple-element.77), channel_id=1, source_target_pairs={{0,16},{1,17},{2,18},{3,19},{4,20},{5,21},{6,22},{7,23},{8,24},{9,... | collective-permute-start | bytes 368648 | tf_op jit(solution)/shard_map/ppermute | solution.py:112
  8.5 3.9 %collective-permute-start.1 = (bf16[2,416,128]{2,1,0:T(8,128)(2,1)S(1)}, bf16[2,416,128]{2,1,0:T(8,128)(2,1)S(1)}, u32[]{:S(2)}, u32[]{:S(2)}) collective-permute-start(bf16[2,416,128]{2,1,0:T(8,128)(2,1)S(1)} %pad_maximum_fusion.9), channel_id=1, source_target_pairs={{0,16},{1,17},{2,18},{3,19},{4,20},{5,21},{6,22},{7,23},{8,24},{9,... | collective-permute-start | bytes 638984 | tf_op jit(solution)/shard_map/ppermute | solution.py:112
  12.5 9.7 %collective-permute-done.12 = bf16[1,480,128]{2,1,0:T(8,128)(2,1)S(1)} collective-permute-done((bf16[1,480,128]{2,1,0:T(8,128)(2,1)S(1)}, bf16[1,480,128]{2,1,0:T(8,128)(2,1)S(1)}, u32[]{:S(2)}, u32[]{:S(2)}) %collective-permute-start.12) | collective-permute-done | bytes 122912 | tf_op jit(solution)/shard_map/ppermute | solution.py:112
  22.1 2.6 %collective-permute-done.6 = bf16[1,480,128]{2,1,0:T(8,128)(2,1)S(1)} collective-permute-done((bf16[1,480,128]{2,1,0:T(8,128)(2,1)S(1)}, bf16[1,480,128]{2,1,0:T(8,128)(2,1)S(1)}, u32[]{:S(2)}, u32[]{:S(2)}) %collective-permute-start.6) | collective-permute-done | bytes 122912 | tf_op jit(solution)/shard_map/ppermute | solution.py:112
  31.1 4.2 %collective-permute-done.7 = bf16[2,480,128]{2,1,0:T(8,128)(2,1)S(1)} collective-permute-done((bf16[2,480,128]{2,1,0:T(8,128)(2,1)S(1)}, bf16[2,480,128]{2,1,0:T(8,128)(2,1)S(1)}, u32[]{:S(2)}, u32[]{:S(2)}) %collective-permute-start.7) | collective-permute-done | bytes 245792 | tf_op jit(solution)/shard_map/ppermute | solution.py:112
  35.5 6.3 %collective-permute-done.2 = bf16[4,416,128]{2,1,0:T(8,128)(2,1)S(1)} collective-permute-done((bf16[4,416,128]{2,1,0:T(8,128)(2,1)S(1)}, bf16[4,416,128]{2,1,0:T(8,128)(2,1)S(1)}, u32[]{:S(2)}, u32[]{:S(2)}) %collective-permute-start.2) | collective-permute-done | bytes 426016 | tf_op jit(solution)/shard_map/ppermute | solution.py:112
  42.5 2.3 %collective-permute-done.14 = bf16[4,480,128]{2,1,0:T(8,128)(2,1)S(1)} collective-permute-done((bf16[4,480,128]{2,1,0:T(8,128)(2,1)S(1)}, bf16[4,480,128]{2,1,0:T(8,128)(2,1)S(1)}, u32[]{:S(2)}, u32[]{:S(2)}) %collective-permute-start.14) | collective-permute-done | bytes 491552 | tf_op jit(solution)/shard_map/ppermute | solution.py:112
  44.8 1.7 collective-permute-done.8
  46.6 4.7 %collective-permute-start.9 = (bf16[8,480,128]{2,1,0:T(8,128)(2,1)S(1)}, bf16[8,480,128]{2,1,0:T(8,128)(2,1)}, u32[]{:S(2)}, u32[]{:S(2)}) collective-permute-start(bf16[8,480,128]{2,1,0:T(8,128)(2,1)S(1)} %pad_maximum_fusion.refs_4_), channel_id=1, source_target_pairs={{0,8},{1,9},{2,10},{3,11},{4,12},{5,13},{6,14},{7,15},{8,0},{9,1},... | collective-permute-start | bytes 2949128 | tf_op jit(solution)/shard_map/ppermute | solution.py:112
  53.0 9.7 %collective-permute-done.3.refs_1_ = bf16[8,416,128]{2,1,0:T(8,128)(2,1)} collective-permute-done((bf16[8,416,128]{2,1,0:T(8,128)(2,1)S(1)}, bf16[8,416,128]{2,1,0:T(8,128)(2,1)}, u32[]{:S(2)}, u32[]{:S(2)}) %collective-permute-start.3) | collective-permute-done | bytes 852000 | tf_op jit(solution)/shard_map/ppermute | solution.py:112
  71.9 26.5 %shard_map.118 = (bf16[640,1536]{1,0:T(8,128)(2,1)}, bf16[1024,640]{1,0:T(8,128)(2,1)}, f32[1,3072]{1,0:T(1,128)S(1)}, bf16[128,640]{1,0:T(8,128)(2,1)}, f32[128...) custom-call(s32[1]{0:T(128)} %bitcast.device_ref, ...), custom_call_target="tpu_custom_call" | custom-call | tf_op jit(solution)/shard_map/pallas_call | solution.py:531
  101.5 6.0 %shard_map.119 = (f32[128,640]{1,0:T(8,128)}, f32[1,3072]{1,0:T(1,128)}, bf16[16,416,128]{2,1,0:T(8,128)(2,1)S(1)}, bf16[16,416,128]{2,1,0:T(8,128)(2,1)S(1)}) custom-call(s32[1]{0:T(128)} %bitcast.device_ref, bf16[128,640]{1,0:T(8,128)(2,1)S(1)} %get-tuple-element.41.delta_attn, f32[128,640]{1,0:T(8,128)S(1)} %get-tuple-element.42.delta_mid, ...), custom_call_target="tpu_custom_call" | custom-call | tf_op jit(solution)/shard_map/pallas_call | solution.py:658
  107.9 3.2 %collective-permute-done.19.refs_3_ = bf16[16,416,128]{2,1,0:T(8,128)(2,1)S(1)} collective-permute-done((bf16[16,416,128]{2,1,0:T(8,128)(2,1)S(1)}, bf16[16,416,128]{2,1,0:T(8,128)(2,1)S(1)}, u32[]{:S(2)}, u32[]{:S(2)}) %collective-permute-start.19) | collective-permute-done | bytes 1703968 | tf_op jit(solution)/shard_map/ppermute | solution.py:112
  114.2 2.0 %collective-permute-start.24 = (bf16[8,464,128]{2,1,0:T(8,128)(2,1)S(1)}, bf16[8,464,128]{2,1,0:T(8,128)(2,1)S(1)}, u32[]{:S(2)}, u32[]{:S(2)}) collective-permute-start(bf16[8,464,128]{2,1,0:T(8,128)(2,1)S(1)} %get-tuple-element.55), channel_id=1, source_target_pairs={{0,8},{1,9},{2,10},{3,11},{4,12},{5,13},{6,14},{7,15},{8,0},{9,1},... | collective-permute-start | bytes 2850824 | tf_op jit(solution)/shard_map/ppermute | solution.py:112
  116.2 19.1 %collective-permute-done.28 = bf16[8,448,128]{2,1,0:T(8,128)(2,1)S(1)} collective-permute-done((bf16[8,448,128]{2,1,0:T(8,128)(2,1)S(1)}, bf16[8,448,128]{2,1,0:T(8,128)(2,1)S(1)}, u32[]{:S(2)}, u32[]{:S(2)}) %collective-permute-start.28) | collective-permute-done | bytes 917536 | tf_op jit(solution)/shard_map/ppermute | solution.py:112
  135.6 2.1 %collective-permute-start.29 = (bf16[4,448,128]{2,1,0:T(8,128)(2,1)S(1)}, bf16[4,448,128]{2,1,0:T(8,128)(2,1)S(1)}, u32[]{:S(2)}, u32[]{:S(2)}) collective-permute-start(bf16[4,448,128]{2,1,0:T(8,128)(2,1)S(1)} %get-tuple-element.70), channel_id=1, source_target_pairs={{0,8},{1,9},{2,10},{3,11},{4,12},{5,13},{6,14},{7,15},{8,0},{9,1},... | collective-permute-start | bytes 1376264 | tf_op jit(solution)/shard_map/ppermute | solution.py:112
  140.5 7.4 %collective-permute-done.29 = bf16[4,448,128]{2,1,0:T(8,128)(2,1)S(1)} collective-permute-done((bf16[4,448,128]{2,1,0:T(8,128)(2,1)S(1)}, bf16[4,448,128]{2,1,0:T(8,128)(2,1)S(1)}, u32[]{:S(2)}, u32[]{:S(2)}) %collective-permute-start.29) | collective-permute-done | bytes 458784 | tf_op jit(solution)/shard_map/ppermute | solution.py:112
  150.1 2.2 %collective-permute-start.22 = (bf16[2,464,128]{2,1,0:T(8,128)(2,1)S(1)}, bf16[2,464,128]{2,1,0:T(8,128)(2,1)S(1)}, u32[]{:S(2)}, u32[]{:S(2)}) collective-permute-start(bf16[2,464,128]{2,1,0:T(8,128)(2,1)S(1)} %get-tuple-element.72), channel_id=1, source_target_pairs={{0,16},{1,17},{2,18},{3,19},{4,20},{5,21},{6,22},{7,23},{8,24},{9,... | collective-permute-start | bytes 712712 | tf_op jit(solution)/shard_map/ppermute | solution.py:112
  153.6 2.8 %collective-permute-done.30 = bf16[2,448,128]{2,1,0:T(8,128)(2,1)S(1)} collective-permute-done((bf16[2,448,128]{2,1,0:T(8,128)(2,1)S(1)}, bf16[2,448,128]{2,1,0:T(8,128)(2,1)S(1)}, u32[]{:S(2)}, u32[]{:S(2)}) %collective-permute-start.30) | collective-permute-done | bytes 229408 | tf_op jit(solution)/shard_map/ppermute | solution.py:112
  157.8 8.0 %collective-permute-done.22 = bf16[2,464,128]{2,1,0:T(8,128)(2,1)S(1)} collective-permute-done((bf16[2,464,128]{2,1,0:T(8,128)(2,1)S(1)}, bf16[2,464,128]{2,1,0:T(8,128)(2,1)S(1)}, u32[]{:S(2)}, u32[]{:S(2)}) %collective-permute-start.22) | collective-permute-done | bytes 237600 | tf_op jit(solution)/shard_map/ppermute | solution.py:112
  166.0 2.7 %collective-permute-start.27 = (bf16[1,464,128]{2,1,0:T(8,128)(2,1)S(1)}, bf16[1,464,128]{2,1,0:T(8,128)(2,1)S(1)}, u32[]{:S(2)}, u32[]{:S(2)}) collective-permute-start(bf16[1,464,128]{2,1,0:T(8,128)(2,1)S(1)} %add_convert_fusion.12), channel_id=1, source_target_pairs={{0,16},{1,17},{2,18},{3,19},{4,20},{5,21},{6,22},{7,23},{8,24},{9,... | collective-permute-start | bytes 356360 | tf_op jit(solution)/shard_map/ppermute | solution.py:112
  168.8 3.5 %collective-permute-done.23 = bf16[1,464,128]{2,1,0:T(8,128)(2,1)S(1)} collective-permute-done((bf16[1,464,128]{2,1,0:T(8,128)(2,1)S(1)}, bf16[1,464,128]{2,1,0:T(8,128)(2,1)S(1)}, u32[]{:S(2)}, u32[]{:S(2)}) %collective-permute-start.23) | collective-permute-done | bytes 118816 | tf_op jit(solution)/shard_map/ppermute | solution.py:112
  172.5 1.7 multiply_subtract_fusion
  (127 shorter events, 35.1 us)
Async XLA Ops:
  5.5 16.6 %collective-permute-start.12 = (bf16[1,480,128]{2,1,0:T(8,128)(2,1)S(1)}, bf16[1,480,128]{2,1,0:T(8,128)(2,1)S(1)}, u32[]{:S(2)}, u32[]{:S(2)}) collective-permute-start(bf16[1,480,128]{2,1,0:T(8,128)(2,1)S(1)} %get-tuple-element.77), channel_id=1, source_target_pairs={{0,16},{1,17},{2,18},{3,19},{4,20},{5,21},{6,22},{7,23},{8,24},{9,... | collective-permute-start | bytes 368648 | tf_op jit(solution)/shard_map/ppermute | solution.py:112
  8.2 16.6 %collective-permute-start.6 = (bf16[1,480,128]{2,1,0:T(8,128)(2,1)S(1)}, bf16[1,480,128]{2,1,0:T(8,128)(2,1)S(1)}, u32[]{:S(2)}, u32[]{:S(2)}) collective-permute-start(bf16[1,480,128]{2,1,0:T(8,128)(2,1)S(1)} %get-tuple-element.78), channel_id=1, source_target_pairs={{0,16},{1,17},{2,18},{3,19},{4,20},{5,21},{6,22},{7,23},{8,24},{9,... | collective-permute-start | bytes 368648 | tf_op jit(solution)/shard_map/ppermute | solution.py:112
  8.5 19.8 %collective-permute-start.1 = (bf16[2,416,128]{2,1,0:T(8,128)(2,1)S(1)}, bf16[2,416,128]{2,1,0:T(8,128)(2,1)S(1)}, u32[]{:S(2)}, u32[]{:S(2)}) collective-permute-start(bf16[2,416,128]{2,1,0:T(8,128)(2,1)S(1)} %pad_maximum_fusion.9), channel_id=1, source_target_pairs={{0,16},{1,17},{2,18},{3,19},{4,20},{5,21},{6,22},{7,23},{8,24},{9,... | collective-permute-start | bytes 638984 | tf_op jit(solution)/shard_map/ppermute | solution.py:112
  26.4 8.9 %collective-permute-start.7 = (bf16[2,480,128]{2,1,0:T(8,128)(2,1)S(1)}, bf16[2,480,128]{2,1,0:T(8,128)(2,1)S(1)}, u32[]{:S(2)}, u32[]{:S(2)}) collective-permute-start(bf16[2,480,128]{2,1,0:T(8,128)(2,1)S(1)} %pad_maximum_fusion.7), channel_id=1, source_target_pairs={{0,2},{1,3},{2,0},{3,1},{4,6},{5,7},{6,4},{7,5},{8,10},{9,11},{10,... | collective-permute-start | bytes 737288 | tf_op jit(solution)/shard_map/ppermute | solution.py:112
  28.3 13.5 %collective-permute-start.2 = (bf16[4,416,128]{2,1,0:T(8,128)(2,1)S(1)}, bf16[4,416,128]{2,1,0:T(8,128)(2,1)S(1)}, u32[]{:S(2)}, u32[]{:S(2)}) collective-permute-start(bf16[4,416,128]{2,1,0:T(8,128)(2,1)S(1)} %pad_maximum_fusion.5), channel_id=1, source_target_pairs={{0,2},{1,3},{2,0},{3,1},{4,6},{5,7},{6,4},{7,5},{8,10},{9,11},{10,... | collective-permute-start | bytes 1277960 | tf_op jit(solution)/shard_map/ppermute | solution.py:112
  35.3 9.5 %collective-permute-start.14 = (bf16[4,480,128]{2,1,0:T(8,128)(2,1)S(1)}, bf16[4,480,128]{2,1,0:T(8,128)(2,1)S(1)}, u32[]{:S(2)}, u32[]{:S(2)}) collective-permute-start(bf16[4,480,128]{2,1,0:T(8,128)(2,1)S(1)} %pad_maximum_fusion.4), channel_id=1, source_target_pairs={{0,8},{1,9},{2,10},{3,11},{4,12},{5,13},{6,14},{7,15},{8,0},{9,1},... | collective-permute-start | bytes 1474568 | tf_op jit(solution)/shard_map/ppermute | solution.py:112
  35.5 11.1 %collective-permute-start.8 = (bf16[4,480,128]{2,1,0:T(8,128)(2,1)S(1)}, bf16[4,480,128]{2,1,0:T(8,128)(2,1)S(1)}, u32[]{:S(2)}, u32[]{:S(2)}) collective-permute-start(bf16[4,480,128]{2,1,0:T(8,128)(2,1)S(1)} %pad_maximum_fusion.3), channel_id=1, source_target_pairs={{0,4},{1,5},{2,6},{3,7},{4,0},{5,1},{6,2},{7,3},{8,12},{9,13},{10,... | collective-permute-start | bytes 1474568 | tf_op jit(solution)/shard_map/ppermute | solution.py:112
  41.9 20.8 %collective-permute-start.3 = (bf16[8,416,128]{2,1,0:T(8,128)(2,1)S(1)}, bf16[8,416,128]{2,1,0:T(8,128)(2,1)}, u32[]{:S(2)}, u32[]{:S(2)}) collective-permute-start(bf16[8,416,128]{2,1,0:T(8,128)(2,1)S(1)} %pad_maximum_fusion.2.refs_0_), channel_id=1, source_target_pairs={{0,4},{1,5},{2,6},{3,7},{4,0},{5,1},{6,2},{7,3},{8,12},{9,13},{10,... | collective-permute-start | bytes 2555912 | tf_op jit(solution)/shard_map/ppermute | solution.py:112
  46.6 18.7 %collective-permute-start.9 = (bf16[8,480,128]{2,1,0:T(8,128)(2,1)S(1)}, bf16[8,480,128]{2,1,0:T(8,128)(2,1)}, u32[]{:S(2)}, u32[]{:S(2)}) collective-permute-start(bf16[8,480,128]{2,1,0:T(8,128)(2,1)S(1)} %pad_maximum_fusion.refs_4_), channel_id=1, source_target_pairs={{0,8},{1,9},{2,10},{3,11},{4,12},{5,13},{6,14},{7,15},{8,0},{9,1},... | collective-permute-start | bytes 2949128 | tf_op jit(solution)/shard_map/ppermute | solution.py:112
  51.5 14.3 %collective-permute-start.15 = (bf16[8,480,128]{2,1,0:T(8,128)(2,1)S(1)}, bf16[8,480,128]{2,1,0:T(8,128)(2,1)}, u32[]{:S(2)}, u32[]{:S(2)}) collective-permute-start(bf16[8,480,128]{2,1,0:T(8,128)(2,1)S(1)} %pad_maximum_fusion.1.refs_8_), channel_id=1, source_target_pairs={{0,2},{1,3},{2,0},{3,1},{4,6},{5,7},{6,4},{7,5},{8,10},{9,11},{10,... | collective-permute-start | bytes 2949128 | tf_op jit(solution)/shard_map/ppermute | solution.py:112
  53.0 10.6 %collective-permute-start.4 = (bf16[8,416,128]{2,1,0:T(8,128)(2,1)S(1)}, bf16[8,416,128]{2,1,0:T(8,128)(2,1)}, u32[]{:S(2)}, u32[]{:S(2)}) collective-permute-start(bf16[8,416,128]{2,1,0:T(8,128)(2,1)S(1)} %pad_maximum_fusion.2.refs_0_), channel_id=1, source_target_pairs={{0,1},{1,0},{2,3},{3,2},{4,5},{5,4},{6,7},{7,6},{8,9},{9,8},{10,11... | collective-permute-start | bytes 2555912 | tf_op jit(solution)/shard_map/ppermute | solution.py:112
  98.4 12.7 %collective-permute-start.18 = (bf16[16,960,128]{2,1,0:T(8,128)(2,1)}, bf16[16,960,128]{2,1,0:T(8,128)(2,1)S(1)}, u32[]{:S(2)}, u32[]{:S(2)}) collective-permute-start(bf16[16,960,128]{2,1,0:T(8,128)(2,1)} %get-tuple-element.49), channel_id=1, source_target_pairs={{0,1},{1,0},{2,3},{3,2},{4,5},{5,4},{6,7},{7,6},{8,9},{9,8},{10,11... | collective-permute-start | bytes 11796488 | tf_op jit(solution)/shard_map/ppermute | solution.py:112
  112.6 22.7 %collective-permute-start.28 = (bf16[8,448,128]{2,1,0:T(8,128)(2,1)S(1)}, bf16[8,448,128]{2,1,0:T(8,128)(2,1)S(1)}, u32[]{:S(2)}, u32[]{:S(2)}) collective-permute-start(bf16[8,448,128]{2,1,0:T(8,128)(2,1)S(1)} %get-tuple-element.57), channel_id=1, source_target_pairs={{0,2},{1,3},{2,0},{3,1},{4,6},{5,7},{6,4},{7,5},{8,10},{9,11},{10,... | collective-permute-start | bytes 2752520 | tf_op jit(solution)/shard_map/ppermute | solution.py:112
  114.2 23.4 %collective-permute-start.20 = (bf16[8,464,128]{2,1,0:T(8,128)(2,1)S(1)}, bf16[8,464,128]{2,1,0:T(8,128)(2,1)S(1)}, u32[]{:S(2)}, u32[]{:S(2)}) collective-permute-start(bf16[8,464,128]{2,1,0:T(8,128)(2,1)S(1)} %get-tuple-element.53), channel_id=1, source_target_pairs={{0,4},{1,5},{2,6},{3,7},{4,0},{5,1},{6,2},{7,3},{8,12},{9,13},{10,... | collective-permute-start | bytes 2850824 | tf_op jit(solution)/shard_map/ppermute | solution.py:112
  114.2 25.3 %collective-permute-start.24 = (bf16[8,464,128]{2,1,0:T(8,128)(2,1)S(1)}, bf16[8,464,128]{2,1,0:T(8,128)(2,1)S(1)}, u32[]{:S(2)}, u32[]{:S(2)}) collective-permute-start(bf16[8,464,128]{2,1,0:T(8,128)(2,1)S(1)} %get-tuple-element.55), channel_id=1, source_target_pairs={{0,8},{1,9},{2,10},{3,11},{4,12},{5,13},{6,14},{7,15},{8,0},{9,1},... | collective-permute-start | bytes 2850824 | tf_op jit(solution)/shard_map/ppermute | solution.py:112
  135.6 12.3 %collective-permute-start.29 = (bf16[4,448,128]{2,1,0:T(8,128)(2,1)S(1)}, bf16[4,448,128]{2,1,0:T(8,128)(2,1)S(1)}, u32[]{:S(2)}, u32[]{:S(2)}) collective-permute-start(bf16[4,448,128]{2,1,0:T(8,128)(2,1)S(1)} %get-tuple-element.70), channel_id=1, source_target_pairs={{0,8},{1,9},{2,10},{3,11},{4,12},{5,13},{6,14},{7,15},{8,0},{9,1},... | collective-permute-start | bytes 1376264 | tf_op jit(solution)/shard_map/ppermute | solution.py:112
  137.9 12.1 %collective-permute-start.21 = (bf16[4,464,128]{2,1,0:T(8,128)(2,1)S(1)}, bf16[4,464,128]{2,1,0:T(8,128)(2,1)S(1)}, u32[]{:S(2)}, u32[]{:S(2)}) collective-permute-start(bf16[4,464,128]{2,1,0:T(8,128)(2,1)S(1)} %get-tuple-element.66), channel_id=1, source_target_pairs={{0,2},{1,3},{2,0},{3,1},{4,6},{5,7},{6,4},{7,5},{8,10},{9,11},{10,... | collective-permute-start | bytes 1425416 | tf_op jit(solution)/shard_map/ppermute | solution.py:112
  139.7 13.7 %collective-permute-start.25 = (bf16[4,464,128]{2,1,0:T(8,128)(2,1)S(1)}, bf16[4,464,128]{2,1,0:T(8,128)(2,1)S(1)}, u32[]{:S(2)}, u32[]{:S(2)}) collective-permute-start(bf16[4,464,128]{2,1,0:T(8,128)(2,1)S(1)} %get-tuple-element.68), channel_id=1, source_target_pairs={{0,4},{1,5},{2,6},{3,7},{4,0},{5,1},{6,2},{7,3},{8,12},{9,13},{10,... | collective-permute-start | bytes 1425416 | tf_op jit(solution)/shard_map/ppermute | solution.py:112
  148.0 8.5 %collective-permute-start.30 = (bf16[2,448,128]{2,1,0:T(8,128)(2,1)S(1)}, bf16[2,448,128]{2,1,0:T(8,128)(2,1)S(1)}, u32[]{:S(2)}, u32[]{:S(2)}) collective-permute-start(bf16[2,448,128]{2,1,0:T(8,128)(2,1)S(1)} %get-tuple-element.76), channel_id=1, source_target_pairs={{0,4},{1,5},{2,6},{3,7},{4,0},{5,1},{6,2},{7,3},{8,12},{9,13},{10,... | collective-permute-start | bytes 688136 | tf_op jit(solution)/shard_map/ppermute | solution.py:112
  150.1 15.7 %collective-permute-start.22 = (bf16[2,464,128]{2,1,0:T(8,128)(2,1)S(1)}, bf16[2,464,128]{2,1,0:T(8,128)(2,1)S(1)}, u32[]{:S(2)}, u32[]{:S(2)}) collective-permute-start(bf16[2,464,128]{2,1,0:T(8,128)(2,1)S(1)} %get-tuple-element.72), channel_id=1, source_target_pairs={{0,16},{1,17},{2,18},{3,19},{4,20},{5,21},{6,22},{7,23},{8,24},{9,... | collective-permute-start | bytes 712712 | tf_op jit(solution)/shard_map/ppermute | solution.py:112
  153.5 12.4 %collective-permute-start.26 = (bf16[2,464,128]{2,1,0:T(8,128)(2,1)S(1)}, bf16[2,464,128]{2,1,0:T(8,128)(2,1)S(1)}, u32[]{:S(2)}, u32[]{:S(2)}) collective-permute-start(bf16[2,464,128]{2,1,0:T(8,128)(2,1)S(1)} %get-tuple-element.74), channel_id=1, source_target_pairs={{0,2},{1,3},{2,0},{3,1},{4,6},{5,7},{6,4},{7,5},{8,10},{9,11},{10,... | collective-permute-start | bytes 712712 | tf_op jit(solution)/shard_map/ppermute | solution.py:112
  156.5 12.2 %collective-permute-start.31 = (bf16[1,448,128]{2,1,0:T(8,128)(2,1)S(1)}, bf16[1,448,128]{2,1,0:T(8,128)(2,1)S(1)}, u32[]{:S(2)}, u32[]{:S(2)}) collective-permute-start(bf16[1,448,128]{2,1,0:T(8,128)(2,1)S(1)} %add_convert_fusion.16), channel_id=1, source_target_pairs={{0,16},{1,17},{2,18},{3,19},{4,20},{5,21},{6,22},{7,23},{8,24},{9,... | collective-permute-start | bytes 344072 | tf_op jit(solution)/shard_map/ppermute | solution.py:112
  165.8 6.4 %collective-permute-start.23 = (bf16[1,464,128]{2,1,0:T(8,128)(2,1)S(1)}, bf16[1,464,128]{2,1,0:T(8,128)(2,1)S(1)}, u32[]{:S(2)}, u32[]{:S(2)}) collective-permute-start(bf16[1,464,128]{2,1,0:T(8,128)(2,1)S(1)} %add_convert_fusion.14), channel_id=1, source_target_pairs={{0,8},{1,9},{2,10},{3,11},{4,12},{5,13},{6,14},{7,15},{8,0},{9,1},... | collective-permute-start | bytes 356360 | tf_op jit(solution)/shard_map/ppermute | solution.py:112
  166.0 6.3 %collective-permute-start.27 = (bf16[1,464,128]{2,1,0:T(8,128)(2,1)S(1)}, bf16[1,464,128]{2,1,0:T(8,128)(2,1)S(1)}, u32[]{:S(2)}, u32[]{:S(2)}) collective-permute-start(bf16[1,464,128]{2,1,0:T(8,128)(2,1)S(1)} %add_convert_fusion.12), channel_id=1, source_target_pairs={{0,16},{1,17},{2,18},{3,19},{4,20},{5,21},{6,22},{7,23},{8,24},{9,... | collective-permute-start | bytes 356360 | tf_op jit(solution)/shard_map/ppermute | solution.py:112
  (25 other events, 224.8 us)

commit v4 on v2

--- a/solution.py
+++ b/solution.py
@@ -445,7 +445,6 @@
 
 def ffn_kernel(
     plan_in,
-    staged,
     plan_out,
     device_ref,
     mid_ref,
@@ -458,32 +457,17 @@
     sources = refs[: len(plan_in)]
     refs = refs[len(plan_in) :]
     block_out, delta_mid_ref, delta_attn_ref, late_gains = refs[:4]
-    targets = refs[4:-10]
-    spread, gate_weight, up_weight, down_weight = refs[-10:-6]
-    gates, ups, hidden, delta_gate, delta_up, sems = refs[-6:]
+    targets = refs[4:-9]
+    spread, gate_weight, up_weight, down_weight = refs[-9:-5]
+    gates, ups, hidden, delta_gate, delta_up = refs[-5:]
     device = device_ref[0]
-    copies, views = [], []
-    for source, (target, first_index, first_row) in zip(sources, staged):
-        count, rows = source.shape[:2]
-        held = targets[target]
-        copies.append(
-            pltpu.make_async_copy(
-                source,
-                held.at[pl.ds(first_index, count), pl.ds(first_row, rows), :],
-                sems.at[len(copies)],
-            )
-        )
-        views.append((held, first_index, count, first_row))
-    for copy in copies:
-        copy.start()
+    views = [(source, 0, source.shape[0], 0) for source in sources]
     mid_stream = mid_ref[...]
     gain_post = gains[:, D + 2 * HD : 2 * D + 2 * HD]
     gain_mid = gains[:, 2 * D + 2 * HD : 3 * D + 2 * HD]
     gain_last = gains[:, 3 * D + 2 * HD :]
     normed_mid = rms_scale(mid_stream, gain_mid).astype(jnp.bfloat16)
-    for copy, plan, view in zip(copies, plan_in, views):
-        copy.wait()
-        spread_blocks(FFN_PADDED, [plan], [view], device, spread, None)
+    spread_blocks(FFN_PADDED, plan_in, views, device, spread, None)
     fold_matrices(
         spread, ((gate_weight, 0, D, FF), (up_weight, 0, D, FF), (down_weight, 0, FF, D))
     )
@@ -533,7 +517,7 @@
 
 
 def run_ffn(
-    plan_in, staged, plan_out, block_shapes, device, mid, attn_out, cotangent, tables, gains, arrays
+    plan_in, plan_out, block_shapes, device, mid, attn_out, cotangent, tables, gains, arrays
 ):
     flat_rows = G2LEN // LANES + FFN_PADDED
     shapes = [
@@ -545,11 +529,10 @@
     wide = pltpu.VMEM((CAP, FF), jnp.float32)
     narrow = pltpu.VMEM((CAP, FF), jnp.bfloat16)
     return pl.pallas_call(
-        functools.partial(ffn_kernel, plan_in, staged, plan_out),
+        functools.partial(ffn_kernel, plan_in, plan_out),
         out_shape=shapes,
         in_specs=[pl.BlockSpec(memory_space=pltpu.SMEM)]
-        + whole_specs(5)
-        + [pl.BlockSpec(memory_space=pltpu.HBM)] * len(arrays),
+        + whole_specs(5 + len(arrays)),
         out_specs=whole_specs(len(shapes)),
         scratch_shapes=[
             pltpu.VMEM((flat_rows, LANES), jnp.float32),
@@ -561,9 +544,8 @@
             narrow,
             narrow,
             narrow,
-            pltpu.SemaphoreType.DMA((len(arrays),)),
         ],
-        compiler_params=pltpu.CompilerParams(vmem_limit_bytes=44 << 20),
+        compiler_params=pltpu.CompilerParams(vmem_limit_bytes=(46 if len(arrays) > 1 else 58) << 20),
         cost_estimate=pl.CostEstimate(flops=0, bytes_accessed=0, transcendentals=0),
     )(device, mid, attn_out, cotangent, tables, gains, *arrays)
 
@@ -841,16 +823,8 @@
     )
     orders = bit_orders(devices, ("yxba", "ayxb", "xayb"))
     out_plan, block_shapes, ffn_parts = scatter_plan(ffn_rows, 0, orders, devices)
-    staged = [(0, 0, 0)]
-    if len(block_shapes) == 2:
-        staged = [
-            (part // 2, part % 2 * (devices // 4), low)
-            for low, _ in cut_rows(ffn_rows, 2)
-            for part in range(4)
-        ]
     block_out, delta_mid, delta_attn, late_gains, *found = run_ffn(
         ffn_plan,
-        staged,
         out_plan,
         block_shapes,
         here,

time: 164 us -> 167 us (1.018)
  transfers between devices with their start and end apart: 32 -> 32, of which waited for: 20 -> 20; matrix products, arithmetic and copies ran while one was open for 2% -> 2% of each run, Pallas kernels for 7% -> 6%
where the time goes in v4:
time: 167 us; the launch traced here: 166 us
  waiting for transfers between devices  85.9 us (51%)
  starting transfers between devices  38.6 us (23%)
  Pallas kernels  32.9 us (20%)
  other arithmetic  5.63 us (3%)
  local copies, waits for them, and re-layouts  2.21 us (1%)
    ppermute x32, waiting for transfers between devices, across(): lax.ppermute(block, 'dp', [(i, i ^ 1 << bit) for i in range(devices)])  85.9 us
    ppermute x32, starting transfers between devices, across(): lax.ppermute(block, 'dp', [(i, i ^ 1 << bit) for i in range(devices)])  38.6 us
    pallas_call x1, Pallas kernels, run_ffn(): pl.pallas_call(functools.partial(ffn_kernel, plan_in, plan_out), out_shap...  20.7 us
    pallas_call x1, Pallas kernels, back_attn(): pl.pallas_call(functools.partial(attn_back_kernel, plan, gain_len), out_s...  6.11 us
    pallas_call x1, Pallas kernels, forward_attn(): pl.pallas_call(functools.partial(attn_forward_kernel, plan, gain_len), ou...  4.61 us
  transfers between devices with their start and end apart: 32, of which 20 were waited for; matrix products, arithmetic and copies ran while one was open for 2% of the time, Pallas kernels for 6%

profile of v4, /device:TPU:0, one launch (start us, length us, event | category | flops | bytes accessed | tf_op | source)
XLA Modules:
  0.0 166.3 jit_solution(8035679325124943962)
XLA Ops:
  2.5 3.0 %collective-permute-start = (bf16[1,416,128]{2,1,0:T(8,128)(2,1)S(1)}, bf16[1,416,128]{2,1,0:T(8,128)(2,1)S(1)}, u32[]{:S(2)}, u32[]{:S(2)}) collective-permute-start(bf16[1,416,128]{2,1,0:T(8,128)(2,1)S(1)} %bitcast.26), channel_id=1, source_target_pairs={{0,8},{1,9},{2,10},{3,11},{4,12},{5,13},{6,14},{7,15},{8,0},{9,1},... | collective-permute-start | bytes 319496 | tf_op jit(solution)/shard_map/ppermute | solution.py:112
  5.5 2.7 %collective-permute-start.12 = (bf16[1,480,128]{2,1,0:T(8,128)(2,1)S(1)}, bf16[1,480,128]{2,1,0:T(8,128)(2,1)S(1)}, u32[]{:S(2)}, u32[]{:S(2)}) collective-permute-start(bf16[1,480,128]{2,1,0:T(8,128)(2,1)S(1)} %get-tuple-element.81), channel_id=1, source_target_pairs={{0,16},{1,17},{2,18},{3,19},{4,20},{5,21},{6,22},{7,23},{8,24},{9,... | collective-permute-start | bytes 368648 | tf_op jit(solution)/shard_map/ppermute | solution.py:112
  8.5 3.9 %collective-permute-start.1 = (bf16[2,416,128]{2,1,0:T(8,128)(2,1)S(1)}, bf16[2,416,128]{2,1,0:T(8,128)(2,1)S(1)}, u32[]{:S(2)}, u32[]{:S(2)}) collective-permute-start(bf16[2,416,128]{2,1,0:T(8,128)(2,1)S(1)} %pad_maximum_fusion.9), channel_id=1, source_target_pairs={{0,16},{1,17},{2,18},{3,19},{4,20},{5,21},{6,22},{7,23},{8,24},{9,... | collective-permute-start | bytes 638984 | tf_op jit(solution)/shard_map/ppermute | solution.py:112
  12.5 9.7 %collective-permute-done.12 = bf16[1,480,128]{2,1,0:T(8,128)(2,1)S(1)} collective-permute-done((bf16[1,480,128]{2,1,0:T(8,128)(2,1)S(1)}, bf16[1,480,128]{2,1,0:T(8,128)(2,1)S(1)}, u32[]{:S(2)}, u32[]{:S(2)}) %collective-permute-start.12) | collective-permute-done | bytes 122912 | tf_op jit(solution)/shard_map/ppermute | solution.py:112
  22.1 2.6 %collective-permute-done.6 = bf16[1,480,128]{2,1,0:T(8,128)(2,1)S(1)} collective-permute-done((bf16[1,480,128]{2,1,0:T(8,128)(2,1)S(1)}, bf16[1,480,128]{2,1,0:T(8,128)(2,1)S(1)}, u32[]{:S(2)}, u32[]{:S(2)}) %collective-permute-start.6) | collective-permute-done | bytes 122912 | tf_op jit(solution)/shard_map/ppermute | solution.py:112
  31.1 4.2 %collective-permute-done.7 = bf16[2,480,128]{2,1,0:T(8,128)(2,1)S(1)} collective-permute-done((bf16[2,480,128]{2,1,0:T(8,128)(2,1)S(1)}, bf16[2,480,128]{2,1,0:T(8,128)(2,1)S(1)}, u32[]{:S(2)}, u32[]{:S(2)}) %collective-permute-start.7) | collective-permute-done | bytes 245792 | tf_op jit(solution)/shard_map/ppermute | solution.py:112
  35.5 6.3 %collective-permute-done.2 = bf16[4,416,128]{2,1,0:T(8,128)(2,1)S(1)} collective-permute-done((bf16[4,416,128]{2,1,0:T(8,128)(2,1)S(1)}, bf16[4,416,128]{2,1,0:T(8,128)(2,1)S(1)}, u32[]{:S(2)}, u32[]{:S(2)}) %collective-permute-start.2) | collective-permute-done | bytes 426016 | tf_op jit(solution)/shard_map/ppermute | solution.py:112
  42.5 2.3 %collective-permute-done.14 = bf16[4,480,128]{2,1,0:T(8,128)(2,1)S(1)} collective-permute-done((bf16[4,480,128]{2,1,0:T(8,128)(2,1)S(1)}, bf16[4,480,128]{2,1,0:T(8,128)(2,1)S(1)}, u32[]{:S(2)}, u32[]{:S(2)}) %collective-permute-start.14) | collective-permute-done | bytes 491552 | tf_op jit(solution)/shard_map/ppermute | solution.py:112
  44.8 1.7 %collective-permute-done.8 = bf16[4,480,128]{2,1,0:T(8,128)(2,1)S(1)} collective-permute-done((bf16[4,480,128]{2,1,0:T(8,128)(2,1)S(1)}, bf16[4,480,128]{2,1,0:T(8,128)(2,1)S(1)}, u32[]{:S(2)}, u32[]{:S(2)}) %collective-permute-start.8) | collective-permute-done | bytes 491552 | tf_op jit(solution)/shard_map/ppermute | solution.py:112
  46.6 4.7 %collective-permute-start.9 = (bf16[8,480,128]{2,1,0:T(8,128)(2,1)S(1)}, bf16[8,480,128]{2,1,0:T(8,128)(2,1)}, u32[]{:S(2)}, u32[]{:S(2)}) collective-permute-start(bf16[8,480,128]{2,1,0:T(8,128)(2,1)S(1)} %pad_maximum_fusion.refs_0_), channel_id=1, source_target_pairs={{0,8},{1,9},{2,10},{3,11},{4,12},{5,13},{6,14},{7,15},{8,0},{9,1},... | collective-permute-start | bytes 2949128 | tf_op jit(solution)/shard_map/ppermute | solution.py:112
  53.0 9.7 %collective-permute-done.3.refs_1_ = bf16[8,416,128]{2,1,0:T(8,128)(2,1)} collective-permute-done((bf16[8,416,128]{2,1,0:T(8,128)(2,1)S(1)}, bf16[8,416,128]{2,1,0:T(8,128)(2,1)}, u32[]{:S(2)}, u32[]{:S(2)}) %collective-permute-start.3) | collective-permute-done | bytes 852000 | tf_op jit(solution)/shard_map/ppermute | solution.py:112
  66.8 4.6 %shard_map.118 = (bf16[640,1536]{1,0:T(8,128)(2,1)S(1)}, bf16[1024,640]{1,0:T(8,128)(2,1)S(1)}, f32[1,3072]{1,0:T(1,128)S(1)}, f32[128,640]{1,0:T(8,128)S(1)}, f32[128,640]{1,0:T(8,128)S(1)}) custom-call(s32[1]{0:T(128)} %bitcast.device_ref, bf16[128,640]{1,0:T(8,128)(2,1)S(1)} %copy-done.1, f32[128,512]{1,0:T(8,128)S(1)} %pad_maximum_fusion.6.tables, ...), custom_call_target="tpu_custom_call" | custom-call | bytes 67108864 | tf_op jit(solution)/shard_map/pallas_call | solution.py:427
  72.7 20.7 %shard_map.119 = (bf16[128,640]{1,0:T(8,128)(2,1)}, f32[128,640]{1,0:T(8,128)S(1)}, bf16[128,640]{1,0:T(8,128)(2,1)S(1)}, f32[3,640]{1,0:T(4,128)S(1)}, bf16[16,...) custom-call(s32[1]{0:T(128)} %bitcast.device_ref, f32[128,640]{1,0:T(8,128)S(1)} %get-tuple-element.34.mid_ref, ...), custom_call_target="tpu_custom_call" | custom-call | tf_op jit(solution)/shard_map/pallas_call | solution.py:531
  93.6 6.1 %shard_map.120 = (f32[128,640]{1,0:T(8,128)}, f32[1,3072]{1,0:T(1,128)}, bf16[16,416,128]{2,1,0:T(8,128)(2,1)S(1)}, bf16[16,416,128]{2,1,0:T(8,128)(2,1)S(1)}) custom-call(s32[1]{0:T(128)} %bitcast.device_ref, bf16[128,640]{1,0:T(8,128)(2,1)S(1)} %get-tuple-element.46.delta_attn, f32[128,640]{1,0:T(8,128)S(1)} %get-tuple-element.47.delta_mid, ...), custom_call_target="tpu_custom_call" | custom-call | tf_op jit(solution)/shard_map/pallas_call | solution.py:650
  100.0 3.4 %collective-permute-done.19.refs_3_ = bf16[16,416,128]{2,1,0:T(8,128)(2,1)S(1)} collective-permute-done((bf16[16,416,128]{2,1,0:T(8,128)(2,1)S(1)}, bf16[16,416,128]{2,1,0:T(8,128)(2,1)S(1)}, u32[]{:S(2)}, u32[]{:S(2)}) %collective-permute-start.19) | collective-permute-done | bytes 1703968 | tf_op jit(solution)/shard_map/ppermute | solution.py:112
  106.4 1.9 %collective-permute-start.24 = (bf16[8,464,128]{2,1,0:T(8,128)(2,1)S(1)}, bf16[8,464,128]{2,1,0:T(8,128)(2,1)S(1)}, u32[]{:S(2)}, u32[]{:S(2)}) collective-permute-start(bf16[8,464,128]{2,1,0:T(8,128)(2,1)S(1)} %get-tuple-element.59), channel_id=1, source_target_pairs={{0,8},{1,9},{2,10},{3,11},{4,12},{5,13},{6,14},{7,15},{8,0},{9,1},... | collective-permute-start | bytes 2850824 | tf_op jit(solution)/shard_map/ppermute | solution.py:112
  108.3 19.1 %collective-permute-done.28 = bf16[8,448,128]{2,1,0:T(8,128)(2,1)S(1)} collective-permute-done((bf16[8,448,128]{2,1,0:T(8,128)(2,1)S(1)}, bf16[8,448,128]{2,1,0:T(8,128)(2,1)S(1)}, u32[]{:S(2)}, u32[]{:S(2)}) %collective-permute-start.28) | collective-permute-done | bytes 917536 | tf_op jit(solution)/shard_map/ppermute | solution.py:112
  127.7 2.1 %collective-permute-start.29 = (bf16[4,448,128]{2,1,0:T(8,128)(2,1)S(1)}, bf16[4,448,128]{2,1,0:T(8,128)(2,1)S(1)}, u32[]{:S(2)}, u32[]{:S(2)}) collective-permute-start(bf16[4,448,128]{2,1,0:T(8,128)(2,1)S(1)} %get-tuple-element.74), channel_id=1, source_target_pairs={{0,8},{1,9},{2,10},{3,11},{4,12},{5,13},{6,14},{7,15},{8,0},{9,1},... | collective-permute-start | bytes 1376264 | tf_op jit(solution)/shard_map/ppermute | solution.py:112
  132.7 7.3 %collective-permute-done.29 = bf16[4,448,128]{2,1,0:T(8,128)(2,1)S(1)} collective-permute-done((bf16[4,448,128]{2,1,0:T(8,128)(2,1)S(1)}, bf16[4,448,128]{2,1,0:T(8,128)(2,1)S(1)}, u32[]{:S(2)}, u32[]{:S(2)}) %collective-permute-start.29) | collective-permute-done | bytes 458784 | tf_op jit(solution)/shard_map/ppermute | solution.py:112
  142.2 2.2 %collective-permute-start.22 = (bf16[2,464,128]{2,1,0:T(8,128)(2,1)S(1)}, bf16[2,464,128]{2,1,0:T(8,128)(2,1)S(1)}, u32[]{:S(2)}, u32[]{:S(2)}) collective-permute-start(bf16[2,464,128]{2,1,0:T(8,128)(2,1)S(1)} %get-tuple-element.76), channel_id=1, source_target_pairs={{0,16},{1,17},{2,18},{3,19},{4,20},{5,21},{6,22},{7,23},{8,24},{9,... | collective-permute-start | bytes 712712 | tf_op jit(solution)/shard_map/ppermute | solution.py:112
  145.7 2.8 %collective-permute-done.30 = bf16[2,448,128]{2,1,0:T(8,128)(2,1)S(1)} collective-permute-done((bf16[2,448,128]{2,1,0:T(8,128)(2,1)S(1)}, bf16[2,448,128]{2,1,0:T(8,128)(2,1)S(1)}, u32[]{:S(2)}, u32[]{:S(2)}) %collective-permute-start.30) | collective-permute-done | bytes 229408 | tf_op jit(solution)/shard_map/ppermute | solution.py:112
  149.9 8.0 %collective-permute-done.22 = bf16[2,464,128]{2,1,0:T(8,128)(2,1)S(1)} collective-permute-done((bf16[2,464,128]{2,1,0:T(8,128)(2,1)S(1)}, bf16[2,464,128]{2,1,0:T(8,128)(2,1)S(1)}, u32[]{:S(2)}, u32[]{:S(2)}) %collective-permute-start.22) | collective-permute-done | bytes 237600 | tf_op jit(solution)/shard_map/ppermute | solution.py:112
  158.1 2.7 %collective-permute-start.27 = (bf16[1,464,128]{2,1,0:T(8,128)(2,1)S(1)}, bf16[1,464,128]{2,1,0:T(8,128)(2,1)S(1)}, u32[]{:S(2)}, u32[]{:S(2)}) collective-permute-start(bf16[1,464,128]{2,1,0:T(8,128)(2,1)S(1)} %add_convert_fusion.12), channel_id=1, source_target_pairs={{0,16},{1,17},{2,18},{3,19},{4,20},{5,21},{6,22},{7,23},{8,24},{9,... | collective-permute-start | bytes 356360 | tf_op jit(solution)/shard_map/ppermute | solution.py:112
  160.8 3.5 %collective-permute-done.23 = bf16[1,464,128]{2,1,0:T(8,128)(2,1)S(1)} collective-permute-done((bf16[1,464,128]{2,1,0:T(8,128)(2,1)S(1)}, bf16[1,464,128]{2,1,0:T(8,128)(2,1)S(1)}, u32[]{:S(2)}, u32[]{:S(2)}) %collective-permute-start.23) | collective-permute-done | bytes 118816 | tf_op jit(solution)/shard_map/ppermute | solution.py:112
  (116 shorter events, 30.2 us)
Async XLA Ops:
  5.5 16.6 %collective-permute-start.12 = (bf16[1,480,128]{2,1,0:T(8,128)(2,1)S(1)}, bf16[1,480,128]{2,1,0:T(8,128)(2,1)S(1)}, u32[]{:S(2)}, u32[]{:S(2)}) collective-permute-start(bf16[1,480,128]{2,1,0:T(8,128)(2,1)S(1)} %get-tuple-element.81), channel_id=1, source_target_pairs={{0,16},{1,17},{2,18},{3,19},{4,20},{5,21},{6,22},{7,23},{8,24},{9,... | collective-permute-start | bytes 368648 | tf_op jit(solution)/shard_map/ppermute | solution.py:112
  8.2 16.6 %collective-permute-start.6 = (bf16[1,480,128]{2,1,0:T(8,128)(2,1)S(1)}, bf16[1,480,128]{2,1,0:T(8,128)(2,1)S(1)}, u32[]{:S(2)}, u32[]{:S(2)}) collective-permute-start(bf16[1,480,128]{2,1,0:T(8,128)(2,1)S(1)} %get-tuple-element.82), channel_id=1, source_target_pairs={{0,16},{1,17},{2,18},{3,19},{4,20},{5,21},{6,22},{7,23},{8,24},{9,... | collective-permute-start | bytes 368648 | tf_op jit(solution)/shard_map/ppermute | solution.py:112
  8.5 19.8 %collective-permute-start.1 = (bf16[2,416,128]{2,1,0:T(8,128)(2,1)S(1)}, bf16[2,416,128]{2,1,0:T(8,128)(2,1)S(1)}, u32[]{:S(2)}, u32[]{:S(2)}) collective-permute-start(bf16[2,416,128]{2,1,0:T(8,128)(2,1)S(1)} %pad_maximum_fusion.9), channel_id=1, source_target_pairs={{0,16},{1,17},{2,18},{3,19},{4,20},{5,21},{6,22},{7,23},{8,24},{9,... | collective-permute-start | bytes 638984 | tf_op jit(solution)/shard_map/ppermute | solution.py:112
  26.4 8.9 %collective-permute-start.7 = (bf16[2,480,128]{2,1,0:T(8,128)(2,1)S(1)}, bf16[2,480,128]{2,1,0:T(8,128)(2,1)S(1)}, u32[]{:S(2)}, u32[]{:S(2)}) collective-permute-start(bf16[2,480,128]{2,1,0:T(8,128)(2,1)S(1)} %pad_maximum_fusion.7), channel_id=1, source_target_pairs={{0,2},{1,3},{2,0},{3,1},{4,6},{5,7},{6,4},{7,5},{8,10},{9,11},{10,... | collective-permute-start | bytes 737288 | tf_op jit(solution)/shard_map/ppermute | solution.py:112
  28.3 13.5 %collective-permute-start.2 = (bf16[4,416,128]{2,1,0:T(8,128)(2,1)S(1)}, bf16[4,416,128]{2,1,0:T(8,128)(2,1)S(1)}, u32[]{:S(2)}, u32[]{:S(2)}) collective-permute-start(bf16[4,416,128]{2,1,0:T(8,128)(2,1)S(1)} %pad_maximum_fusion.5), channel_id=1, source_target_pairs={{0,2},{1,3},{2,0},{3,1},{4,6},{5,7},{6,4},{7,5},{8,10},{9,11},{10,... | collective-permute-start | bytes 1277960 | tf_op jit(solution)/shard_map/ppermute | solution.py:112
  35.3 9.5 %collective-permute-start.14 = (bf16[4,480,128]{2,1,0:T(8,128)(2,1)S(1)}, bf16[4,480,128]{2,1,0:T(8,128)(2,1)S(1)}, u32[]{:S(2)}, u32[]{:S(2)}) collective-permute-start(bf16[4,480,128]{2,1,0:T(8,128)(2,1)S(1)} %pad_maximum_fusion.4), channel_id=1, source_target_pairs={{0,8},{1,9},{2,10},{3,11},{4,12},{5,13},{6,14},{7,15},{8,0},{9,1},... | collective-permute-start | bytes 1474568 | tf_op jit(solution)/shard_map/ppermute | solution.py:112
  35.5 11.1 %collective-permute-start.8 = (bf16[4,480,128]{2,1,0:T(8,128)(2,1)S(1)}, bf16[4,480,128]{2,1,0:T(8,128)(2,1)S(1)}, u32[]{:S(2)}, u32[]{:S(2)}) collective-permute-start(bf16[4,480,128]{2,1,0:T(8,128)(2,1)S(1)} %pad_maximum_fusion.3), channel_id=1, source_target_pairs={{0,4},{1,5},{2,6},{3,7},{4,0},{5,1},{6,2},{7,3},{8,12},{9,13},{10,... | collective-permute-start | bytes 1474568 | tf_op jit(solution)/shard_map/ppermute | solution.py:112
  41.9 20.8 %collective-permute-start.3 = (bf16[8,416,128]{2,1,0:T(8,128)(2,1)S(1)}, bf16[8,416,128]{2,1,0:T(8,128)(2,1)}, u32[]{:S(2)}, u32[]{:S(2)}) collective-permute-start(bf16[8,416,128]{2,1,0:T(8,128)(2,1)S(1)} %pad_maximum_fusion.2.refs_0_), channel_id=1, source_target_pairs={{0,4},{1,5},{2,6},{3,7},{4,0},{5,1},{6,2},{7,3},{8,12},{9,13},{10,... | collective-permute-start | bytes 2555912 | tf_op jit(solution)/shard_map/ppermute | solution.py:112
  46.6 18.7 %collective-permute-start.9 = (bf16[8,480,128]{2,1,0:T(8,128)(2,1)S(1)}, bf16[8,480,128]{2,1,0:T(8,128)(2,1)}, u32[]{:S(2)}, u32[]{:S(2)}) collective-permute-start(bf16[8,480,128]{2,1,0:T(8,128)(2,1)S(1)} %pad_maximum_fusion.refs_0_), channel_id=1, source_target_pairs={{0,8},{1,9},{2,10},{3,11},{4,12},{5,13},{6,14},{7,15},{8,0},{9,1},... | collective-permute-start | bytes 2949128 | tf_op jit(solution)/shard_map/ppermute | solution.py:112
  51.5 14.3 %collective-permute-start.15 = (bf16[8,480,128]{2,1,0:T(8,128)(2,1)S(1)}, bf16[8,480,128]{2,1,0:T(8,128)(2,1)}, u32[]{:S(2)}, u32[]{:S(2)}) collective-permute-start(bf16[8,480,128]{2,1,0:T(8,128)(2,1)S(1)} %pad_maximum_fusion.1.refs_4_), channel_id=1, source_target_pairs={{0,2},{1,3},{2,0},{3,1},{4,6},{5,7},{6,4},{7,5},{8,10},{9,11},{10,... | collective-permute-start | bytes 2949128 | tf_op jit(solution)/shard_map/ppermute | solution.py:112
  53.0 10.6 %collective-permute-start.4 = (bf16[8,416,128]{2,1,0:T(8,128)(2,1)S(1)}, bf16[8,416,128]{2,1,0:T(8,128)(2,1)}, u32[]{:S(2)}, u32[]{:S(2)}) collective-permute-start(bf16[8,416,128]{2,1,0:T(8,128)(2,1)S(1)} %pad_maximum_fusion.2.refs_0_), channel_id=1, source_target_pairs={{0,1},{1,0},{2,3},{3,2},{4,5},{5,4},{6,7},{7,6},{8,9},{9,8},{10,11... | collective-permute-start | bytes 2555912 | tf_op jit(solution)/shard_map/ppermute | solution.py:112
  63.1 8.3 %collective-permute-start.10 = (bf16[8,480,128]{2,1,0:T(8,128)(2,1)S(1)}, bf16[8,480,128]{2,1,0:T(8,128)(2,1)S(1)}, u32[]{:S(2)}, u32[]{:S(2)}) collective-permute-start(bf16[8,480,128]{2,1,0:T(8,128)(2,1)S(1)} %pad_maximum_fusion.refs_0_), channel_id=1, source_target_pairs={{0,1},{1,0},{2,3},{3,2},{4,5},{5,4},{6,7},{7,6},{8,9},{9,8},{10,11... | collective-permute-start | bytes 2949128 | tf_op jit(solution)/shard_map/ppermute | solution.py:112
  63.6 7.8 %collective-permute-start.16 = (bf16[8,480,128]{2,1,0:T(8,128)(2,1)S(1)}, bf16[8,480,128]{2,1,0:T(8,128)(2,1)S(1)}, u32[]{:S(2)}, u32[]{:S(2)}) collective-permute-start(bf16[8,480,128]{2,1,0:T(8,128)(2,1)S(1)} %pad_maximum_fusion.1.refs_4_), channel_id=1, source_target_pairs={{0,1},{1,0},{2,3},{3,2},{4,5},{5,4},{6,7},{7,6},{8,9},{9,8},{10,11... | collective-permute-start | bytes 2949128 | tf_op jit(solution)/shard_map/ppermute | solution.py:112
  93.3 10.0 %collective-permute-start.18 = (bf16[16,960,128]{2,1,0:T(8,128)(2,1)}, bf16[16,960,128]{2,1,0:T(8,128)(2,1)S(1)}, u32[]{:S(2)}, u32[]{:S(2)}) collective-permute-start(bf16[16,960,128]{2,1,0:T(8,128)(2,1)} %get-tuple-element.53), channel_id=1, source_target_pairs={{0,1},{1,0},{2,3},{3,2},{4,5},{5,4},{6,7},{7,6},{8,9},{9,8},{10,11... | collective-permute-start | bytes 11796488 | tf_op jit(solution)/shard_map/ppermute | solution.py:112
  104.9 22.6 %collective-permute-start.28 = (bf16[8,448,128]{2,1,0:T(8,128)(2,1)S(1)}, bf16[8,448,128]{2,1,0:T(8,128)(2,1)S(1)}, u32[]{:S(2)}, u32[]{:S(2)}) collective-permute-start(bf16[8,448,128]{2,1,0:T(8,128)(2,1)S(1)} %get-tuple-element.61), channel_id=1, source_target_pairs={{0,2},{1,3},{2,0},{3,1},{4,6},{5,7},{6,4},{7,5},{8,10},{9,11},{10,... | collective-permute-start | bytes 2752520 | tf_op jit(solution)/shard_map/ppermute | solution.py:112
  106.4 23.3 %collective-permute-start.20 = (bf16[8,464,128]{2,1,0:T(8,128)(2,1)S(1)}, bf16[8,464,128]{2,1,0:T(8,128)(2,1)S(1)}, u32[]{:S(2)}, u32[]{:S(2)}) collective-permute-start(bf16[8,464,128]{2,1,0:T(8,128)(2,1)S(1)} %get-tuple-element.57), channel_id=1, source_target_pairs={{0,4},{1,5},{2,6},{3,7},{4,0},{5,1},{6,2},{7,3},{8,12},{9,13},{10,... | collective-permute-start | bytes 2850824 | tf_op jit(solution)/shard_map/ppermute | solution.py:112
  106.4 25.1 %collective-permute-start.24 = (bf16[8,464,128]{2,1,0:T(8,128)(2,1)S(1)}, bf16[8,464,128]{2,1,0:T(8,128)(2,1)S(1)}, u32[]{:S(2)}, u32[]{:S(2)}) collective-permute-start(bf16[8,464,128]{2,1,0:T(8,128)(2,1)S(1)} %get-tuple-element.59), channel_id=1, source_target_pairs={{0,8},{1,9},{2,10},{3,11},{4,12},{5,13},{6,14},{7,15},{8,0},{9,1},... | collective-permute-start | bytes 2850824 | tf_op jit(solution)/shard_map/ppermute | solution.py:112
  127.7 12.3 %collective-permute-start.29 = (bf16[4,448,128]{2,1,0:T(8,128)(2,1)S(1)}, bf16[4,448,128]{2,1,0:T(8,128)(2,1)S(1)}, u32[]{:S(2)}, u32[]{:S(2)}) collective-permute-start(bf16[4,448,128]{2,1,0:T(8,128)(2,1)S(1)} %get-tuple-element.74), channel_id=1, source_target_pairs={{0,8},{1,9},{2,10},{3,11},{4,12},{5,13},{6,14},{7,15},{8,0},{9,1},... | collective-permute-start | bytes 1376264 | tf_op jit(solution)/shard_map/ppermute | solution.py:112
  130.0 12.1 %collective-permute-start.21 = (bf16[4,464,128]{2,1,0:T(8,128)(2,1)S(1)}, bf16[4,464,128]{2,1,0:T(8,128)(2,1)S(1)}, u32[]{:S(2)}, u32[]{:S(2)}) collective-permute-start(bf16[4,464,128]{2,1,0:T(8,128)(2,1)S(1)} %get-tuple-element.70), channel_id=1, source_target_pairs={{0,2},{1,3},{2,0},{3,1},{4,6},{5,7},{6,4},{7,5},{8,10},{9,11},{10,... | collective-permute-start | bytes 1425416 | tf_op jit(solution)/shard_map/ppermute | solution.py:112
  131.8 13.7 %collective-permute-start.25 = (bf16[4,464,128]{2,1,0:T(8,128)(2,1)S(1)}, bf16[4,464,128]{2,1,0:T(8,128)(2,1)S(1)}, u32[]{:S(2)}, u32[]{:S(2)}) collective-permute-start(bf16[4,464,128]{2,1,0:T(8,128)(2,1)S(1)} %get-tuple-element.72), channel_id=1, source_target_pairs={{0,4},{1,5},{2,6},{3,7},{4,0},{5,1},{6,2},{7,3},{8,12},{9,13},{10,... | collective-permute-start | bytes 1425416 | tf_op jit(solution)/shard_map/ppermute | solution.py:112
  140.1 8.4 %collective-permute-start.30 = (bf16[2,448,128]{2,1,0:T(8,128)(2,1)S(1)}, bf16[2,448,128]{2,1,0:T(8,128)(2,1)S(1)}, u32[]{:S(2)}, u32[]{:S(2)}) collective-permute-start(bf16[2,448,128]{2,1,0:T(8,128)(2,1)S(1)} %get-tuple-element.80), channel_id=1, source_target_pairs={{0,4},{1,5},{2,6},{3,7},{4,0},{5,1},{6,2},{7,3},{8,12},{9,13},{10,... | collective-permute-start | bytes 688136 | tf_op jit(solution)/shard_map/ppermute | solution.py:112
  142.2 15.7 %collective-permute-start.22 = (bf16[2,464,128]{2,1,0:T(8,128)(2,1)S(1)}, bf16[2,464,128]{2,1,0:T(8,128)(2,1)S(1)}, u32[]{:S(2)}, u32[]{:S(2)}) collective-permute-start(bf16[2,464,128]{2,1,0:T(8,128)(2,1)S(1)} %get-tuple-element.76), channel_id=1, source_target_pairs={{0,16},{1,17},{2,18},{3,19},{4,20},{5,21},{6,22},{7,23},{8,24},{9,... | collective-permute-start | bytes 712712 | tf_op jit(solution)/shard_map/ppermute | solution.py:112
  145.6 12.4 %collective-permute-start.26 = (bf16[2,464,128]{2,1,0:T(8,128)(2,1)S(1)}, bf16[2,464,128]{2,1,0:T(8,128)(2,1)S(1)}, u32[]{:S(2)}, u32[]{:S(2)}) collective-permute-start(bf16[2,464,128]{2,1,0:T(8,128)(2,1)S(1)} %get-tuple-element.78), channel_id=1, source_target_pairs={{0,2},{1,3},{2,0},{3,1},{4,6},{5,7},{6,4},{7,5},{8,10},{9,11},{10,... | collective-permute-start | bytes 712712 | tf_op jit(solution)/shard_map/ppermute | solution.py:112
  148.6 12.2 %collective-permute-start.31 = (bf16[1,448,128]{2,1,0:T(8,128)(2,1)S(1)}, bf16[1,448,128]{2,1,0:T(8,128)(2,1)S(1)}, u32[]{:S(2)}, u32[]{:S(2)}) collective-permute-start(bf16[1,448,128]{2,1,0:T(8,128)(2,1)S(1)} %add_convert_fusion.16), channel_id=1, source_target_pairs={{0,16},{1,17},{2,18},{3,19},{4,20},{5,21},{6,22},{7,23},{8,24},{9,... | collective-permute-start | bytes 344072 | tf_op jit(solution)/shard_map/ppermute | solution.py:112
  (19 other events, 148.7 us)

commit v5 on v2

--- a/solution.py
+++ b/solution.py
@@ -710,6 +710,9 @@
 
 def scatter_plan(each, tail_rows, orders, devices):
     parts = cut_rows(each + tail_rows, len(orders))
+    if not tail_rows and each % (3 * ROWS) == 0:
+        first = each // 3 - 3 * ROWS
+        parts = [(0, first), (first, 2 * each // 3 - 2 * ROWS), (2 * each // 3 - 2 * ROWS, each)]
     half = devices // 2
     if each % ROWS:
         return [(0, [], 0, 0, devices * each, 0, 0)], [(1, devices * each, LANES)], parts

time: 164 us -> 168 us (1.024)
  waiting for transfers between devices: 85.9 us -> 89.5 us
    ppermute x32, waiting for transfers between devices: 85.9 us -> 89.5 us  [across(): lax.ppermute(block, 'dp', [(i, i ^ 1 << bit) for i in range(devices)])]
  transfers between devices with their start and end apart: 32 -> 32, of which waited for: 20 -> 23; matrix products, arithmetic and copies ran while one was open for 2% -> 2% of each run, Pallas kernels for 7% -> 6%
where the time goes in v5:
time: 168 us
  waiting for transfers between devices  89.5 us (53%)
  starting transfers between devices  38.8 us (23%)
  Pallas kernels  31.6 us (19%)
  other arithmetic  5.7 us (3%)
    ppermute x32, waiting for transfers between devices, across(): lax.ppermute(block, 'dp', [(i, i ^ 1 << bit) for i in range(devices)])  89.5 us
    ppermute x32, starting transfers between devices, across(): lax.ppermute(block, 'dp', [(i, i ^ 1 << bit) for i in range(devices)])  38.8 us
    pallas_call x1, Pallas kernels, run_ffn(): pl.pallas_call(functools.partial(ffn_kernel, plan_in, staged, plan_out),...  19.4 us
    pallas_call x1, Pallas kernels, back_attn(): pl.pallas_call(functools.partial(attn_back_kernel, plan, gain_len), out_s...  6.12 us
    pallas_call x1, Pallas kernels, forward_attn(): pl.pallas_call(functools.partial(attn_forward_kernel, plan, gain_len), ou...  4.61 us
  transfers between devices with their start and end apart: 32, of which 23 were waited for; matrix products, arithmetic and copies ran while one was open for 2% of the time, Pallas kernels for 6%

profile of v5, /device:TPU:0, one launch (start us, length us, event | category | flops | bytes accessed | tf_op | source)
XLA Modules:
  0.0 167.8 jit_solution(13519670266735448713)
XLA Ops:
  2.5 3.0 %collective-permute-start = (bf16[1,416,128]{2,1,0:T(8,128)(2,1)S(1)}, bf16[1,416,128]{2,1,0:T(8,128)(2,1)S(1)}, u32[]{:S(2)}, u32[]{:S(2)}) collective-permute-start(bf16[1,416,128]{2,1,0:T(8,128)(2,1)S(1)} %bitcast.26), channel_id=1, source_target_pairs={{0,8},{1,9},{2,10},{3,11},{4,12},{5,13},{6,14},{7,15},{8,0},{9,1},... | collective-permute-start | bytes 319496 | tf_op jit(solution)/shard_map/ppermute | solution.py:112
  5.5 2.7 %collective-permute-start.12 = (bf16[1,480,128]{2,1,0:T(8,128)(2,1)S(1)}, bf16[1,480,128]{2,1,0:T(8,128)(2,1)S(1)}, u32[]{:S(2)}, u32[]{:S(2)}) collective-permute-start(bf16[1,480,128]{2,1,0:T(8,128)(2,1)S(1)} %get-tuple-element.81), channel_id=1, source_target_pairs={{0,16},{1,17},{2,18},{3,19},{4,20},{5,21},{6,22},{7,23},{8,24},{9,... | collective-permute-start | bytes 368648 | tf_op jit(solution)/shard_map/ppermute | solution.py:112
  8.5 3.9 %collective-permute-start.1 = (bf16[2,416,128]{2,1,0:T(8,128)(2,1)S(1)}, bf16[2,416,128]{2,1,0:T(8,128)(2,1)S(1)}, u32[]{:S(2)}, u32[]{:S(2)}) collective-permute-start(bf16[2,416,128]{2,1,0:T(8,128)(2,1)S(1)} %pad_maximum_fusion.9), channel_id=1, source_target_pairs={{0,16},{1,17},{2,18},{3,19},{4,20},{5,21},{6,22},{7,23},{8,24},{9,... | collective-permute-start | bytes 638984 | tf_op jit(solution)/shard_map/ppermute | solution.py:112
  12.5 9.7 %collective-permute-done.12 = bf16[1,480,128]{2,1,0:T(8,128)(2,1)S(1)} collective-permute-done((bf16[1,480,128]{2,1,0:T(8,128)(2,1)S(1)}, bf16[1,480,128]{2,1,0:T(8,128)(2,1)S(1)}, u32[]{:S(2)}, u32[]{:S(2)}) %collective-permute-start.12) | collective-permute-done | bytes 122912 | tf_op jit(solution)/shard_map/ppermute | solution.py:112
  22.1 2.6 %collective-permute-done.6 = bf16[1,480,128]{2,1,0:T(8,128)(2,1)S(1)} collective-permute-done((bf16[1,480,128]{2,1,0:T(8,128)(2,1)S(1)}, bf16[1,480,128]{2,1,0:T(8,128)(2,1)S(1)}, u32[]{:S(2)}, u32[]{:S(2)}) %collective-permute-start.6) | collective-permute-done | bytes 122912 | tf_op jit(solution)/shard_map/ppermute | solution.py:112
  31.1 4.2 %collective-permute-done.7 = bf16[2,480,128]{2,1,0:T(8,128)(2,1)S(1)} collective-permute-done((bf16[2,480,128]{2,1,0:T(8,128)(2,1)S(1)}, bf16[2,480,128]{2,1,0:T(8,128)(2,1)S(1)}, u32[]{:S(2)}, u32[]{:S(2)}) %collective-permute-start.7) | collective-permute-done | bytes 245792 | tf_op jit(solution)/shard_map/ppermute | solution.py:112
  35.5 6.3 %collective-permute-done.2 = bf16[4,416,128]{2,1,0:T(8,128)(2,1)S(1)} collective-permute-done((bf16[4,416,128]{2,1,0:T(8,128)(2,1)S(1)}, bf16[4,416,128]{2,1,0:T(8,128)(2,1)S(1)}, u32[]{:S(2)}, u32[]{:S(2)}) %collective-permute-start.2) | collective-permute-done | bytes 426016 | tf_op jit(solution)/shard_map/ppermute | solution.py:112
  42.5 2.3 %collective-permute-done.14 = bf16[4,480,128]{2,1,0:T(8,128)(2,1)S(1)} collective-permute-done((bf16[4,480,128]{2,1,0:T(8,128)(2,1)S(1)}, bf16[4,480,128]{2,1,0:T(8,128)(2,1)S(1)}, u32[]{:S(2)}, u32[]{:S(2)}) %collective-permute-start.14) | collective-permute-done | bytes 491552 | tf_op jit(solution)/shard_map/ppermute | solution.py:112
  44.8 1.7 %collective-permute-done.8 = bf16[4,480,128]{2,1,0:T(8,128)(2,1)S(1)} collective-permute-done((bf16[4,480,128]{2,1,0:T(8,128)(2,1)S(1)}, bf16[4,480,128]{2,1,0:T(8,128)(2,1)S(1)}, u32[]{:S(2)}, u32[]{:S(2)}) %collective-permute-start.8) | collective-permute-done | bytes 491552 | tf_op jit(solution)/shard_map/ppermute | solution.py:112
  46.6 4.7 %collective-permute-start.9 = (bf16[8,480,128]{2,1,0:T(8,128)(2,1)S(1)}, bf16[8,480,128]{2,1,0:T(8,128)(2,1)}, u32[]{:S(2)}, u32[]{:S(2)}) collective-permute-start(bf16[8,480,128]{2,1,0:T(8,128)(2,1)S(1)} %pad_maximum_fusion.refs_0_), channel_id=1, source_target_pairs={{0,8},{1,9},{2,10},{3,11},{4,12},{5,13},{6,14},{7,15},{8,0},{9,1},... | collective-permute-start | bytes 2949128 | tf_op jit(solution)/shard_map/ppermute | solution.py:112
  53.0 9.7 %collective-permute-done.3.refs_1_ = bf16[8,416,128]{2,1,0:T(8,128)(2,1)} collective-permute-done((bf16[8,416,128]{2,1,0:T(8,128)(2,1)S(1)}, bf16[8,416,128]{2,1,0:T(8,128)(2,1)}, u32[]{:S(2)}, u32[]{:S(2)}) %collective-permute-start.3) | collective-permute-done | bytes 852000 | tf_op jit(solution)/shard_map/ppermute | solution.py:112
  66.8 4.6 %shard_map.118 = (bf16[640,1536]{1,0:T(8,128)(2,1)S(1)}, bf16[1024,640]{1,0:T(8,128)(2,1)S(1)}, f32[1,3072]{1,0:T(1,128)S(1)}, f32[128,640]{1,0:T(8,128)S(1)}, f32[128,640]{1,0:T(8,128)S(1)}) custom-call(s32[1]{0:T(128)} %bitcast.device_ref, bf16[128,640]{1,0:T(8,128)(2,1)S(1)} %copy-done.1, f32[128,512]{1,0:T(8,128)S(1)} %pad_maximum_fusion.6.tables, ...), custom_call_target="tpu_custom_call" | custom-call | bytes 67108864 | tf_op jit(solution)/shard_map/pallas_call | solution.py:427
  71.4 19.4 %shard_map.119 = (bf16[128,640]{1,0:T(8,128)(2,1)}, f32[128,640]{1,0:T(8,128)S(1)}, bf16[128,640]{1,0:T(8,128)(2,1)S(1)}, f32[3,640]{1,0:T(4,128)S(1)}, bf16[16,...) custom-call(s32[1]{0:T(128)} %bitcast.device_ref, f32[128,640]{1,0:T(8,128)S(1)} %get-tuple-element.34.mid_ref, ...), custom_call_target="tpu_custom_call" | custom-call | tf_op jit(solution)/shard_map/pallas_call | solution.py:547
  91.2 6.1 %shard_map.120 = (f32[128,640]{1,0:T(8,128)}, f32[1,3072]{1,0:T(1,128)}, bf16[16,416,128]{2,1,0:T(8,128)(2,1)S(1)}, bf16[16,416,128]{2,1,0:T(8,128)(2,1)S(1)}) custom-call(s32[1]{0:T(128)} %bitcast.device_ref, bf16[128,640]{1,0:T(8,128)(2,1)S(1)} %get-tuple-element.46.delta_attn, f32[128,640]{1,0:T(8,128)S(1)} %get-tuple-element.47.delta_mid, ...), custom_call_target="tpu_custom_call" | custom-call | tf_op jit(solution)/shard_map/pallas_call | solution.py:668
  97.5 3.4 %collective-permute-done.19.refs_3_ = bf16[16,416,128]{2,1,0:T(8,128)(2,1)S(1)} collective-permute-done((bf16[16,416,128]{2,1,0:T(8,128)(2,1)S(1)}, bf16[16,416,128]{2,1,0:T(8,128)(2,1)S(1)}, u32[]{:S(2)}, u32[]{:S(2)}) %collective-permute-start.19) | collective-permute-done | bytes 1703968 | tf_op jit(solution)/shard_map/ppermute | solution.py:112
  102.5 2.0 %collective-permute-start.24 = (bf16[8,480,128]{2,1,0:T(8,128)(2,1)S(1)}, bf16[8,480,128]{2,1,0:T(8,128)(2,1)S(1)}, u32[]{:S(2)}, u32[]{:S(2)}) collective-permute-start(bf16[8,480,128]{2,1,0:T(8,128)(2,1)S(1)} %get-tuple-element.59), channel_id=1, source_target_pairs={{0,8},{1,9},{2,10},{3,11},{4,12},{5,13},{6,14},{7,15},{8,0},{9,1},... | collective-permute-start | bytes 2949128 | tf_op jit(solution)/shard_map/ppermute | solution.py:112
  105.9 17.6 %collective-permute-done.20 = bf16[8,416,128]{2,1,0:T(8,128)(2,1)S(1)} collective-permute-done((bf16[8,416,128]{2,1,0:T(8,128)(2,1)S(1)}, bf16[8,416,128]{2,1,0:T(8,128)(2,1)S(1)}, u32[]{:S(2)}, u32[]{:S(2)}) %collective-permute-start.20) | collective-permute-done | bytes 852000 | tf_op jit(solution)/shard_map/ppermute | solution.py:112
  127.0 1.7 %collective-permute-start.25 = (bf16[4,480,128]{2,1,0:T(8,128)(2,1)S(1)}, bf16[4,480,128]{2,1,0:T(8,128)(2,1)S(1)}, u32[]{:S(2)}, u32[]{:S(2)}) collective-permute-start(bf16[4,480,128]{2,1,0:T(8,128)(2,1)S(1)} %get-tuple-element.70), channel_id=1, source_target_pairs={{0,4},{1,5},{2,6},{3,7},{4,0},{5,1},{6,2},{7,3},{8,12},{9,13},{10,... | collective-permute-start | bytes 1474568 | tf_op jit(solution)/shard_map/ppermute | solution.py:112
  130.8 6.5 %collective-permute-done.21 = bf16[4,416,128]{2,1,0:T(8,128)(2,1)S(1)} collective-permute-done((bf16[4,416,128]{2,1,0:T(8,128)(2,1)S(1)}, bf16[4,416,128]{2,1,0:T(8,128)(2,1)S(1)}, u32[]{:S(2)}, u32[]{:S(2)}) %collective-permute-start.21) | collective-permute-done | bytes 426016 | tf_op jit(solution)/shard_map/ppermute | solution.py:112
  141.6 7.7 %collective-permute-done.22 = bf16[2,416,128]{2,1,0:T(8,128)(2,1)S(1)} collective-permute-done((bf16[2,416,128]{2,1,0:T(8,128)(2,1)S(1)}, bf16[2,416,128]{2,1,0:T(8,128)(2,1)S(1)}, u32[]{:S(2)}, u32[]{:S(2)}) %collective-permute-start.22) | collective-permute-done | bytes 213024 | tf_op jit(solution)/shard_map/ppermute | solution.py:112
  151.0 3.1 %collective-permute-done.23 = bf16[1,416,128]{2,1,0:T(8,128)(2,1)S(1)} collective-permute-done((bf16[1,416,128]{2,1,0:T(8,128)(2,1)S(1)}, bf16[1,416,128]{2,1,0:T(8,128)(2,1)S(1)}, u32[]{:S(2)}, u32[]{:S(2)}) %collective-permute-start.23) | collective-permute-done | bytes 106528 | tf_op jit(solution)/shard_map/ppermute | solution.py:112
  156.5 2.2 %collective-permute-start.31 = (bf16[1,480,128]{2,1,0:T(8,128)(2,1)S(1)}, bf16[1,480,128]{2,1,0:T(8,128)(2,1)S(1)}, u32[]{:S(2)}, u32[]{:S(2)}) collective-permute-start(bf16[1,480,128]{2,1,0:T(8,128)(2,1)S(1)} %add_convert_fusion.12), channel_id=1, source_target_pairs={{0,16},{1,17},{2,18},{3,19},{4,20},{5,21},{6,22},{7,23},{8,24},{9,... | collective-permute-start | bytes 368648 | tf_op jit(solution)/shard_map/ppermute | solution.py:112
  158.7 5.9 %collective-permute-done.27 = bf16[1,480,128]{2,1,0:T(8,128)(2,1)S(1)} collective-permute-done((bf16[1,480,128]{2,1,0:T(8,128)(2,1)S(1)}, bf16[1,480,128]{2,1,0:T(8,128)(2,1)S(1)}, u32[]{:S(2)}, u32[]{:S(2)}) %collective-permute-start.27) | collective-permute-done | bytes 122912 | tf_op jit(solution)/shard_map/ppermute | solution.py:112
  166.1 1.7 %multiply_subtract_fusion = (f32[174176]{0:T(1024)}, f32[174176]{0:T(1024)}, f32[174176]{0:T(1024)}) fusion(f32[174176]{0:T(1024)S(1)} %copy-done.3, f32[174176]{0:T(1024)S(1)} %constant_dynamic-update-slice_fusion, f32[174176]{0:T(1024)S(1)} %copy-done.5, f32[174176]{0:T(1024)S(1)} %copy-done.6), kind=kLoop, calls=%fused_computation.11 | loop fusion | flops 2612640 | bytes 4876928 | tf_op jit(solution)/shard_map/sub | solution.py:797
  (112 shorter events, 33.9 us)
Async XLA Ops:
  5.5 16.6 %collective-permute-start.12 = (bf16[1,480,128]{2,1,0:T(8,128)(2,1)S(1)}, bf16[1,480,128]{2,1,0:T(8,128)(2,1)S(1)}, u32[]{:S(2)}, u32[]{:S(2)}) collective-permute-start(bf16[1,480,128]{2,1,0:T(8,128)(2,1)S(1)} %get-tuple-element.81), channel_id=1, source_target_pairs={{0,16},{1,17},{2,18},{3,19},{4,20},{5,21},{6,22},{7,23},{8,24},{9,... | collective-permute-start | bytes 368648 | tf_op jit(solution)/shard_map/ppermute | solution.py:112
  8.2 16.6 %collective-permute-start.6 = (bf16[1,480,128]{2,1,0:T(8,128)(2,1)S(1)}, bf16[1,480,128]{2,1,0:T(8,128)(2,1)S(1)}, u32[]{:S(2)}, u32[]{:S(2)}) collective-permute-start(bf16[1,480,128]{2,1,0:T(8,128)(2,1)S(1)} %get-tuple-element.82), channel_id=1, source_target_pairs={{0,16},{1,17},{2,18},{3,19},{4,20},{5,21},{6,22},{7,23},{8,24},{9,... | collective-permute-start | bytes 368648 | tf_op jit(solution)/shard_map/ppermute | solution.py:112
  8.5 19.8 %collective-permute-start.1 = (bf16[2,416,128]{2,1,0:T(8,128)(2,1)S(1)}, bf16[2,416,128]{2,1,0:T(8,128)(2,1)S(1)}, u32[]{:S(2)}, u32[]{:S(2)}) collective-permute-start(bf16[2,416,128]{2,1,0:T(8,128)(2,1)S(1)} %pad_maximum_fusion.9), channel_id=1, source_target_pairs={{0,16},{1,17},{2,18},{3,19},{4,20},{5,21},{6,22},{7,23},{8,24},{9,... | collective-permute-start | bytes 638984 | tf_op jit(solution)/shard_map/ppermute | solution.py:112
  26.4 8.9 %collective-permute-start.7 = (bf16[2,480,128]{2,1,0:T(8,128)(2,1)S(1)}, bf16[2,480,128]{2,1,0:T(8,128)(2,1)S(1)}, u32[]{:S(2)}, u32[]{:S(2)}) collective-permute-start(bf16[2,480,128]{2,1,0:T(8,128)(2,1)S(1)} %pad_maximum_fusion.7), channel_id=1, source_target_pairs={{0,2},{1,3},{2,0},{3,1},{4,6},{5,7},{6,4},{7,5},{8,10},{9,11},{10,... | collective-permute-start | bytes 737288 | tf_op jit(solution)/shard_map/ppermute | solution.py:112
  28.3 13.5 %collective-permute-start.2 = (bf16[4,416,128]{2,1,0:T(8,128)(2,1)S(1)}, bf16[4,416,128]{2,1,0:T(8,128)(2,1)S(1)}, u32[]{:S(2)}, u32[]{:S(2)}) collective-permute-start(bf16[4,416,128]{2,1,0:T(8,128)(2,1)S(1)} %pad_maximum_fusion.5), channel_id=1, source_target_pairs={{0,2},{1,3},{2,0},{3,1},{4,6},{5,7},{6,4},{7,5},{8,10},{9,11},{10,... | collective-permute-start | bytes 1277960 | tf_op jit(solution)/shard_map/ppermute | solution.py:112
  35.3 9.5 %collective-permute-start.14 = (bf16[4,480,128]{2,1,0:T(8,128)(2,1)S(1)}, bf16[4,480,128]{2,1,0:T(8,128)(2,1)S(1)}, u32[]{:S(2)}, u32[]{:S(2)}) collective-permute-start(bf16[4,480,128]{2,1,0:T(8,128)(2,1)S(1)} %pad_maximum_fusion.4), channel_id=1, source_target_pairs={{0,8},{1,9},{2,10},{3,11},{4,12},{5,13},{6,14},{7,15},{8,0},{9,1},... | collective-permute-start | bytes 1474568 | tf_op jit(solution)/shard_map/ppermute | solution.py:112
  35.5 11.1 %collective-permute-start.8 = (bf16[4,480,128]{2,1,0:T(8,128)(2,1)S(1)}, bf16[4,480,128]{2,1,0:T(8,128)(2,1)S(1)}, u32[]{:S(2)}, u32[]{:S(2)}) collective-permute-start(bf16[4,480,128]{2,1,0:T(8,128)(2,1)S(1)} %pad_maximum_fusion.3), channel_id=1, source_target_pairs={{0,4},{1,5},{2,6},{3,7},{4,0},{5,1},{6,2},{7,3},{8,12},{9,13},{10,... | collective-permute-start | bytes 1474568 | tf_op jit(solution)/shard_map/ppermute | solution.py:112
  41.9 20.8 %collective-permute-start.3 = (bf16[8,416,128]{2,1,0:T(8,128)(2,1)S(1)}, bf16[8,416,128]{2,1,0:T(8,128)(2,1)}, u32[]{:S(2)}, u32[]{:S(2)}) collective-permute-start(bf16[8,416,128]{2,1,0:T(8,128)(2,1)S(1)} %pad_maximum_fusion.2.refs_0_), channel_id=1, source_target_pairs={{0,4},{1,5},{2,6},{3,7},{4,0},{5,1},{6,2},{7,3},{8,12},{9,13},{10,... | collective-permute-start | bytes 2555912 | tf_op jit(solution)/shard_map/ppermute | solution.py:112
  46.6 18.7 %collective-permute-start.9 = (bf16[8,480,128]{2,1,0:T(8,128)(2,1)S(1)}, bf16[8,480,128]{2,1,0:T(8,128)(2,1)}, u32[]{:S(2)}, u32[]{:S(2)}) collective-permute-start(bf16[8,480,128]{2,1,0:T(8,128)(2,1)S(1)} %pad_maximum_fusion.refs_0_), channel_id=1, source_target_pairs={{0,8},{1,9},{2,10},{3,11},{4,12},{5,13},{6,14},{7,15},{8,0},{9,1},... | collective-permute-start | bytes 2949128 | tf_op jit(solution)/shard_map/ppermute | solution.py:112
  51.5 14.3 %collective-permute-start.15 = (bf16[8,480,128]{2,1,0:T(8,128)(2,1)S(1)}, bf16[8,480,128]{2,1,0:T(8,128)(2,1)}, u32[]{:S(2)}, u32[]{:S(2)}) collective-permute-start(bf16[8,480,128]{2,1,0:T(8,128)(2,1)S(1)} %pad_maximum_fusion.1.refs_4_), channel_id=1, source_target_pairs={{0,2},{1,3},{2,0},{3,1},{4,6},{5,7},{6,4},{7,5},{8,10},{9,11},{10,... | collective-permute-start | bytes 2949128 | tf_op jit(solution)/shard_map/ppermute | solution.py:112
  53.0 10.6 %collective-permute-start.4 = (bf16[8,416,128]{2,1,0:T(8,128)(2,1)S(1)}, bf16[8,416,128]{2,1,0:T(8,128)(2,1)}, u32[]{:S(2)}, u32[]{:S(2)}) collective-permute-start(bf16[8,416,128]{2,1,0:T(8,128)(2,1)S(1)} %pad_maximum_fusion.2.refs_0_), channel_id=1, source_target_pairs={{0,1},{1,0},{2,3},{3,2},{4,5},{5,4},{6,7},{7,6},{8,9},{9,8},{10,11... | collective-permute-start | bytes 2555912 | tf_op jit(solution)/shard_map/ppermute | solution.py:112
  63.1 8.3 %collective-permute-start.10 = (bf16[8,480,128]{2,1,0:T(8,128)(2,1)S(1)}, bf16[8,480,128]{2,1,0:T(8,128)(2,1)S(1)}, u32[]{:S(2)}, u32[]{:S(2)}) collective-permute-start(bf16[8,480,128]{2,1,0:T(8,128)(2,1)S(1)} %pad_maximum_fusion.refs_0_), channel_id=1, source_target_pairs={{0,1},{1,0},{2,3},{3,2},{4,5},{5,4},{6,7},{7,6},{8,9},{9,8},{10,11... | collective-permute-start | bytes 2949128 | tf_op jit(solution)/shard_map/ppermute | solution.py:112
  63.6 7.8 %collective-permute-start.16 = (bf16[8,480,128]{2,1,0:T(8,128)(2,1)S(1)}, bf16[8,480,128]{2,1,0:T(8,128)(2,1)S(1)}, u32[]{:S(2)}, u32[]{:S(2)}) collective-permute-start(bf16[8,480,128]{2,1,0:T(8,128)(2,1)S(1)} %pad_maximum_fusion.1.refs_4_), channel_id=1, source_target_pairs={{0,1},{1,0},{2,3},{3,2},{4,5},{5,4},{6,7},{7,6},{8,9},{9,8},{10,11... | collective-permute-start | bytes 2949128 | tf_op jit(solution)/shard_map/ppermute | solution.py:112
  90.8 10.1 %collective-permute-start.18 = (bf16[16,960,128]{2,1,0:T(8,128)(2,1)}, bf16[16,960,128]{2,1,0:T(8,128)(2,1)S(1)}, u32[]{:S(2)}, u32[]{:S(2)}) collective-permute-start(bf16[16,960,128]{2,1,0:T(8,128)(2,1)} %get-tuple-element.53), channel_id=1, source_target_pairs={{0,1},{1,0},{2,3},{3,2},{4,5},{5,4},{6,7},{7,6},{8,9},{9,8},{10,11... | collective-permute-start | bytes 11796488 | tf_op jit(solution)/shard_map/ppermute | solution.py:112
  102.4 21.2 %collective-permute-start.20 = (bf16[8,416,128]{2,1,0:T(8,128)(2,1)S(1)}, bf16[8,416,128]{2,1,0:T(8,128)(2,1)S(1)}, u32[]{:S(2)}, u32[]{:S(2)}) collective-permute-start(bf16[8,416,128]{2,1,0:T(8,128)(2,1)S(1)} %get-tuple-element.57), channel_id=1, source_target_pairs={{0,4},{1,5},{2,6},{3,7},{4,0},{5,1},{6,2},{7,3},{8,12},{9,13},{10,... | collective-permute-start | bytes 2555912 | tf_op jit(solution)/shard_map/ppermute | solution.py:112
  102.5 24.2 %collective-permute-start.24 = (bf16[8,480,128]{2,1,0:T(8,128)(2,1)S(1)}, bf16[8,480,128]{2,1,0:T(8,128)(2,1)S(1)}, u32[]{:S(2)}, u32[]{:S(2)}) collective-permute-start(bf16[8,480,128]{2,1,0:T(8,128)(2,1)S(1)} %get-tuple-element.59), channel_id=1, source_target_pairs={{0,8},{1,9},{2,10},{3,11},{4,12},{5,13},{6,14},{7,15},{8,0},{9,1},... | collective-permute-start | bytes 2949128 | tf_op jit(solution)/shard_map/ppermute | solution.py:112
  104.4 24.6 %collective-permute-start.28 = (bf16[8,480,128]{2,1,0:T(8,128)(2,1)S(1)}, bf16[8,480,128]{2,1,0:T(8,128)(2,1)S(1)}, u32[]{:S(2)}, u32[]{:S(2)}) collective-permute-start(bf16[8,480,128]{2,1,0:T(8,128)(2,1)S(1)} %get-tuple-element.61), channel_id=1, source_target_pairs={{0,2},{1,3},{2,0},{3,1},{4,6},{5,7},{6,4},{7,5},{8,10},{9,11},{10,... | collective-permute-start | bytes 2949128 | tf_op jit(solution)/shard_map/ppermute | solution.py:112
  123.8 13.5 %collective-permute-start.21 = (bf16[4,416,128]{2,1,0:T(8,128)(2,1)S(1)}, bf16[4,416,128]{2,1,0:T(8,128)(2,1)S(1)}, u32[]{:S(2)}, u32[]{:S(2)}) collective-permute-start(bf16[4,416,128]{2,1,0:T(8,128)(2,1)S(1)} %get-tuple-element.74), channel_id=1, source_target_pairs={{0,2},{1,3},{2,0},{3,1},{4,6},{5,7},{6,4},{7,5},{8,10},{9,11},{10,... | collective-permute-start | bytes 1277960 | tf_op jit(solution)/shard_map/ppermute | solution.py:112
  127.0 12.9 %collective-permute-start.25 = (bf16[4,480,128]{2,1,0:T(8,128)(2,1)S(1)}, bf16[4,480,128]{2,1,0:T(8,128)(2,1)S(1)}, u32[]{:S(2)}, u32[]{:S(2)}) collective-permute-start(bf16[4,480,128]{2,1,0:T(8,128)(2,1)S(1)} %get-tuple-element.70), channel_id=1, source_target_pairs={{0,4},{1,5},{2,6},{3,7},{4,0},{5,1},{6,2},{7,3},{8,12},{9,13},{10,... | collective-permute-start | bytes 1474568 | tf_op jit(solution)/shard_map/ppermute | solution.py:112
  129.3 20.1 %collective-permute-start.29 = (bf16[4,480,128]{2,1,0:T(8,128)(2,1)S(1)}, bf16[4,480,128]{2,1,0:T(8,128)(2,1)S(1)}, u32[]{:S(2)}, u32[]{:S(2)}) collective-permute-start(bf16[4,480,128]{2,1,0:T(8,128)(2,1)S(1)} %get-tuple-element.72), channel_id=1, source_target_pairs={{0,8},{1,9},{2,10},{3,11},{4,12},{5,13},{6,14},{7,15},{8,0},{9,1},... | collective-permute-start | bytes 1474568 | tf_op jit(solution)/shard_map/ppermute | solution.py:112
  137.4 11.9 %collective-permute-start.22 = (bf16[2,416,128]{2,1,0:T(8,128)(2,1)S(1)}, bf16[2,416,128]{2,1,0:T(8,128)(2,1)S(1)}, u32[]{:S(2)}, u32[]{:S(2)}) collective-permute-start(bf16[2,416,128]{2,1,0:T(8,128)(2,1)S(1)} %get-tuple-element.80), channel_id=1, source_target_pairs={{0,16},{1,17},{2,18},{3,19},{4,20},{5,21},{6,22},{7,23},{8,24},{9,... | collective-permute-start | bytes 638984 | tf_op jit(solution)/shard_map/ppermute | solution.py:112
  140.1 14.2 %collective-permute-start.26 = (bf16[2,480,128]{2,1,0:T(8,128)(2,1)S(1)}, bf16[2,480,128]{2,1,0:T(8,128)(2,1)S(1)}, u32[]{:S(2)}, u32[]{:S(2)}) collective-permute-start(bf16[2,480,128]{2,1,0:T(8,128)(2,1)S(1)} %get-tuple-element.76), channel_id=1, source_target_pairs={{0,2},{1,3},{2,0},{3,1},{4,6},{5,7},{6,4},{7,5},{8,10},{9,11},{10,... | collective-permute-start | bytes 737288 | tf_op jit(solution)/shard_map/ppermute | solution.py:112
  154.3 10.2 %collective-permute-start.27 = (bf16[1,480,128]{2,1,0:T(8,128)(2,1)S(1)}, bf16[1,480,128]{2,1,0:T(8,128)(2,1)S(1)}, u32[]{:S(2)}, u32[]{:S(2)}) collective-permute-start(bf16[1,480,128]{2,1,0:T(8,128)(2,1)S(1)} %add_convert_fusion.14), channel_id=1, source_target_pairs={{0,16},{1,17},{2,18},{3,19},{4,20},{5,21},{6,22},{7,23},{8,24},{9,... | collective-permute-start | bytes 368648 | tf_op jit(solution)/shard_map/ppermute | solution.py:112
  156.5 9.4 %collective-permute-start.31 = (bf16[1,480,128]{2,1,0:T(8,128)(2,1)S(1)}, bf16[1,480,128]{2,1,0:T(8,128)(2,1)S(1)}, u32[]{:S(2)}, u32[]{:S(2)}) collective-permute-start(bf16[1,480,128]{2,1,0:T(8,128)(2,1)S(1)} %add_convert_fusion.12), channel_id=1, source_target_pairs={{0,16},{1,17},{2,18},{3,19},{4,20},{5,21},{6,22},{7,23},{8,24},{9,... | collective-permute-start | bytes 368648 | tf_op jit(solution)/shard_map/ppermute | solution.py:112
  (17 other events, 160.0 us)
